TPU v7x, 256 devices: a whole 4x4x8 slice. The times are simulated.
256 devices in a mesh: band: 32 (over x_lo, z, core), domain: 8 (over y, x_hi).
Axes of the slice: x: 4 (x_hi: 2, x_lo: 2; x = x_hi * 2 + x_lo), y: 4, z: 8, core: 2. Of those that a mesh axis runs over, the one named last changes fastest.
Arguments:
- orbitals: float32 [512, 64, 4096], P('band', 'domain'), may hold values from -6 to 6
- previous: float32 [512, 64, 4096], P('band', 'domain'), may hold values from -6 to 6
- potential: float32 [64, 4096], P('domain'), may hold values from -3 to 3
- rotation: float32 [512, 512], P(None, 'band'), may hold values from -1 to 1
- accumulated: float32 [512, 64, 4096], P('band', 'domain'), may hold values from -6 to 6
- panel: int32 [1], replicated, may hold values from 0 to 131071
Outputs:
- filtered: float32 [512, 64, 4096], P('band', 'domain')
- rotated: float32 [512, 64, 4096], P('band', 'domain')
All inputs are finite; a program needn't handle non-finite values.
Results may differ from a plain program's by a relative error of at most 0.000059.
Values sent between devices are 32-bit elements; how exact they have to be, the bound alone decides.
No kernel may reach another device: no remote copies, remote signals or barrier semaphores. Data moves between devices by JAX's collectives and lax.ppermute only.
A program may use at most 192 MiB of HBM per device.

v0:
```python
import numpy as np
import jax
import jax.numpy as jnp
from jax import lax
from jax.experimental import pallas as pl
from jax.experimental.pallas import tpu as pltpu
from jax.sharding import PartitionSpec as P


coefs = (
    -5369.0 / 1800.0,
    12.0 / 7.0,
    -15.0 / 56.0,
    10.0 / 189.0,
    -1.0 / 112.0,
    2.0 / 1925.0,
    -1.0 / 16632.0,
)
SCALE = -2.0 / 14.0
ROW = 64
LANES = 128
WIDTH = 6
ROWS_X = 2
RING = 8
CORES = 2


def row_matrix():
    out = np.zeros((LANES, LANES))
    for i in range(LANES):
        base = i - i % ROW
        for k in range(1, 7):
            for s in (k, -k):
                out[base + (i + s) % ROW, i] += SCALE * coefs[k]
    return out.astype(np.float32)


def mixed(full, spare, limit, below):
    sub = lax.broadcasted_iota(jnp.int32, full.shape, 0)
    return jnp.where(sub < limit, full, spare) if below else jnp.where(sub >= limit, full, spare)


def pack_body(orb, head, tail):
    for i in range(orb.shape[0]):
        for g in range(orb.shape[2] // (4 * LANES)):
            tiles = [orb[i, :, (4 * g + m) * LANES : (4 * g + m + 1) * LANES] for m in range(4)]
            for m in range(3):
                spare = pltpu.roll(tiles[3], 6 - 2 * m, 0)
                span = slice((3 * g + m) * LANES, (3 * g + m + 1) * LANES)
                head[i, :, span] = mixed(tiles[m], spare, WIDTH, True)
                tail[i, :, span] = mixed(tiles[m], spare, 2, False)


def unpacked(side, i, first):
    out = []
    for g in range(side.shape[2] // (3 * LANES)):
        three = [side[i, :, (3 * g + m) * LANES : (3 * g + m + 1) * LANES] for m in range(3)]
        rolled = [pltpu.roll(v, 2 + 2 * m, 0) for m, v in enumerate(three)]
        last = mixed(rolled[0], mixed(rolled[1], rolled[2], first + 4, True), first + 2, True)
        out += three + [last]
    return out


def pack(orb):
    n, planes, cells = orb.shape
    thin = cells * WIDTH // planes
    step = min(n, 4)
    return pl.pallas_call(
        pack_body,
        grid=(n // step,),
        in_specs=[pl.BlockSpec((step, planes, cells), lambda i: (i, 0, 0))],
        out_specs=[pl.BlockSpec((step, planes, thin), lambda i: (i, 0, 0))] * 2,
        out_shape=[jax.ShapeDtypeStruct((n, planes, thin), jnp.float32)] * 2,
        cost_estimate=pl.CostEstimate(flops=0, bytes_accessed=10 * n * planes * cells, transcendentals=0),
    )(orb)


def filter_one(i, orb, low, high, prev, pot, mat, out, ext, half, rowsum):
    planes = orb.shape[1]
    tiles = orb.shape[2] // LANES
    span = 3 * planes
    low_tiles = unpacked(low, i, 2)
    high_tiles = unpacked(high, i, 0)
    lane = lax.broadcasted_iota(jnp.int32, (planes, LANES), 1)
    rolled = None
    first = None
    for t in range(tiles):
        tile = orb[i, :, t * LANES : (t + 1) * LANES]
        ext[span * t : span * t + planes, :] = low_tiles[t]
        ext[span * t + planes : span * t + 2 * planes, :] = tile
        ext[span * t + 2 * planes : span * t + 3 * planes, :] = high_tiles[t]
        now = pltpu.roll(tile, ROW, 1)
        if t:
            half[(t - 1) * planes : t * planes, :] = jnp.where(lane < ROW, rolled, now)
        else:
            first = now
        rolled = now
    half[(tiles - 1) * planes : tiles * planes, :] = jnp.where(lane < ROW, rolled, first)
    cells = jnp.concatenate([orb[i, :, t * LANES : (t + 1) * LANES] for t in range(tiles)], axis=0)
    rowsum[...] = jnp.dot(cells, mat[...], precision=lax.Precision.HIGHEST, preferred_element_type=jnp.float32)
    for t in range(tiles):
        base = span * t + planes
        centre = orb[i, :, t * LANES : (t + 1) * LANES]

        def flat(step):
            u = (t + step) % tiles
            return orb[i, :, u * LANES : (u + 1) * LANES]

        def odd(step):
            u = (t + step) % tiles
            return half[u * planes : (u + 1) * planes, :]

        total = rowsum[t * planes : (t + 1) * planes, :]
        for k in range(1, 7):
            pair = ext[base + k : base + k + planes, :] + ext[base - k : base - k + planes, :]
            if k % 2:
                pair = pair + (odd((k - 1) // 2) + odd(-(k + 1) // 2))
            else:
                pair = pair + (flat(k // 2) + flat(-(k // 2)))
            total = total + np.float32(SCALE * coefs[k]) * pair
        diag = pot[:, t * LANES : (t + 1) * LANES] * np.float32(1 / 14.0) + np.float32(3 * SCALE * coefs[0] - 36.0 / 14.0)
        out[i, :, t * LANES : (t + 1) * LANES] = total + diag * centre - prev[i, :, t * LANES : (t + 1) * LANES]


def filter_body(orb, *refs):
    @pl.loop(0, orb.shape[0])
    def _(i):
        filter_one(i, orb, *refs)


def apply_filter(orb, low, high, prev, pot):
    n, planes, cells = orb.shape
    tiles = cells // LANES
    thin = cells * WIDTH // planes
    step = min(n, 4)
    whole = pl.BlockSpec((step, planes, cells), lambda i: (i, 0, 0))
    side = pl.BlockSpec((step, planes, thin), lambda i: (i, 0, 0))
    return pl.pallas_call(
        filter_body,
        grid=(n // step,),
        in_specs=[
            whole,
            side,
            side,
            whole,
            pl.BlockSpec((planes, cells), lambda i: (0, 0)),
            pl.BlockSpec((LANES, LANES), lambda i: (0, 0)),
        ],
        out_specs=whole,
        out_shape=jax.ShapeDtypeStruct((n, planes, cells), jnp.float32),
        scratch_shapes=[
            pltpu.VMEM((tiles * 3 * planes, LANES), jnp.float32),
            pltpu.VMEM((tiles * planes, LANES), jnp.float32),
            pltpu.VMEM((tiles * planes, LANES), jnp.float32),
        ],
        cost_estimate=pl.CostEstimate(
            flops=n * planes * cells * 1600, bytes_accessed=19 * n * planes * cells, transcendentals=0
        ),
    )(orb, low, high, prev, pot, jnp.asarray(row_matrix()))


def weights_body(scalars, rows, plan, high, low):
    z, core, first = scalars[0], scalars[1], scalars[2]
    offset, which, other = plan[0:1, :], plan[1:2, :], plan[2:3, :]
    seat_core = jnp.where(other == 1, 1 - core, core)
    share = plan[3:4, :]
    order = first + ((z + offset) & (RING - 1)) * share + which + seat_core * (RING * share)
    count, span = rows.shape
    columns = order.shape[1]
    planes = high.shape[0] // count
    pick = lax.broadcasted_iota(jnp.int32, (span, columns), 0) == order
    wide = jnp.dot(rows[...], pick.astype(jnp.float32), precision=lax.Precision.HIGHEST, preferred_element_type=jnp.float32)
    row = lax.broadcasted_iota(jnp.int32, (planes, columns), 0)
    col = lax.broadcasted_iota(jnp.int32, (planes, columns), 1)
    same = (col & (planes - 1)) == row
    for j in range(count):
        full = jnp.where(same, wide[j : j + 1, :], 0.0)
        top = full.astype(jnp.bfloat16).astype(jnp.float32)
        high[j * planes : (j + 1) * planes, :] = top
        low[j * planes : (j + 1) * planes, :] = full - top


def weights(rotation, plan, z, core, chip, share, planes):
    turned = rotation.T
    count = turned.shape[0]
    panel = CORES * RING * share
    per = LANES // panel
    table = np.repeat(np.asarray([(o, i, c, share) for o, i, c in plan], np.int32).T, planes, axis=1)
    table = np.concatenate([table, np.zeros((8 - table.shape[0], table.shape[1]), np.int32)])
    scalars = jnp.stack([z, core, (chip % per) * panel, chip // per])
    shape = (count * planes, table.shape[1])
    return pl.pallas_call(
        weights_body,
        grid_spec=pltpu.PrefetchScalarGridSpec(
            num_scalar_prefetch=1,
            grid=(1,),
            in_specs=[
                pl.BlockSpec((count, LANES), lambda i, s: (0, s[3])),
                pl.BlockSpec(table.shape, lambda i, s: (0, 0)),
            ],
            out_specs=[pl.BlockSpec(shape, lambda i, s: (0, 0))] * 2,
        ),
        out_shape=[jax.ShapeDtypeStruct(shape, jnp.float32)] * 2,
        cost_estimate=pl.CostEstimate(flops=10**6, bytes_accessed=10**6, transcendentals=0),
    )(scalars, turned, jnp.asarray(table))


def panel_body(acc, *rest):
    blocks, (high, low, out) = rest[:-3], rest[-3:]
    n, planes, width = acc.shape
    block = jnp.concatenate([b[...].reshape(b.shape[0] * planes, width) for b in blocks], axis=0)
    block_high = block.astype(jnp.bfloat16)
    block_low = (block - block_high.astype(jnp.float32)).astype(jnp.bfloat16)
    high = high[...].astype(jnp.bfloat16)
    low = low[...].astype(jnp.bfloat16)
    dot = lambda a, b: jnp.dot(a, b, preferred_element_type=jnp.float32)
    prod = dot(high, block_high) + (dot(high, block_low) + dot(low, block_high))
    out[...] = acc[...] + prod.reshape(n, planes, width)


def add_panel(acc, blocks, high, low):
    n, planes, cells = acc.shape
    chunk = cells // 4
    spec = lambda m: pl.BlockSpec((m, planes, chunk), lambda i: (0, 0, i))
    k = sum(b.shape[0] for b in blocks)
    full = pl.BlockSpec(high.shape, lambda i: (0, 0))
    return pl.pallas_call(
        panel_body,
        grid=(cells // chunk,),
        in_specs=[spec(n)] + [spec(b.shape[0]) for b in blocks] + [full, full],
        out_specs=spec(n),
        out_shape=jax.ShapeDtypeStruct(acc.shape, jnp.float32),
        cost_estimate=pl.CostEstimate(
            flops=6 * n * planes * planes * k * cells, bytes_accessed=4 * (2 * n + k) * planes * cells, transcendentals=0
        ),
    )(acc, *blocks, high, low)


def seat(x, z, core):
    return (x * RING + z % RING) * CORES + core


def everywhere(step):
    return [
        (seat(x, z, c), seat(*step(x, z, c))) for x in range(ROWS_X) for z in range(RING) for c in range(CORES)
    ]


ONWARD = everywhere(lambda x, z, c: (x, z + 1, c))
BACK = everywhere(lambda x, z, c: (x, z - 1, c))
ACROSS = everywhere(lambda x, z, c: (1 - x, z, c))
PARTNER = everywhere(lambda x, z, c: (x, z, 1 - c))


def deal_body(z, block, *hands):
    for i, hand in enumerate(hands):
        share = hand.shape[0]
        for m in range(share):
            hand[m] = block[((z[0] + i) & (RING - 1)) * share + m]


def deal(block, z):
    n, planes, cells = block.shape
    share = n // RING
    hand = pl.BlockSpec((share, planes, cells), lambda i, z: (0, 0, 0))
    return pl.pallas_call(
        deal_body,
        grid_spec=pltpu.PrefetchScalarGridSpec(
            num_scalar_prefetch=1,
            grid=(1,),
            in_specs=[pl.BlockSpec(block.shape, lambda i, z: (0, 0, 0))],
            out_specs=[hand] * RING,
        ),
        out_shape=[jax.ShapeDtypeStruct((share, planes, cells), jnp.float32)] * RING,
        cost_estimate=pl.CostEstimate(flops=0, bytes_accessed=8 * n * planes * cells, transcendentals=0),
    )(z[None], block)


def relay(hands, offset):
    share = hands[0].shape[0]
    half = share // 2
    root = offset == 0
    up = lax.ppermute(hands[4][:half], "band", ONWARD)
    down = lax.ppermute(hands[4][half:], "band", BACK)
    up, down = jnp.concatenate([up, up]), jnp.concatenate([down, down])
    for step in (3, 2, 1):
        up = jnp.where(root, hands[step], up)
        down = jnp.where(root, hands[RING - step], down)
        up = lax.ppermute(up, "band", ONWARD)
        down = lax.ppermute(down, "band", BACK)
    middle = jnp.concatenate([up[:half], down[:half]])
    far = jnp.where(offset < 4, up, jnp.where(offset == 4, middle, down))
    return jnp.where(root, hands[0], far)


def halo(head, tail):
    size = lax.axis_size("domain")
    low = lax.ppermute(tail, "domain", [(i, (i + 1) % size) for i in range(size)])
    high = lax.ppermute(head, "domain", [((i + 1) % size, i) for i in range(size)])
    return low, high


def step(orbitals, previous, potential, rotation, accumulated, panel):
    count = orbitals.shape[0]
    share = count // RING
    where = lax.axis_index("band")
    x, z, core = where >> 4, (where >> 1) & 7, where & 1
    chip = panel[0] & (ROWS_X * RING - 1)
    root_x, root_z = chip >> 3, chip & 7

    offset = (z - root_z) & (RING - 1)

    hands = deal(orbitals, z)
    ends = pack(orbitals)
    low, high = halo(*ends)
    hands_before = deal(previous, z)
    piece = relay(hands, offset)
    before = relay(hands_before, offset)
    ends = pack(piece)
    below, above = halo(*ends)
    piece = apply_filter(piece, below, above, before, potential)
    other = lax.ppermute(piece, "band", ACROSS)
    piece = jnp.where(x == root_x, piece, other)
    filtered = apply_filter(orbitals, low, high, previous, potential)

    blocks = [piece]
    plan = [(0, 0), (0, 1)]
    up = down = piece
    for hop in (1, 2, 3):
        up = lax.ppermute(up, "band", ONWARD)
        down = lax.ppermute(down, "band", BACK)
        blocks += [up, down]
        plan += [(-hop, 0), (-hop, 1), (hop, 0), (hop, 1)]
    blocks += [lax.ppermute(up, "band", ONWARD)]
    plan += [(-4, 0), (-4, 1)]
    blocks += [lax.ppermute(b, "band", PARTNER) for b in blocks]
    plan = [(o, i, c) for c in range(CORES) for o, i in plan]
    coefficients = weights(rotation, plan, z, core, chip, share, orbitals.shape[1])
    rotated = add_panel(accumulated, blocks, *coefficients)
    return filtered, rotated


def solution(mesh):
    in_specs = (
        P("band", "domain", None),
        P("band", "domain", None),
        P("domain", None),
        P(None, "band"),
        P("band", "domain", None),
        P(),
    )
    out_specs = (P("band", "domain", None), P("band", "domain", None))
    return jax.shard_map(step, mesh=mesh, in_specs=in_specs, out_specs=out_specs, check_vma=False)
```

profile of v0, /device:TPU:1, one launch (start us, length us, event | category | flops | bytes accessed | tf_op | source)
XLA Modules:
  0.0 179.9 jit_solution(11671027709510160714)
XLA Ops:
  0.6 3.0 %shard_map.108 = (f32[2,8,4096]{2,1,0:T(8,128)}, f32[2,8,4096]{2,1,0:T(8,128)}, f32[2,8,4096]{2,1,0:T(8,128)}, f32[2,8,4096]{2,1,0:T(8,128)}, f32[2,8,4096]{2,1,...) custom-call(s32[1]{0:T(128)} %bitcast.1.z, f32[16,8,4096]{2,1,0:T(8,128)} %block.3), custom_call_target="tpu_custom_call" | custom-call | bytes 4194304 | tf_op jit(solution)/shard_map/pallas_call | solution.py:266
  4.7 6.5 %collective-permute-start.16 = (f32[1,8,4096]{2,1,0:T(8,128)S(1)}, f32[1,8,4096]{2,1,0:T(8,128)S(1)}, u32[]{:S(2)}, u32[]{:S(2)}) collective-permute-start(f32[1,8,4096]{2,1,0:T(8,128)S(1)} %get-tuple-element.46), channel_id=1, source_target_pairs={{0,112},{8,120},{16,0},{24,8},{32,16},{40,24},{48,32},{56,40},{64,... | collective-permute-start | bytes 393224 | tf_op jit(solution)/shard_map/ppermute | solution.py:284
  11.2 3.1 %shard_map.106 = (f32[2,8,4096]{2,1,0:T(8,128)}, f32[2,8,4096]{2,1,0:T(8,128)}, f32[2,8,4096]{2,1,0:T(8,128)}, f32[2,8,4096]{2,1,0:T(8,128)}, f32[2,8,4096]{2,1,...) custom-call(s32[1]{0:T(128)} %bitcast.1.z, f32[16,8,4096]{2,1,0:T(8,128)} %block.2), custom_call_target="tpu_custom_call" | custom-call | bytes 4194304 | tf_op jit(solution)/shard_map/pallas_call | solution.py:266
  15.3 2.7 %collective-permute-start.6 = (f32[1,8,4096]{2,1,0:T(8,128)S(1)}, f32[1,8,4096]{2,1,0:T(8,128)S(1)}, u32[]{:S(2)}, u32[]{:S(2)}) collective-permute-start(f32[1,8,4096]{2,1,0:T(8,128)S(1)} %get-tuple-element.48), channel_id=1, source_target_pairs={{0,112},{8,120},{16,0},{24,8},{32,16},{40,24},{48,32},{56,40},{64,... | collective-permute-start | bytes 393224 | tf_op jit(solution)/shard_map/ppermute | solution.py:284
  19.0 2.7 %collective-permute-start.17 = (f32[2,8,4096]{2,1,0:T(8,128)S(1)}, f32[2,8,4096]{2,1,0:T(8,128)S(1)}, u32[]{:S(2)}, u32[]{:S(2)}) collective-permute-start(f32[2,8,4096]{2,1,0:T(8,128)S(1)} %maximum_select_fusion.4), channel_id=1, source_target_pairs={{0,112},{8,120},{16,0},{24,8},{32,16},{40,24},{48,32},{56,40},{64,... | collective-permute-start | bytes 786440 | tf_op jit(solution)/shard_map/ppermute | solution.py:290
  23.3 2.7 %collective-permute-start.7 = (f32[2,8,4096]{2,1,0:T(8,128)S(1)}, f32[2,8,4096]{2,1,0:T(8,128)S(1)}, u32[]{:S(2)}, u32[]{:S(2)}) collective-permute-start(f32[2,8,4096]{2,1,0:T(8,128)S(1)} %maximum_select_fusion.1), channel_id=1, source_target_pairs={{0,112},{8,120},{16,0},{24,8},{32,16},{40,24},{48,32},{56,40},{64,... | collective-permute-start | bytes 786440 | tf_op jit(solution)/shard_map/ppermute | solution.py:290
  28.7 2.7 %collective-permute-start.18 = (f32[2,8,4096]{2,1,0:T(8,128)S(1)}, f32[2,8,4096]{2,1,0:T(8,128)S(1)}, u32[]{:S(2)}, u32[]{:S(2)}) collective-permute-start(f32[2,8,4096]{2,1,0:T(8,128)S(1)} %broadcast_select_fusion.1), channel_id=1, source_target_pairs={{0,112},{8,120},{16,0},{24,8},{32,16},{40,24},{48,32},{56,40},{64,... | collective-permute-start | bytes 786440 | tf_op jit(solution)/shard_map/ppermute | solution.py:290
  31.4 2.7 %collective-permute-done.3 = f32[2,8,4096]{2,1,0:T(8,128)S(1)} collective-permute-done((f32[2,8,4096]{2,1,0:T(8,128)S(1)}, f32[2,8,4096]{2,1,0:T(8,128)S(1)}, u32[]{:S(2)}, u32[]{:S(2)}) %collective-permute-start.3) | collective-permute-done | bytes 262176 | tf_op jit(solution)/shard_map/ppermute | solution.py:289
  34.3 2.7 %collective-permute-start.8 = (f32[2,8,4096]{2,1,0:T(8,128)S(1)}, f32[2,8,4096]{2,1,0:T(8,128)S(1)}, u32[]{:S(2)}, u32[]{:S(2)}) collective-permute-start(f32[2,8,4096]{2,1,0:T(8,128)S(1)} %broadcast_select_fusion.5), channel_id=1, source_target_pairs={{0,112},{8,120},{16,0},{24,8},{32,16},{40,24},{48,32},{56,40},{64,... | collective-permute-start | bytes 786440 | tf_op jit(solution)/shard_map/ppermute | solution.py:290
  37.0 2.7 %collective-permute-done.14 = f32[2,8,4096]{2,1,0:T(8,128)S(1)} collective-permute-done((f32[2,8,4096]{2,1,0:T(8,128)S(1)}, f32[2,8,4096]{2,1,0:T(8,128)S(1)}, u32[]{:S(2)}, u32[]{:S(2)}) %collective-permute-start.14) | collective-permute-done | bytes 262176 | tf_op jit(solution)/shard_map/ppermute | solution.py:289
  39.8 5.5 %collective-permute-done.4 = f32[2,8,4096]{2,1,0:T(8,128)S(1)} collective-permute-done((f32[2,8,4096]{2,1,0:T(8,128)S(1)}, f32[2,8,4096]{2,1,0:T(8,128)S(1)}, u32[]{:S(2)}, u32[]{:S(2)}) %collective-permute-start.4) | collective-permute-done | bytes 262176 | tf_op jit(solution)/shard_map/ppermute | solution.py:289
  45.5 2.9 %collective-permute-start.9 = (f32[2,8,4096]{2,1,0:T(8,128)S(1)}, f32[2,8,4096]{2,1,0:T(8,128)S(1)}, u32[]{:S(2)}, u32[]{:S(2)}) collective-permute-start(f32[2,8,4096]{2,1,0:T(8,128)S(1)} %broadcast_select_fusion.4), channel_id=1, source_target_pairs={{0,112},{8,120},{16,0},{24,8},{32,16},{40,24},{48,32},{56,40},{64,... | collective-permute-start | bytes 786440 | tf_op jit(solution)/shard_map/ppermute | solution.py:290
  48.6 8.0 %collective-permute-done.5 = f32[2,8,4096]{2,1,0:T(8,128)S(1)} collective-permute-done((f32[2,8,4096]{2,1,0:T(8,128)S(1)}, f32[2,8,4096]{2,1,0:T(8,128)S(1)}, u32[]{:S(2)}, u32[]{:S(2)}) %collective-permute-start.5) | collective-permute-done | bytes 262176 | tf_op jit(solution)/shard_map/ppermute | solution.py:289
  59.1 2.7 %collective-permute-start.10 = (f32[2,8,3072]{2,1,0:T(8,128)}, f32[2,8,3072]{2,1,0:T(8,128)S(1)}, u32[]{:S(2)}, u32[]{:S(2)}) collective-permute-start(f32[2,8,3072]{2,1,0:T(8,128)} %get-tuple-element.34), channel_id=1, source_target_pairs={{0,1},{1,2},{2,3},{3,4},{4,5},{5,6},{6,7},{7,0},{8,9},{9,10},{10,1... | collective-permute-start | bytes 589832 | tf_op jit(solution)/shard_map/ppermute | solution.py:298
  61.8 2.5 %collective-permute-start.11 = (f32[2,8,3072]{2,1,0:T(8,128)}, f32[2,8,3072]{2,1,0:T(8,128)S(1)}, u32[]{:S(2)}, u32[]{:S(2)}) collective-permute-start(f32[2,8,3072]{2,1,0:T(8,128)} %get-tuple-element.35), channel_id=1, source_target_pairs={{1,0},{2,1},{3,2},{4,3},{5,4},{6,5},{7,6},{0,7},{9,8},{10,9},{11,1... | collective-permute-start | bytes 589832 | tf_op jit(solution)/shard_map/ppermute | solution.py:299
  65.1 2.5 %collective-permute-done.10.refs_0_ = f32[2,8,3072]{2,1,0:T(8,128)S(1)} collective-permute-done((f32[2,8,3072]{2,1,0:T(8,128)}, f32[2,8,3072]{2,1,0:T(8,128)S(1)}, u32[]{:S(2)}, u32[]{:S(2)}) %collective-permute-start.10) | collective-permute-done | bytes 196640 | tf_op jit(solution)/shard_map/ppermute | solution.py:298
  67.6 2.6 %collective-permute-done.11.refs_1_ = f32[2,8,3072]{2,1,0:T(8,128)S(1)} collective-permute-done((f32[2,8,3072]{2,1,0:T(8,128)}, f32[2,8,3072]{2,1,0:T(8,128)S(1)}, u32[]{:S(2)}, u32[]{:S(2)}) %collective-permute-start.11) | collective-permute-done | bytes 196640 | tf_op jit(solution)/shard_map/ppermute | solution.py:299
  70.8 2.6 %shard_map.109 = f32[2,8,4096]{2,1,0:T(8,128)} custom-call(f32[2,8,4096]{2,1,0:T(8,128)} %fusion.1.orb, f32[2,8,3072]{2,1,0:T(8,128)} %copy-done.21, f32[2,8,3072]{2,1,0:T(8,128)} %copy-done.22, f32[2,8,4096]{2,1,0:T(8,128)} %fusion.3.refs_2_, f32[8,4096]{1,0:T(8,128)} %refs_3_.3, f32[128,128]{1,0:T(8,128)} %constant.46.clone.refs_4_), custom_call_target="tpu_custom_call" | custom-call | flops 104857600 | bytes 1245184 | tf_op jit(solution)/shard_map/pallas_call | solution.py:138
  74.6 4.0 %shard_map.104 = (f32[16,8,3072]{2,1,0:T(8,128)}, f32[16,8,3072]{2,1,0:T(8,128)}) custom-call(f32[16,8,4096]{2,1,0:T(8,128)} %block.2), custom_call_target="tpu_custom_call" | custom-call | bytes 5242880 | tf_op jit(solution)/shard_map/pallas_call | solution.py:68
  80.8 3.2 %collective-permute-start.1 = (f32[16,8,3072]{2,1,0:T(8,128)}, f32[16,8,3072]{2,1,0:T(8,128)S(1)}, u32[]{:S(2)}, u32[]{:S(2)}) collective-permute-start(f32[16,8,3072]{2,1,0:T(8,128)} %get-tuple-element.25), channel_id=1, source_target_pairs={{1,0},{2,1},{3,2},{4,3},{5,4},{6,5},{7,6},{0,7},{9,8},{10,9},{11,1... | collective-permute-start | bytes 4718600 | tf_op jit(solution)/shard_map/ppermute | solution.py:299
  85.1 2.7 %collective-permute-start.22 = (f32[2,8,4096]{2,1,0:T(8,128)S(1)}, f32[2,8,4096]{2,1,0:T(8,128)S(1)}, u32[]{:S(2)}, u32[]{:S(2)}) collective-permute-start(f32[2,8,4096]{2,1,0:T(8,128)S(1)} %broadcast_select_fusion.8.rest_0_), channel_id=1, source_target_pairs={{0,112},{8,120},{16,0},{24,8},{32,16},{40,24},{48,32},{56,40},{64,... | collective-permute-start | bytes 786440 | tf_op jit(solution)/shard_map/ppermute | solution.py:331
  87.8 4.1 %collective-permute-done.21.rest_1_ = f32[2,8,4096]{2,1,0:T(8,128)S(1)} collective-permute-done((f32[2,8,4096]{2,1,0:T(8,128)S(1)}, f32[2,8,4096]{2,1,0:T(8,128)S(1)}, u32[]{:S(2)}, u32[]{:S(2)}) %collective-permute-start.21) | collective-permute-done | bytes 262176 | tf_op jit(solution)/shard_map/ppermute | solution.py:330
  91.8 2.7 %collective-permute-start.24 = (f32[2,8,4096]{2,1,0:T(8,128)S(1)}, f32[2,8,4096]{2,1,0:T(8,128)}, u32[]{:S(2)}, u32[]{:S(2)}) collective-permute-start(f32[2,8,4096]{2,1,0:T(8,128)S(1)} %collective-permute-done.22.rest_2_), channel_id=1, source_target_pairs={{0,112},{8,120},{16,0},{24,8},{32,16},{40,24},{48,32},{56,40},{64,... | collective-permute-start | bytes 786440 | tf_op jit(solution)/shard_map/ppermute | solution.py:331
  94.5 4.3 %collective-permute-done.23.rest_3_ = f32[2,8,4096]{2,1,0:T(8,128)} collective-permute-done((f32[2,8,4096]{2,1,0:T(8,128)S(1)}, f32[2,8,4096]{2,1,0:T(8,128)}, u32[]{:S(2)}, u32[]{:S(2)}) %collective-permute-start.23) | collective-permute-done | bytes 262176 | tf_op jit(solution)/shard_map/ppermute | solution.py:330
  98.8 6.5 %collective-permute-start.28 = (f32[2,8,4096]{2,1,0:T(8,128)S(1)}, f32[2,8,4096]{2,1,0:T(8,128)S(1)}, u32[]{:S(2)}, u32[]{:S(2)}) collective-permute-start(f32[2,8,4096]{2,1,0:T(8,128)S(1)} %broadcast_select_fusion.8.rest_0_), channel_id=1, source_target_pairs={{0,8},{8,0},{16,24},{24,16},{32,40},{40,32},{48,56},{56,48},{64,72... | collective-permute-start | bytes 786440 | tf_op jit(solution)/shard_map/ppermute | solution.py:336
  105.3 13.5 %collective-permute-done.refs_0_ = f32[16,8,3072]{2,1,0:T(8,128)S(1)} collective-permute-done((f32[16,8,3072]{2,1,0:T(8,128)}, f32[16,8,3072]{2,1,0:T(8,128)S(1)}, u32[]{:S(2)}, u32[]{:S(2)}) %collective-permute-start) | collective-permute-done | bytes 1572896 | tf_op jit(solution)/shard_map/ppermute | solution.py:298
  118.8 4.4 %collective-permute-start.30 = (f32[2,8,4096]{2,1,0:T(8,128)S(1)}, f32[2,8,4096]{2,1,0:T(8,128)S(1)}, u32[]{:S(2)}, u32[]{:S(2)}) collective-permute-start(f32[2,8,4096]{2,1,0:T(8,128)S(1)} %collective-permute-done.22.rest_2_), channel_id=1, source_target_pairs={{0,8},{8,0},{16,24},{24,16},{32,40},{40,32},{48,56},{56,48},{64,72... | collective-permute-start | bytes 786440 | tf_op jit(solution)/shard_map/ppermute | solution.py:336
  123.2 26.2 %collective-permute-done.1.refs_1_ = f32[16,8,3072]{2,1,0:T(8,128)S(1)} collective-permute-done((f32[16,8,3072]{2,1,0:T(8,128)}, f32[16,8,3072]{2,1,0:T(8,128)S(1)}, u32[]{:S(2)}, u32[]{:S(2)}) %collective-permute-start.1) | collective-permute-done | bytes 1572896 | tf_op jit(solution)/shard_map/ppermute | solution.py:299
  149.5 3.4 %collective-permute-start.29 = (f32[2,8,4096]{2,1,0:T(8,128)S(1)}, f32[2,8,4096]{2,1,0:T(8,128)S(1)}, u32[]{:S(2)}, u32[]{:S(2)}) collective-permute-start(f32[2,8,4096]{2,1,0:T(8,128)S(1)} %collective-permute-done.21.rest_1_), channel_id=1, source_target_pairs={{0,8},{8,0},{16,24},{24,16},{32,40},{40,32},{48,56},{56,48},{64,72... | collective-permute-start | bytes 786440 | tf_op jit(solution)/shard_map/ppermute | solution.py:336
  155.9 5.1 %collective-permute-done.26.rest_6_ = f32[2,8,4096]{2,1,0:T(8,128)} collective-permute-done((f32[2,8,4096]{2,1,0:T(8,128)}, f32[2,8,4096]{2,1,0:T(8,128)}, u32[]{:S(2)}, u32[]{:S(2)}) %collective-permute-start.26) | collective-permute-done | bytes 262176 | tf_op jit(solution)/shard_map/ppermute | solution.py:331
  166.1 8.1 %shard_map.105 = f32[16,8,4096]{2,1,0:T(8,128)} custom-call(f32[16,8,4096]{2,1,0:T(8,128)} %block.2, f32[16,8,3072]{2,1,0:T(8,128)} %copy-done, f32[16,8,3072]{2,1,0:T(8,128)} %copy-done.1, f32[16,8,4096]{2,1,0:T(8,128)} %block.3, f32[8,4096]{1,0:T(8,128)} %refs_3_.3, f32[128,128]{1,0:T(8,128)} %constant.46.clone.refs_4_), custom_call_target="tpu_custom_call" | custom-call | flops 838860800 | bytes 9961472 | tf_op jit(solution)/shard_map/pallas_call | solution.py:138
  174.2 5.5 %shard_map.111 = f32[16,8,4096]{2,1,0:T(8,128)} custom-call(f32[16,8,4096]{2,1,0:T(8,128)} %acc.1, f32[2,8,4096]{2,1,0:T(8,128)} %copy-done.2, f32[2,8,4096]{2,1,0:T(8,128)} %copy-done.3, f32[2,8,4096]{2,1,0:T(8,128)} %copy-done.4, f32[2,8,4096]{2,1,0:T(8,128)} %collective-permute-done.23.rest_3_, f32[2,8,4096]{2,1,0:T(8,128)} %collective-permute-done.24.rest_4_, ...), custom_call_target="tpu_custom_call" | custom-call | flops 805306368 | bytes 8388608 | tf_op jit(solution)/shard_map/pallas_call | solution.py:227
  (116 shorter events, 23.6 us)
Async XLA Ops:
  4.7 14.2 %collective-permute-start.16 = (f32[1,8,4096]{2,1,0:T(8,128)S(1)}, f32[1,8,4096]{2,1,0:T(8,128)S(1)}, u32[]{:S(2)}, u32[]{:S(2)}) collective-permute-start(f32[1,8,4096]{2,1,0:T(8,128)S(1)} %get-tuple-element.46), channel_id=1, source_target_pairs={{0,112},{8,120},{16,0},{24,8},{32,16},{40,24},{48,32},{56,40},{64,... | collective-permute-start | bytes 393224 | tf_op jit(solution)/shard_map/ppermute | solution.py:284
  11.2 7.5 %collective-permute-start.12 = (f32[1,8,4096]{2,1,0:T(8,128)S(1)}, f32[1,8,4096]{2,1,0:T(8,128)S(1)}, u32[]{:S(2)}, u32[]{:S(2)}) collective-permute-start(f32[1,8,4096]{2,1,0:T(8,128)S(1)} %get-tuple-element.47), channel_id=1, source_target_pairs={{0,16},{8,24},{16,32},{24,40},{32,48},{40,56},{48,64},{56,72},{64,... | collective-permute-start | bytes 393224 | tf_op jit(solution)/shard_map/ppermute | solution.py:283
  15.3 7.9 %collective-permute-start.6 = (f32[1,8,4096]{2,1,0:T(8,128)S(1)}, f32[1,8,4096]{2,1,0:T(8,128)S(1)}, u32[]{:S(2)}, u32[]{:S(2)}) collective-permute-start(f32[1,8,4096]{2,1,0:T(8,128)S(1)} %get-tuple-element.48), channel_id=1, source_target_pairs={{0,112},{8,120},{16,0},{24,8},{32,16},{40,24},{48,32},{56,40},{64,... | collective-permute-start | bytes 393224 | tf_op jit(solution)/shard_map/ppermute | solution.py:284
  18.8 9.6 %collective-permute-start.13 = (f32[2,8,4096]{2,1,0:T(8,128)S(1)}, f32[2,8,4096]{2,1,0:T(8,128)S(1)}, u32[]{:S(2)}, u32[]{:S(2)}) collective-permute-start(f32[2,8,4096]{2,1,0:T(8,128)S(1)} %maximum_select_fusion.3), channel_id=1, source_target_pairs={{0,16},{8,24},{16,32},{24,40},{32,48},{40,56},{48,64},{56,72},{64,... | collective-permute-start | bytes 786440 | tf_op jit(solution)/shard_map/ppermute | solution.py:289
  19.0 9.6 %collective-permute-start.17 = (f32[2,8,4096]{2,1,0:T(8,128)S(1)}, f32[2,8,4096]{2,1,0:T(8,128)S(1)}, u32[]{:S(2)}, u32[]{:S(2)}) collective-permute-start(f32[2,8,4096]{2,1,0:T(8,128)S(1)} %maximum_select_fusion.4), channel_id=1, source_target_pairs={{0,112},{8,120},{16,0},{24,8},{32,16},{40,24},{48,32},{56,40},{64,... | collective-permute-start | bytes 786440 | tf_op jit(solution)/shard_map/ppermute | solution.py:290
  23.1 10.9 %collective-permute-start.3 = (f32[2,8,4096]{2,1,0:T(8,128)S(1)}, f32[2,8,4096]{2,1,0:T(8,128)S(1)}, u32[]{:S(2)}, u32[]{:S(2)}) collective-permute-start(f32[2,8,4096]{2,1,0:T(8,128)S(1)} %maximum_select_fusion), channel_id=1, source_target_pairs={{0,16},{8,24},{16,32},{24,40},{32,48},{40,56},{48,64},{56,72},{64,... | collective-permute-start | bytes 786440 | tf_op jit(solution)/shard_map/ppermute | solution.py:289
  23.3 10.9 %collective-permute-start.7 = (f32[2,8,4096]{2,1,0:T(8,128)S(1)}, f32[2,8,4096]{2,1,0:T(8,128)S(1)}, u32[]{:S(2)}, u32[]{:S(2)}) collective-permute-start(f32[2,8,4096]{2,1,0:T(8,128)S(1)} %maximum_select_fusion.1), channel_id=1, source_target_pairs={{0,112},{8,120},{16,0},{24,8},{32,16},{40,24},{48,32},{56,40},{64,... | collective-permute-start | bytes 786440 | tf_op jit(solution)/shard_map/ppermute | solution.py:290
  28.5 11.2 %collective-permute-start.14 = (f32[2,8,4096]{2,1,0:T(8,128)S(1)}, f32[2,8,4096]{2,1,0:T(8,128)S(1)}, u32[]{:S(2)}, u32[]{:S(2)}) collective-permute-start(f32[2,8,4096]{2,1,0:T(8,128)S(1)} %broadcast_select_fusion.3), channel_id=1, source_target_pairs={{0,16},{8,24},{16,32},{24,40},{32,48},{40,56},{48,64},{56,72},{64,... | collective-permute-start | bytes 786440 | tf_op jit(solution)/shard_map/ppermute | solution.py:289
  28.7 19.7 %collective-permute-start.18 = (f32[2,8,4096]{2,1,0:T(8,128)S(1)}, f32[2,8,4096]{2,1,0:T(8,128)S(1)}, u32[]{:S(2)}, u32[]{:S(2)}) collective-permute-start(f32[2,8,4096]{2,1,0:T(8,128)S(1)} %broadcast_select_fusion.1), channel_id=1, source_target_pairs={{0,112},{8,120},{16,0},{24,8},{32,16},{40,24},{48,32},{56,40},{64,... | collective-permute-start | bytes 786440 | tf_op jit(solution)/shard_map/ppermute | solution.py:290
  34.1 11.2 %collective-permute-start.4 = (f32[2,8,4096]{2,1,0:T(8,128)S(1)}, f32[2,8,4096]{2,1,0:T(8,128)S(1)}, u32[]{:S(2)}, u32[]{:S(2)}) collective-permute-start(f32[2,8,4096]{2,1,0:T(8,128)S(1)} %broadcast_select_fusion.7), channel_id=1, source_target_pairs={{0,16},{8,24},{16,32},{24,40},{32,48},{40,56},{48,64},{56,72},{64,... | collective-permute-start | bytes 786440 | tf_op jit(solution)/shard_map/ppermute | solution.py:289
  34.3 11.2 %collective-permute-start.8 = (f32[2,8,4096]{2,1,0:T(8,128)S(1)}, f32[2,8,4096]{2,1,0:T(8,128)S(1)}, u32[]{:S(2)}, u32[]{:S(2)}) collective-permute-start(f32[2,8,4096]{2,1,0:T(8,128)S(1)} %broadcast_select_fusion.5), channel_id=1, source_target_pairs={{0,112},{8,120},{16,0},{24,8},{32,16},{40,24},{48,32},{56,40},{64,... | collective-permute-start | bytes 786440 | tf_op jit(solution)/shard_map/ppermute | solution.py:290
  39.7 24.6 %collective-permute-start.15 = (f32[2,8,4096]{2,1,0:T(8,128)S(1)}, f32[2,8,4096]{2,1,0:T(8,128)S(1)}, u32[]{:S(2)}, u32[]{:S(2)}) collective-permute-start(f32[2,8,4096]{2,1,0:T(8,128)S(1)} %broadcast_select_fusion.2), channel_id=1, source_target_pairs={{0,16},{8,24},{16,32},{24,40},{32,48},{40,56},{48,64},{56,72},{64,... | collective-permute-start | bytes 786440 | tf_op jit(solution)/shard_map/ppermute | solution.py:289
  45.3 11.2 %collective-permute-start.5 = (f32[2,8,4096]{2,1,0:T(8,128)S(1)}, f32[2,8,4096]{2,1,0:T(8,128)S(1)}, u32[]{:S(2)}, u32[]{:S(2)}) collective-permute-start(f32[2,8,4096]{2,1,0:T(8,128)S(1)} %broadcast_select_fusion.6), channel_id=1, source_target_pairs={{0,16},{8,24},{16,32},{24,40},{32,48},{40,56},{48,64},{56,72},{64,... | collective-permute-start | bytes 786440 | tf_op jit(solution)/shard_map/ppermute | solution.py:289
  45.5 11.1 %collective-permute-start.9 = (f32[2,8,4096]{2,1,0:T(8,128)S(1)}, f32[2,8,4096]{2,1,0:T(8,128)S(1)}, u32[]{:S(2)}, u32[]{:S(2)}) collective-permute-start(f32[2,8,4096]{2,1,0:T(8,128)S(1)} %broadcast_select_fusion.4), channel_id=1, source_target_pairs={{0,112},{8,120},{16,0},{24,8},{32,16},{40,24},{48,32},{56,40},{64,... | collective-permute-start | bytes 786440 | tf_op jit(solution)/shard_map/ppermute | solution.py:290
  48.4 15.9 %collective-permute-start.19 = (f32[2,8,4096]{2,1,0:T(8,128)S(1)}, f32[2,8,4096]{2,1,0:T(8,128)S(1)}, u32[]{:S(2)}, u32[]{:S(2)}) collective-permute-start(f32[2,8,4096]{2,1,0:T(8,128)S(1)} %broadcast_select_fusion), channel_id=1, source_target_pairs={{0,112},{8,120},{16,0},{24,8},{32,16},{40,24},{48,32},{56,40},{64,... | collective-permute-start | bytes 786440 | tf_op jit(solution)/shard_map/ppermute | solution.py:290
  59.1 8.5 %collective-permute-start.10 = (f32[2,8,3072]{2,1,0:T(8,128)}, f32[2,8,3072]{2,1,0:T(8,128)S(1)}, u32[]{:S(2)}, u32[]{:S(2)}) collective-permute-start(f32[2,8,3072]{2,1,0:T(8,128)} %get-tuple-element.34), channel_id=1, source_target_pairs={{0,1},{1,2},{2,3},{3,4},{4,5},{5,6},{6,7},{7,0},{8,9},{9,10},{10,1... | collective-permute-start | bytes 589832 | tf_op jit(solution)/shard_map/ppermute | solution.py:298
  61.8 8.3 %collective-permute-start.11 = (f32[2,8,3072]{2,1,0:T(8,128)}, f32[2,8,3072]{2,1,0:T(8,128)S(1)}, u32[]{:S(2)}, u32[]{:S(2)}) collective-permute-start(f32[2,8,3072]{2,1,0:T(8,128)} %get-tuple-element.35), channel_id=1, source_target_pairs={{1,0},{2,1},{3,2},{4,3},{5,4},{6,5},{7,6},{0,7},{9,8},{10,9},{11,1... | collective-permute-start | bytes 589832 | tf_op jit(solution)/shard_map/ppermute | solution.py:299
  73.4 10.6 %collective-permute-start.20 = (f32[2,8,4096]{2,1,0:T(8,128)}, f32[2,8,4096]{2,1,0:T(8,128)}, u32[]{:S(2)}, u32[]{:S(2)}) collective-permute-start(f32[2,8,4096]{2,1,0:T(8,128)} %shard_map.109), channel_id=1, source_target_pairs={{0,128},{8,136},{16,144},{24,152},{32,160},{40,168},{48,176},{56,1... | collective-permute-start | bytes 786440 | tf_op jit(solution)/shard_map/ppermute | solution.py:322
  78.6 40.2 %collective-permute-start = (f32[16,8,3072]{2,1,0:T(8,128)}, f32[16,8,3072]{2,1,0:T(8,128)S(1)}, u32[]{:S(2)}, u32[]{:S(2)}) collective-permute-start(f32[16,8,3072]{2,1,0:T(8,128)} %get-tuple-element.24), channel_id=1, source_target_pairs={{0,1},{1,2},{2,3},{3,4},{4,5},{5,6},{6,7},{7,0},{8,9},{9,10},{10,1... | collective-permute-start | bytes 4718600 | tf_op jit(solution)/shard_map/ppermute | solution.py:298
  80.8 68.7 %collective-permute-start.1 = (f32[16,8,3072]{2,1,0:T(8,128)}, f32[16,8,3072]{2,1,0:T(8,128)S(1)}, u32[]{:S(2)}, u32[]{:S(2)}) collective-permute-start(f32[16,8,3072]{2,1,0:T(8,128)} %get-tuple-element.25), channel_id=1, source_target_pairs={{1,0},{2,1},{3,2},{4,3},{5,4},{6,5},{7,6},{0,7},{9,8},{10,9},{11,1... | collective-permute-start | bytes 4718600 | tf_op jit(solution)/shard_map/ppermute | solution.py:299
  91.8 7.0 %collective-permute-start.23 = (f32[2,8,4096]{2,1,0:T(8,128)S(1)}, f32[2,8,4096]{2,1,0:T(8,128)}, u32[]{:S(2)}, u32[]{:S(2)}) collective-permute-start(f32[2,8,4096]{2,1,0:T(8,128)S(1)} %collective-permute-done.21.rest_1_), channel_id=1, source_target_pairs={{0,16},{8,24},{16,32},{24,40},{32,48},{40,56},{48,64},{56,72},{64,... | collective-permute-start | bytes 786440 | tf_op jit(solution)/shard_map/ppermute | solution.py:330
  91.8 61.0 %collective-permute-start.24 = (f32[2,8,4096]{2,1,0:T(8,128)S(1)}, f32[2,8,4096]{2,1,0:T(8,128)}, u32[]{:S(2)}, u32[]{:S(2)}) collective-permute-start(f32[2,8,4096]{2,1,0:T(8,128)S(1)} %collective-permute-done.22.rest_2_), channel_id=1, source_target_pairs={{0,112},{8,120},{16,0},{24,8},{32,16},{40,24},{48,32},{56,40},{64,... | collective-permute-start | bytes 786440 | tf_op jit(solution)/shard_map/ppermute | solution.py:331
  98.8 54.0 %collective-permute-start.25 = (f32[2,8,4096]{2,1,0:T(8,128)}, f32[2,8,4096]{2,1,0:T(8,128)}, u32[]{:S(2)}, u32[]{:S(2)}) collective-permute-start(f32[2,8,4096]{2,1,0:T(8,128)} %collective-permute-done.23.rest_3_), channel_id=1, source_target_pairs={{0,16},{8,24},{16,32},{24,40},{32,48},{40,56},{48,64},{56,72},{64,... | collective-permute-start | bytes 786440 | tf_op jit(solution)/shard_map/ppermute | solution.py:330
  98.8 55.5 %collective-permute-start.28 = (f32[2,8,4096]{2,1,0:T(8,128)S(1)}, f32[2,8,4096]{2,1,0:T(8,128)S(1)}, u32[]{:S(2)}, u32[]{:S(2)}) collective-permute-start(f32[2,8,4096]{2,1,0:T(8,128)S(1)} %broadcast_select_fusion.8.rest_0_), channel_id=1, source_target_pairs={{0,8},{8,0},{16,24},{24,16},{32,40},{40,32},{48,56},{56,48},{64,72... | collective-permute-start | bytes 786440 | tf_op jit(solution)/shard_map/ppermute | solution.py:336
  118.8 36.5 %collective-permute-start.30 = (f32[2,8,4096]{2,1,0:T(8,128)S(1)}, f32[2,8,4096]{2,1,0:T(8,128)S(1)}, u32[]{:S(2)}, u32[]{:S(2)}) collective-permute-start(f32[2,8,4096]{2,1,0:T(8,128)S(1)} %collective-permute-done.22.rest_2_), channel_id=1, source_target_pairs={{0,8},{8,0},{16,24},{24,16},{32,40},{40,32},{48,56},{56,48},{64,72... | collective-permute-start | bytes 786440 | tf_op jit(solution)/shard_map/ppermute | solution.py:336
  152.8 8.1 %collective-permute-start.26 = (f32[2,8,4096]{2,1,0:T(8,128)}, f32[2,8,4096]{2,1,0:T(8,128)}, u32[]{:S(2)}, u32[]{:S(2)}) collective-permute-start(f32[2,8,4096]{2,1,0:T(8,128)} %collective-permute-done.24.rest_4_), channel_id=1, source_target_pairs={{0,112},{8,120},{16,0},{24,8},{32,16},{40,24},{48,32},{56,40},{64,... | collective-permute-start | bytes 786440 | tf_op jit(solution)/shard_map/ppermute | solution.py:331
  152.8 9.4 %collective-permute-start.27 = (f32[2,8,4096]{2,1,0:T(8,128)}, f32[2,8,4096]{2,1,0:T(8,128)}, u32[]{:S(2)}, u32[]{:S(2)}) collective-permute-start(f32[2,8,4096]{2,1,0:T(8,128)} %collective-permute-done.25.rest_5_), channel_id=1, source_target_pairs={{0,16},{8,24},{16,32},{24,40},{32,48},{40,56},{48,64},{56,72},{64,... | collective-permute-start | bytes 786440 | tf_op jit(solution)/shard_map/ppermute | solution.py:334
  154.3 19.8 %collective-permute-start.32 = (f32[2,8,4096]{2,1,0:T(8,128)}, f32[2,8,4096]{2,1,0:T(8,128)}, u32[]{:S(2)}, u32[]{:S(2)}) collective-permute-start(f32[2,8,4096]{2,1,0:T(8,128)} %collective-permute-done.24.rest_4_), channel_id=1, source_target_pairs={{0,8},{8,0},{16,24},{24,16},{32,40},{40,32},{48,56},{56,48},{64,72... | collective-permute-start | bytes 786440 | tf_op jit(solution)/shard_map/ppermute | solution.py:336
  155.3 18.9 %collective-permute-start.31 = (f32[2,8,4096]{2,1,0:T(8,128)}, f32[2,8,4096]{2,1,0:T(8,128)}, u32[]{:S(2)}, u32[]{:S(2)}) collective-permute-start(f32[2,8,4096]{2,1,0:T(8,128)} %collective-permute-done.23.rest_3_), channel_id=1, source_target_pairs={{0,8},{8,0},{16,24},{24,16},{32,40},{40,32},{48,56},{56,48},{64,72... | collective-permute-start | bytes 786440 | tf_op jit(solution)/shard_map/ppermute | solution.py:336
  155.4 18.8 %collective-permute-start.33 = (f32[2,8,4096]{2,1,0:T(8,128)}, f32[2,8,4096]{2,1,0:T(8,128)}, u32[]{:S(2)}, u32[]{:S(2)}) collective-permute-start(f32[2,8,4096]{2,1,0:T(8,128)} %collective-permute-done.25.rest_5_), channel_id=1, source_target_pairs={{0,8},{8,0},{16,24},{24,16},{32,40},{40,32},{48,56},{56,48},{64,72... | collective-permute-start | bytes 786440 | tf_op jit(solution)/shard_map/ppermute | solution.py:336
  160.9 13.2 %collective-permute-start.34 = (f32[2,8,4096]{2,1,0:T(8,128)}, f32[2,8,4096]{2,1,0:T(8,128)}, u32[]{:S(2)}, u32[]{:S(2)}) collective-permute-start(f32[2,8,4096]{2,1,0:T(8,128)} %collective-permute-done.26.rest_6_), channel_id=1, source_target_pairs={{0,8},{8,0},{16,24},{24,16},{32,40},{40,32},{48,56},{56,48},{64,72... | collective-permute-start | bytes 786440 | tf_op jit(solution)/shard_map/ppermute | solution.py:336
  162.2 12.0 %collective-permute-start.35 = (f32[2,8,4096]{2,1,0:T(8,128)}, f32[2,8,4096]{2,1,0:T(8,128)}, u32[]{:S(2)}, u32[]{:S(2)}) collective-permute-start(f32[2,8,4096]{2,1,0:T(8,128)} %collective-permute-done.27.rest_7_), channel_id=1, source_target_pairs={{0,8},{8,0},{16,24},{24,16},{32,40},{40,32},{48,56},{56,48},{64,72... | collective-permute-start | bytes 786440 | tf_op jit(solution)/shard_map/ppermute | solution.py:336
  (27 other events, 535.6 us)
where the time goes:
time: 181 us; the launch traced here: 180 us
  waiting for transfers between devices  81.2 us (45%)
  starting transfers between devices  60 us (33%)
  Pallas kernels  30.3 us (17%)
  other arithmetic  3.49 us (2%)
  local copies, waits for them, and re-layouts  2.92 us (2%)
  between operations  1.9 us (1%)
    ppermute x2, waiting for transfers between devices, halo(): lax.ppermute(head, 'domain', [((i + 1) % size, i) for i in range(size)])  28.8 us
    ppermute x6, waiting for transfers between devices, relay(): up = lax.ppermute(up, 'band', ONWARD)  21.3 us
    ppermute x8, starting transfers between devices, step(): blocks += [lax.ppermute(b, 'band', PARTNER) for b in blocks]  17.7 us
    ppermute x2, waiting for transfers between devices, halo(): lax.ppermute(tail, 'domain', [(i, (i + 1) % size) for i in range(size)])  15.9 us
    ppermute x6, starting transfers between devices, relay(): down = lax.ppermute(down, 'band', BACK)  13.9 us
    pallas_call x2, Pallas kernels, apply_filter(): pl.pallas_call(filter_body, grid=(n // step,), in_specs=[whole, side, sid...  10.7 us
    ppermute x2, starting transfers between devices, relay(): down = lax.ppermute(hands[4][half:], 'band', BACK)  9.22 us
    ppermute x3, waiting for transfers between devices, step(): up = lax.ppermute(up, 'band', ONWARD)  8.38 us
  transfers between devices with their start and end apart: 36, of which 14 were waited for; matrix products, arithmetic and copies ran while one was open for 3% of the time, Pallas kernels for 11%

commit v1 on v0

--- a/solution.py
+++ b/solution.py
@@ -25,6 +25,10 @@
 CORES = 2
 
 
+def room(mib):
+    return pltpu.CompilerParams(vmem_limit_bytes=mib << 20)
+
+
 def row_matrix():
     out = np.zeros((LANES, LANES))
     for i in range(LANES):
@@ -61,16 +65,18 @@
     return out
 
 
-def pack(orb):
-    n, planes, cells = orb.shape
+def pack(orb, first=0, n=None):
+    n = n or orb.shape[0]
+    planes, cells = orb.shape[1:]
     thin = cells * WIDTH // planes
     step = min(n, 4)
     return pl.pallas_call(
         pack_body,
         grid=(n // step,),
-        in_specs=[pl.BlockSpec((step, planes, cells), lambda i: (i, 0, 0))],
+        in_specs=[pl.BlockSpec((step, planes, cells), lambda i: (i + first // step, 0, 0))],
         out_specs=[pl.BlockSpec((step, planes, thin), lambda i: (i, 0, 0))] * 2,
         out_shape=[jax.ShapeDtypeStruct((n, planes, thin), jnp.float32)] * 2,
+        compiler_params=room(8),
         cost_estimate=pl.CostEstimate(flops=0, bytes_accessed=10 * n * planes * cells, transcendentals=0),
     )(orb)
 
@@ -122,41 +128,49 @@
         out[i, :, t * LANES : (t + 1) * LANES] = total + diag * centre - prev[i, :, t * LANES : (t + 1) * LANES]
 
 
-def filter_body(orb, *refs):
+def filter_body(orb, low, high, prev, pot, mat, *rest):
     @pl.loop(0, orb.shape[0])
     def _(i):
-        filter_one(i, orb, *refs)
-
-
-def apply_filter(orb, low, high, prev, pot):
-    n, planes, cells = orb.shape
+        filter_one(i, orb, low, high, prev, pot, mat, *rest[-4:])
+
+
+def apply_filter(orb, low, high, prev, pot, first=0, into=None):
+    total, planes, cells = orb.shape
+    n = low.shape[0]
     tiles = cells // LANES
     thin = cells * WIDTH // planes
     step = min(n, 4)
-    whole = pl.BlockSpec((step, planes, cells), lambda i: (i, 0, 0))
+    whole = pl.BlockSpec((step, planes, cells), lambda i: (i + first // step, 0, 0))
     side = pl.BlockSpec((step, planes, thin), lambda i: (i, 0, 0))
+    args = [orb, low, high, prev, pot, jnp.asarray(row_matrix())]
+    specs = [
+        whole,
+        side,
+        side,
+        whole,
+        pl.BlockSpec((planes, cells), lambda i: (0, 0)),
+        pl.BlockSpec((LANES, LANES), lambda i: (0, 0)),
+    ]
+    if into is not None:
+        args.append(into)
+        specs.append(pl.BlockSpec(memory_space=pl.ANY))
     return pl.pallas_call(
         filter_body,
         grid=(n // step,),
-        in_specs=[
-            whole,
-            side,
-            side,
-            whole,
-            pl.BlockSpec((planes, cells), lambda i: (0, 0)),
-            pl.BlockSpec((LANES, LANES), lambda i: (0, 0)),
-        ],
+        in_specs=specs,
         out_specs=whole,
-        out_shape=jax.ShapeDtypeStruct((n, planes, cells), jnp.float32),
+        out_shape=jax.ShapeDtypeStruct((total, planes, cells), jnp.float32),
+        input_output_aliases={} if into is None else {6: 0},
         scratch_shapes=[
             pltpu.VMEM((tiles * 3 * planes, LANES), jnp.float32),
             pltpu.VMEM((tiles * planes, LANES), jnp.float32),
             pltpu.VMEM((tiles * planes, LANES), jnp.float32),
         ],
+        compiler_params=room(14),
         cost_estimate=pl.CostEstimate(
             flops=n * planes * cells * 1600, bytes_accessed=19 * n * planes * cells, transcendentals=0
         ),
-    )(orb, low, high, prev, pot, jnp.asarray(row_matrix()))
+    )(*args)
 
 
 def weights_body(scalars, rows, plan, high, low):
@@ -201,6 +215,7 @@
             out_specs=[pl.BlockSpec(shape, lambda i, s: (0, 0))] * 2,
         ),
         out_shape=[jax.ShapeDtypeStruct(shape, jnp.float32)] * 2,
+        compiler_params=room(6),
         cost_estimate=pl.CostEstimate(flops=10**6, bytes_accessed=10**6, transcendentals=0),
     )(scalars, turned, jnp.asarray(table))
 
@@ -230,6 +245,7 @@
         in_specs=[spec(n)] + [spec(b.shape[0]) for b in blocks] + [full, full],
         out_specs=spec(n),
         out_shape=jax.ShapeDtypeStruct(acc.shape, jnp.float32),
+        compiler_params=room(20),
         cost_estimate=pl.CostEstimate(
             flops=6 * n * planes * planes * k * cells, bytes_accessed=4 * (2 * n + k) * planes * cells, transcendentals=0
         ),
@@ -252,45 +268,76 @@
 PARTNER = everywhere(lambda x, z, c: (x, z, 1 - c))
 
 
-def deal_body(z, block, *hands):
-    for i, hand in enumerate(hands):
-        share = hand.shape[0]
-        for m in range(share):
-            hand[m] = block[((z[0] + i) & (RING - 1)) * share + m]
-
-
-def deal(block, z):
+def pick_body(place, hand, moved, out):
+    for m in range(out.shape[0]):
+        out[m] = jnp.where(place[1] == 0, hand[m], moved[min(m, moved.shape[0] - 1)])
+
+
+def pick(block, place, step, moved):
     n, planes, cells = block.shape
     share = n // RING
-    hand = pl.BlockSpec((share, planes, cells), lambda i, z: (0, 0, 0))
-    return pl.pallas_call(
-        deal_body,
+    hand = lambda index: pl.BlockSpec((share, planes, cells), index)
+    return pl.pallas_call(
+        pick_body,
         grid_spec=pltpu.PrefetchScalarGridSpec(
             num_scalar_prefetch=1,
             grid=(1,),
-            in_specs=[pl.BlockSpec(block.shape, lambda i, z: (0, 0, 0))],
-            out_specs=[hand] * RING,
+            in_specs=[
+                hand(lambda i, s: ((s[0] + step) & (RING - 1), 0, 0)),
+                pl.BlockSpec(memory_space=pltpu.VMEM),
+            ],
+            out_specs=pl.BlockSpec(memory_space=pltpu.VMEM),
         ),
-        out_shape=[jax.ShapeDtypeStruct((share, planes, cells), jnp.float32)] * RING,
-        cost_estimate=pl.CostEstimate(flops=0, bytes_accessed=8 * n * planes * cells, transcendentals=0),
-    )(z[None], block)
-
-
-def relay(hands, offset):
-    share = hands[0].shape[0]
+        out_shape=jax.ShapeDtypeStruct((share, planes, cells), jnp.float32),
+        compiler_params=room(3),
+        cost_estimate=pl.CostEstimate(flops=0, bytes_accessed=12 * share * planes * cells, transcendentals=0),
+    )(place, block, moved)
+
+
+def settle_body(place, own, up, down, piece, *ends):
+    offset = place[1]
+    half = own.shape[0] // 2
+    for m in range(own.shape[0]):
+        middle = up[m] if m < half else down[m - half]
+        far = jnp.where(offset < 4, up[m], jnp.where(offset == 4, middle, down[m]))
+        piece[m] = jnp.where(offset == 0, own[m], far)
+    if ends:
+        pack_body(piece, *ends)
+
+
+def settle(block, place, up, down, packed):
+    share, planes, cells = up.shape
+    hand = lambda index: pl.BlockSpec((share, planes, cells), index)
+    still = pl.BlockSpec(memory_space=pltpu.VMEM)
+    thin = (share, planes, cells * WIDTH // planes)
+    shapes = [up.shape] + [thin] * (2 if packed else 0)
+    return pl.pallas_call(
+        settle_body,
+        grid_spec=pltpu.PrefetchScalarGridSpec(
+            num_scalar_prefetch=1,
+            grid=(1,),
+            in_specs=[hand(lambda i, s: (s[0], 0, 0)), still, still],
+            out_specs=[still] * len(shapes),
+        ),
+        out_shape=[jax.ShapeDtypeStruct(shape, jnp.float32) for shape in shapes],
+        compiler_params=room(5),
+        cost_estimate=pl.CostEstimate(flops=0, bytes_accessed=20 * share * planes * cells, transcendentals=0),
+    )(place, block, up, down)
+
+
+def relay(block, place, packed):
+    share = block.shape[0] // RING
     half = share // 2
-    root = offset == 0
-    up = lax.ppermute(hands[4][:half], "band", ONWARD)
-    down = lax.ppermute(hands[4][half:], "band", BACK)
-    up, down = jnp.concatenate([up, up]), jnp.concatenate([down, down])
+    start = ((place[0] + 4) & (RING - 1)) * share
+    size = (half,) + block.shape[1:]
+    up = lax.ppermute(lax.dynamic_slice(block, (start, 0, 0), size), "band", ONWARD)
+    down = lax.ppermute(lax.dynamic_slice(block, (start + half, 0, 0), size), "band", BACK)
     for step in (3, 2, 1):
-        up = jnp.where(root, hands[step], up)
-        down = jnp.where(root, hands[RING - step], down)
+        up = pick(block, place, step, up)
+        down = pick(block, place, RING - step, down)
         up = lax.ppermute(up, "band", ONWARD)
         down = lax.ppermute(down, "band", BACK)
-    middle = jnp.concatenate([up[:half], down[:half]])
-    far = jnp.where(offset < 4, up, jnp.where(offset == 4, middle, down))
-    return jnp.where(root, hands[0], far)
+    return settle(block, place, up, down, packed)
 
 
 def halo(head, tail):
@@ -310,18 +357,21 @@
 
     offset = (z - root_z) & (RING - 1)
 
-    hands = deal(orbitals, z)
-    ends = pack(orbitals)
-    low, high = halo(*ends)
-    hands_before = deal(previous, z)
-    piece = relay(hands, offset)
-    before = relay(hands_before, offset)
-    ends = pack(piece)
+    early = count // 2
+    ends = pack(orbitals, 0, early)
+    sides_early = halo(*ends)
+    ends = pack(orbitals, early, count - early)
+    sides_late = halo(*ends)
+
+    place = jnp.stack([z, offset])
+    piece, *ends = relay(orbitals, place, True)
+    (before,) = relay(previous, place, False)
     below, above = halo(*ends)
     piece = apply_filter(piece, below, above, before, potential)
     other = lax.ppermute(piece, "band", ACROSS)
     piece = jnp.where(x == root_x, piece, other)
-    filtered = apply_filter(orbitals, low, high, previous, potential)
+    filtered = apply_filter(orbitals, *sides_early, previous, potential)
+    filtered = apply_filter(orbitals, *sides_late, previous, potential, early, filtered)
 
     blocks = [piece]
     plan = [(0, 0), (0, 1)]

time: 181 us -> 172 us (0.950)
  waiting for transfers between devices: 81.2 us -> 50.2 us
  starting transfers between devices: 60 us -> 83.8 us
  local copies, waits for them, and re-layouts: 2.92 us -> 9.37 us
  Pallas kernels: 30.3 us -> 25.8 us
  other arithmetic: 3.49 us -> 0.18 us
    ppermute x2 -> x3, waiting for transfers between devices: 28.8 us -> 8.38 us  [halo(): lax.ppermute(head, 'domain', [((i + 1) % size, i) for i in range(size)])]
    ppermute x6, waiting for transfers between devices: 21.3 us -> 5.3 us  [relay(): up = lax.ppermute(up, 'band', ONWARD)]
    ppermute x8, starting transfers between devices: 17.7 us -> 30.9 us  [step(): blocks += [lax.ppermute(b, 'band', PARTNER) for b in blocks]]
    ppermute x3, waiting for transfers between devices: 8.38 us -> 0.01 us  [step(): up = lax.ppermute(up, 'band', ONWARD)]
    unnamed x46 -> x40, local copies, waits for them, and re-layouts: 0.78 us -> 8.36 us
    ppermute x4, waiting for transfers between devices: 1.4 us -> 6.91 us  [the longest x2 6.9 us: relay(): lax.ppermute(lax.dynamic_slice(block, (start, 0, 0), size), 'band', ONWARD)]
    ppermute x2 -> x3, starting transfers between devices: 5.7 us -> 11 us  [halo(): lax.ppermute(head, 'domain', [((i + 1) % size, i) for i in range(size)])]
    ppermute x2 -> x3, waiting for transfers between devices: 15.9 us -> 21 us  [halo(): lax.ppermute(tail, 'domain', [(i, (i + 1) % size) for i in range(size)])]
  transfers between devices with their start and end apart: 36 -> 38, of which waited for: 14 -> 14; matrix products, arithmetic and copies ran while one was open for 3% -> 0% of each run, Pallas kernels for 11% -> 12%
where the time goes in v1:
time: 172 us; the launch traced here: 171 us
  starting transfers between devices  83.8 us (49%)
  waiting for transfers between devices  50.2 us (29%)
  Pallas kernels  25.8 us (15%)
  local copies, waits for them, and re-layouts  9.37 us (5%)
    ppermute x8, starting transfers between devices, step(): blocks += [lax.ppermute(b, 'band', PARTNER) for b in blocks]  30.9 us
    ppermute x3, waiting for transfers between devices, halo(): lax.ppermute(tail, 'domain', [(i, (i + 1) % size) for i in range(size)])  21 us
    ppermute x6, starting transfers between devices, relay(): down = lax.ppermute(down, 'band', BACK)  16.6 us
    ppermute x3, starting transfers between devices, halo(): lax.ppermute(head, 'domain', [((i + 1) % size, i) for i in range(size)])  11 us
    pallas_call x3, Pallas kernels, apply_filter(): pl.pallas_call(filter_body, grid=(n // step,), in_specs=specs, out_specs=...  9.88 us
    ppermute x3, starting transfers between devices, step(): down = lax.ppermute(down, 'band', BACK)  8.92 us
    ppermute x3, waiting for transfers between devices, halo(): lax.ppermute(head, 'domain', [((i + 1) % size, i) for i in range(size)])  8.38 us
    unnamed x40, local copies, waits for them, and re-layouts  8.36 us
  transfers between devices with their start and end apart: 38, of which 14 were waited for; matrix products, arithmetic and copies ran while one was open for 0% of the time, Pallas kernels for 12%

profile of v1, /device:TPU:1, one launch (start us, length us, event | category | flops | bytes accessed | tf_op | source)
XLA Modules:
  0.0 171.2 jit_solution(2480652780738072987)
XLA Ops:
  1.6 2.5 %collective-permute-start.4 = (f32[1,8,4096]{2,1,0:T(8,128)S(1)}, f32[1,8,4096]{2,1,0:T(8,128)S(1)}, u32[]{:S(2)}, u32[]{:S(2)}) collective-permute-start(f32[1,8,4096]{2,1,0:T(8,128)S(1)} %get-tuple-element.23), channel_id=1, source_target_pairs={{0,16},{8,24},{16,32},{24,40},{32,48},{40,56},{48,64},{56,72},{64,... | collective-permute-start | bytes 393224 | tf_op jit(solution)/shard_map/ppermute | solution.py:333
  4.2 4.0 %collective-permute-start.8 = (f32[1,8,4096]{2,1,0:T(8,128)S(1)}, f32[1,8,4096]{2,1,0:T(8,128)S(1)}, u32[]{:S(2)}, u32[]{:S(2)}) collective-permute-start(f32[1,8,4096]{2,1,0:T(8,128)S(1)} %get-tuple-element.22), channel_id=1, source_target_pairs={{0,112},{8,120},{16,0},{24,8},{32,16},{40,24},{48,32},{56,40},{64,... | collective-permute-start | bytes 393224 | tf_op jit(solution)/shard_map/ppermute | solution.py:334
  8.9 2.4 %collective-permute-done.4.moved = f32[1,8,4096]{2,1,0:T(8,128)S(1)} collective-permute-done((f32[1,8,4096]{2,1,0:T(8,128)S(1)}, f32[1,8,4096]{2,1,0:T(8,128)S(1)}, u32[]{:S(2)}, u32[]{:S(2)}) %collective-permute-start.4) | collective-permute-done | bytes 131104 | tf_op jit(solution)/shard_map/ppermute | solution.py:333
  14.1 2.7 %collective-permute-start.9 = (f32[2,8,4096]{2,1,0:T(8,128)S(1)}, f32[2,8,4096]{2,1,0:T(8,128)S(1)}, u32[]{:S(2)}, u32[]{:S(2)}) collective-permute-start(f32[2,8,4096]{2,1,0:T(8,128)S(1)} %shard_map.120), channel_id=1, source_target_pairs={{0,112},{8,120},{16,0},{24,8},{32,16},{40,24},{48,32},{56,40},{64,... | collective-permute-start | bytes 786440 | tf_op jit(solution)/shard_map/ppermute | solution.py:339
  17.0 2.7 %collective-permute-start.18 = (f32[1,8,4096]{2,1,0:T(8,128)S(1)}, f32[1,8,4096]{2,1,0:T(8,128)S(1)}, u32[]{:S(2)}, u32[]{:S(2)}) collective-permute-start(f32[1,8,4096]{2,1,0:T(8,128)S(1)} %get-tuple-element.20), channel_id=1, source_target_pairs={{0,112},{8,120},{16,0},{24,8},{32,16},{40,24},{48,32},{56,40},{64,... | collective-permute-start | bytes 393224 | tf_op jit(solution)/shard_map/ppermute | solution.py:334
  19.7 4.5 %collective-permute-done.14.moved = f32[1,8,4096]{2,1,0:T(8,128)S(1)} collective-permute-done((f32[1,8,4096]{2,1,0:T(8,128)S(1)}, f32[1,8,4096]{2,1,0:T(8,128)S(1)}, u32[]{:S(2)}, u32[]{:S(2)}) %collective-permute-start.14) | collective-permute-done | bytes 131104 | tf_op jit(solution)/shard_map/ppermute | solution.py:333
  25.4 2.7 %collective-permute-start.19 = (f32[2,8,4096]{2,1,0:T(8,128)S(1)}, f32[2,8,4096]{2,1,0:T(8,128)S(1)}, u32[]{:S(2)}, u32[]{:S(2)}) collective-permute-start(f32[2,8,4096]{2,1,0:T(8,128)S(1)} %shard_map.127), channel_id=1, source_target_pairs={{0,112},{8,120},{16,0},{24,8},{32,16},{40,24},{48,32},{56,40},{64,... | collective-permute-start | bytes 786440 | tf_op jit(solution)/shard_map/ppermute | solution.py:339
  29.4 2.7 %collective-permute-start.10 = (f32[2,8,4096]{2,1,0:T(8,128)S(1)}, f32[2,8,4096]{2,1,0:T(8,128)S(1)}, u32[]{:S(2)}, u32[]{:S(2)}) collective-permute-start(f32[2,8,4096]{2,1,0:T(8,128)S(1)} %shard_map.121), channel_id=1, source_target_pairs={{0,112},{8,120},{16,0},{24,8},{32,16},{40,24},{48,32},{56,40},{64,... | collective-permute-start | bytes 786440 | tf_op jit(solution)/shard_map/ppermute | solution.py:339
  33.4 2.7 %collective-permute-start.20 = (f32[2,8,4096]{2,1,0:T(8,128)S(1)}, f32[2,8,4096]{2,1,0:T(8,128)S(1)}, u32[]{:S(2)}, u32[]{:S(2)}) collective-permute-start(f32[2,8,4096]{2,1,0:T(8,128)S(1)} %shard_map.128), channel_id=1, source_target_pairs={{0,112},{8,120},{16,0},{24,8},{32,16},{40,24},{48,32},{56,40},{64,... | collective-permute-start | bytes 786440 | tf_op jit(solution)/shard_map/ppermute | solution.py:339
  39.6 2.7 %collective-permute-start.11 = (f32[2,8,4096]{2,1,0:T(8,128)S(1)}, f32[2,8,4096]{2,1,0:T(8,128)S(1)}, u32[]{:S(2)}, u32[]{:S(2)}) collective-permute-start(f32[2,8,4096]{2,1,0:T(8,128)S(1)} %shard_map.122), channel_id=1, source_target_pairs={{0,112},{8,120},{16,0},{24,8},{32,16},{40,24},{48,32},{56,40},{64,... | collective-permute-start | bytes 786440 | tf_op jit(solution)/shard_map/ppermute | solution.py:339
  45.2 2.9 %collective-permute-start.21 = (f32[2,8,4096]{2,1,0:T(8,128)S(1)}, f32[2,8,4096]{2,1,0:T(8,128)S(1)}, u32[]{:S(2)}, u32[]{:S(2)}) collective-permute-start(f32[2,8,4096]{2,1,0:T(8,128)S(1)} %shard_map.129), channel_id=1, source_target_pairs={{0,112},{8,120},{16,0},{24,8},{32,16},{40,24},{48,32},{56,40},{64,... | collective-permute-start | bytes 786440 | tf_op jit(solution)/shard_map/ppermute | solution.py:339
  50.2 2.8 %collective-permute-start.12 = (f32[2,8,3072]{2,1,0:T(8,128)S(1)}, f32[2,8,3072]{2,1,0:T(8,128)S(1)}, u32[]{:S(2)}, u32[]{:S(2)}) collective-permute-start(f32[2,8,3072]{2,1,0:T(8,128)S(1)} %get-tuple-element.16), channel_id=1, source_target_pairs={{0,1},{1,2},{2,3},{3,4},{4,5},{5,6},{6,7},{7,0},{8,9},{9,10},{10,1... | collective-permute-start | bytes 589832 | tf_op jit(solution)/shard_map/ppermute | solution.py:345
  53.1 2.5 %collective-permute-start.13 = (f32[2,8,3072]{2,1,0:T(8,128)S(1)}, f32[2,8,3072]{2,1,0:T(8,128)S(1)}, u32[]{:S(2)}, u32[]{:S(2)}) collective-permute-start(f32[2,8,3072]{2,1,0:T(8,128)S(1)} %get-tuple-element.17), channel_id=1, source_target_pairs={{1,0},{2,1},{3,2},{4,3},{5,4},{6,5},{7,6},{0,7},{9,8},{10,9},{11,1... | collective-permute-start | bytes 589832 | tf_op jit(solution)/shard_map/ppermute | solution.py:346
  56.2 2.4 %collective-permute-done.12.low = f32[2,8,3072]{2,1,0:T(8,128)S(1)} collective-permute-done((f32[2,8,3072]{2,1,0:T(8,128)S(1)}, f32[2,8,3072]{2,1,0:T(8,128)S(1)}, u32[]{:S(2)}, u32[]{:S(2)}) %collective-permute-start.12) | collective-permute-done | bytes 196640 | tf_op jit(solution)/shard_map/ppermute | solution.py:345
  62.7 2.4 %collective-permute-start.2 = (f32[8,8,3072]{2,1,0:T(8,128)}, f32[8,8,3072]{2,1,0:T(8,128)}, u32[]{:S(2)}, u32[]{:S(2)}) collective-permute-start(f32[8,8,3072]{2,1,0:T(8,128)} %get-tuple-element.13), channel_id=1, source_target_pairs={{0,1},{1,2},{2,3},{3,4},{4,5},{5,6},{6,7},{7,0},{8,9},{9,10},{10,1... | collective-permute-start | bytes 2359304 | tf_op jit(solution)/shard_map/ppermute | solution.py:345
  65.1 3.3 %collective-permute-start.3 = (f32[8,8,3072]{2,1,0:T(8,128)}, f32[8,8,3072]{2,1,0:T(8,128)}, u32[]{:S(2)}, u32[]{:S(2)}) collective-permute-start(f32[8,8,3072]{2,1,0:T(8,128)} %get-tuple-element.14), channel_id=1, source_target_pairs={{1,0},{2,1},{3,2},{4,3},{5,4},{6,5},{7,6},{0,7},{9,8},{10,9},{11,1... | collective-permute-start | bytes 2359304 | tf_op jit(solution)/shard_map/ppermute | solution.py:346
  69.7 5.1 %collective-permute-start.1 = (f32[8,8,3072]{2,1,0:T(8,128)}, f32[8,8,3072]{2,1,0:T(8,128)}, u32[]{:S(2)}, u32[]{:S(2)}) collective-permute-start(f32[8,8,3072]{2,1,0:T(8,128)} %get-tuple-element.12), channel_id=1, source_target_pairs={{1,0},{2,1},{3,2},{4,3},{5,4},{6,5},{7,6},{0,7},{9,8},{10,9},{11,1... | collective-permute-start | bytes 2359304 | tf_op jit(solution)/shard_map/ppermute | solution.py:346
  74.9 10.3 %collective-permute-done.2.low = f32[8,8,3072]{2,1,0:T(8,128)} collective-permute-done((f32[8,8,3072]{2,1,0:T(8,128)}, f32[8,8,3072]{2,1,0:T(8,128)}, u32[]{:S(2)}, u32[]{:S(2)}) %collective-permute-start.2) | collective-permute-done | bytes 786464 | tf_op jit(solution)/shard_map/ppermute | solution.py:345
  85.2 2.5 %collective-permute-start.24 = (f32[2,8,4096]{2,1,0:T(8,128)S(1)}, f32[2,8,4096]{2,1,0:T(8,128)S(1)}, u32[]{:S(2)}, u32[]{:S(2)}) collective-permute-start(f32[2,8,4096]{2,1,0:T(8,128)S(1)} %broadcast_select_fusion.rest_0_), channel_id=1, source_target_pairs={{0,112},{8,120},{16,0},{24,8},{32,16},{40,24},{48,32},{56,40},{64,... | collective-permute-start | bytes 786440 | tf_op jit(solution)/shard_map/ppermute | solution.py:381
  87.7 3.3 %collective-permute-done.24.rest_2_ = f32[2,8,4096]{2,1,0:T(8,128)S(1)} collective-permute-done((f32[2,8,4096]{2,1,0:T(8,128)S(1)}, f32[2,8,4096]{2,1,0:T(8,128)S(1)}, u32[]{:S(2)}, u32[]{:S(2)}) %collective-permute-start.24) | collective-permute-done | bytes 262176 | tf_op jit(solution)/shard_map/ppermute | solution.py:381
  91.0 3.5 %collective-permute-start.26 = (f32[2,8,4096]{2,1,0:T(8,128)S(1)}, f32[2,8,4096]{2,1,0:T(8,128)}, u32[]{:S(2)}, u32[]{:S(2)}) collective-permute-start(f32[2,8,4096]{2,1,0:T(8,128)S(1)} %collective-permute-done.24.rest_2_), channel_id=1, source_target_pairs={{0,112},{8,120},{16,0},{24,8},{32,16},{40,24},{48,32},{56,40},{64,... | collective-permute-start | bytes 786440 | tf_op jit(solution)/shard_map/ppermute | solution.py:381
  94.6 5.4 %collective-permute-done.3.high = f32[8,8,3072]{2,1,0:T(8,128)} collective-permute-done((f32[8,8,3072]{2,1,0:T(8,128)}, f32[8,8,3072]{2,1,0:T(8,128)}, u32[]{:S(2)}, u32[]{:S(2)}) %collective-permute-start.3) | collective-permute-done | bytes 786464 | tf_op jit(solution)/shard_map/ppermute | solution.py:346
  100.0 10.5 %collective-permute-start.30 = (f32[2,8,4096]{2,1,0:T(8,128)S(1)}, f32[2,8,4096]{2,1,0:T(8,128)S(1)}, u32[]{:S(2)}, u32[]{:S(2)}) collective-permute-start(f32[2,8,4096]{2,1,0:T(8,128)S(1)} %broadcast_select_fusion.rest_0_), channel_id=1, source_target_pairs={{0,8},{8,0},{16,24},{24,16},{32,40},{40,32},{48,56},{56,48},{64,72... | collective-permute-start | bytes 786440 | tf_op jit(solution)/shard_map/ppermute | solution.py:386
  110.5 8.3 %collective-permute-done.low = f32[8,8,3072]{2,1,0:T(8,128)S(1)} collective-permute-done((f32[8,8,3072]{2,1,0:T(8,128)}, f32[8,8,3072]{2,1,0:T(8,128)S(1)}, u32[]{:S(2)}, u32[]{:S(2)}) %collective-permute-start) | collective-permute-done | bytes 786464 | tf_op jit(solution)/shard_map/ppermute | solution.py:345
  118.8 12.2 %collective-permute-start.32 = (f32[2,8,4096]{2,1,0:T(8,128)S(1)}, f32[2,8,4096]{2,1,0:T(8,128)S(1)}, u32[]{:S(2)}, u32[]{:S(2)}) collective-permute-start(f32[2,8,4096]{2,1,0:T(8,128)S(1)} %collective-permute-done.24.rest_2_), channel_id=1, source_target_pairs={{0,8},{8,0},{16,24},{24,16},{32,40},{40,32},{48,56},{56,48},{64,72... | collective-permute-start | bytes 786440 | tf_op jit(solution)/shard_map/ppermute | solution.py:386
  133.7 5.4 %collective-permute-start.31 = (f32[2,8,4096]{2,1,0:T(8,128)S(1)}, f32[2,8,4096]{2,1,0:T(8,128)S(1)}, u32[]{:S(2)}, u32[]{:S(2)}) collective-permute-start(f32[2,8,4096]{2,1,0:T(8,128)S(1)} %collective-permute-done.23.rest_1_), channel_id=1, source_target_pairs={{0,8},{8,0},{16,24},{24,16},{32,40},{40,32},{48,56},{56,48},{64,72... | collective-permute-start | bytes 786440 | tf_op jit(solution)/shard_map/ppermute | solution.py:386
  139.9 2.9 %collective-permute-start.28 = (f32[2,8,4096]{2,1,0:T(8,128)}, f32[2,8,4096]{2,1,0:T(8,128)}, u32[]{:S(2)}, u32[]{:S(2)}) collective-permute-start(f32[2,8,4096]{2,1,0:T(8,128)} %collective-permute-done.26.rest_4_), channel_id=1, source_target_pairs={{0,112},{8,120},{16,0},{24,8},{32,16},{40,24},{48,32},{56,40},{64,... | collective-permute-start | bytes 786440 | tf_op jit(solution)/shard_map/ppermute | solution.py:381
  145.7 3.0 %collective-permute-done.28.rest_6_ = f32[2,8,4096]{2,1,0:T(8,128)} collective-permute-done((f32[2,8,4096]{2,1,0:T(8,128)}, f32[2,8,4096]{2,1,0:T(8,128)}, u32[]{:S(2)}, u32[]{:S(2)}) %collective-permute-start.28) | collective-permute-done | bytes 262176 | tf_op jit(solution)/shard_map/ppermute | solution.py:381
  149.6 2.3 %collective-permute-done.29.rest_7_ = f32[2,8,4096]{2,1,0:T(8,128)} collective-permute-done((f32[2,8,4096]{2,1,0:T(8,128)}, f32[2,8,4096]{2,1,0:T(8,128)}, u32[]{:S(2)}, u32[]{:S(2)}) %collective-permute-start.29) | collective-permute-done | bytes 262176 | tf_op jit(solution)/shard_map/ppermute | solution.py:384
  157.0 4.6 %shard_map.115.rest_0_ = f32[16,8,4096]{2,1,0:T(8,128)} custom-call(f32[16,8,4096]{2,1,0:T(8,128)S(1)} %copy-done.1, f32[8,8,3072]{2,1,0:T(8,128)} %collective-permute-done.2.low, f32[8,8,3072]{2,1,0:T(8,128)} %collective-permute-done.3.high, f32[16,8,4096]{2,1,0:T(8,128)S(1)} %copy-done.3, f32[8,4096]{1,0:T(8,128)S(1)} %copy-done.5, f32[128,128]{1,0:T(8,128)S(1)} %copy-done.7), custom_call_target="tpu_custom_call" | custom-call | flops 419430400 | bytes 4980736 | tf_op jit(solution)/shard_map/pallas_call | solution.py:157
  161.7 4.6 %shard_map.116 = f32[16,8,4096]{2,1,0:T(8,128)} custom-call(f32[16,8,4096]{2,1,0:T(8,128)S(1)} %copy-done.1, f32[8,8,3072]{2,1,0:T(8,128)S(1)} %collective-permute-done.low, f32[8,8,3072]{2,1,0:T(8,128)} %collective-permute-done.1.high, f32[16,8,4096]{2,1,0:T(8,128)S(1)} %copy-done.3, f32[8,4096]{1,0:T(8,128)S(1)} %copy-done.5, ...), custom_call_target="tpu_custom_call", output_to_operand_aliasing={{}: (6, {})} | custom-call | flops 419430400 | bytes 4980736 | tf_op jit(solution)/shard_map/pallas_call | solution.py:157
  166.4 4.8 %shard_map.133 = f32[16,8,4096]{2,1,0:T(8,128)} custom-call(f32[16,8,4096]{2,1,0:T(8,128)S(1)} %copy-done.4, f32[2,8,4096]{2,1,0:T(8,128)S(1)} %broadcast_select_fusion.rest_0_, f32[2,8,4096]{2,1,0:T(8,128)S(1)} %copy-done.9, f32[2,8,4096]{2,1,0:T(8,128)S(1)} %copy-done.11, f32[2,8,4096]{2,1,0:T(8,128)} %collective-permute-done.25.rest_3_, ...), custom_call_target="tpu_custom_call" | custom-call | flops 805306368 | bytes 8388608 | tf_op jit(solution)/shard_map/pallas_call | solution.py:242
  (110 shorter events, 34.5 us)
Async XLA Ops:
  1.6 9.7 %collective-permute-start.4 = (f32[1,8,4096]{2,1,0:T(8,128)S(1)}, f32[1,8,4096]{2,1,0:T(8,128)S(1)}, u32[]{:S(2)}, u32[]{:S(2)}) collective-permute-start(f32[1,8,4096]{2,1,0:T(8,128)S(1)} %get-tuple-element.23), channel_id=1, source_target_pairs={{0,16},{8,24},{16,32},{24,40},{32,48},{40,56},{48,64},{56,72},{64,... | collective-permute-start | bytes 393224 | tf_op jit(solution)/shard_map/ppermute | solution.py:333
  4.2 9.4 %collective-permute-start.8 = (f32[1,8,4096]{2,1,0:T(8,128)S(1)}, f32[1,8,4096]{2,1,0:T(8,128)S(1)}, u32[]{:S(2)}, u32[]{:S(2)}) collective-permute-start(f32[1,8,4096]{2,1,0:T(8,128)S(1)} %get-tuple-element.22), channel_id=1, source_target_pairs={{0,112},{8,120},{16,0},{24,8},{32,16},{40,24},{48,32},{56,40},{64,... | collective-permute-start | bytes 393224 | tf_op jit(solution)/shard_map/ppermute | solution.py:334
  13.5 14.7 %collective-permute-start.5 = (f32[2,8,4096]{2,1,0:T(8,128)S(1)}, f32[2,8,4096]{2,1,0:T(8,128)S(1)}, u32[]{:S(2)}, u32[]{:S(2)}) collective-permute-start(f32[2,8,4096]{2,1,0:T(8,128)S(1)} %shard_map.117), channel_id=1, source_target_pairs={{0,16},{8,24},{16,32},{24,40},{32,48},{40,56},{48,64},{56,72},{64,... | collective-permute-start | bytes 786440 | tf_op jit(solution)/shard_map/ppermute | solution.py:338
  14.1 14.7 %collective-permute-start.9 = (f32[2,8,4096]{2,1,0:T(8,128)S(1)}, f32[2,8,4096]{2,1,0:T(8,128)S(1)}, u32[]{:S(2)}, u32[]{:S(2)}) collective-permute-start(f32[2,8,4096]{2,1,0:T(8,128)S(1)} %shard_map.120), channel_id=1, source_target_pairs={{0,112},{8,120},{16,0},{24,8},{32,16},{40,24},{48,32},{56,40},{64,... | collective-permute-start | bytes 786440 | tf_op jit(solution)/shard_map/ppermute | solution.py:339
  17.0 7.8 %collective-permute-start.18 = (f32[1,8,4096]{2,1,0:T(8,128)S(1)}, f32[1,8,4096]{2,1,0:T(8,128)S(1)}, u32[]{:S(2)}, u32[]{:S(2)}) collective-permute-start(f32[1,8,4096]{2,1,0:T(8,128)S(1)} %get-tuple-element.20), channel_id=1, source_target_pairs={{0,112},{8,120},{16,0},{24,8},{32,16},{40,24},{48,32},{56,40},{64,... | collective-permute-start | bytes 393224 | tf_op jit(solution)/shard_map/ppermute | solution.py:334
  28.7 9.6 %collective-permute-start.6 = (f32[2,8,4096]{2,1,0:T(8,128)S(1)}, f32[2,8,4096]{2,1,0:T(8,128)S(1)}, u32[]{:S(2)}, u32[]{:S(2)}) collective-permute-start(f32[2,8,4096]{2,1,0:T(8,128)S(1)} %shard_map.118), channel_id=1, source_target_pairs={{0,16},{8,24},{16,32},{24,40},{32,48},{40,56},{48,64},{56,72},{64,... | collective-permute-start | bytes 786440 | tf_op jit(solution)/shard_map/ppermute | solution.py:338
  29.4 9.6 %collective-permute-start.10 = (f32[2,8,4096]{2,1,0:T(8,128)S(1)}, f32[2,8,4096]{2,1,0:T(8,128)S(1)}, u32[]{:S(2)}, u32[]{:S(2)}) collective-permute-start(f32[2,8,4096]{2,1,0:T(8,128)S(1)} %shard_map.121), channel_id=1, source_target_pairs={{0,112},{8,120},{16,0},{24,8},{32,16},{40,24},{48,32},{56,40},{64,... | collective-permute-start | bytes 786440 | tf_op jit(solution)/shard_map/ppermute | solution.py:339
  32.7 11.2 %collective-permute-start.16 = (f32[2,8,4096]{2,1,0:T(8,128)S(1)}, f32[2,8,4096]{2,1,0:T(8,128)S(1)}, u32[]{:S(2)}, u32[]{:S(2)}) collective-permute-start(f32[2,8,4096]{2,1,0:T(8,128)S(1)} %shard_map.125), channel_id=1, source_target_pairs={{0,16},{8,24},{16,32},{24,40},{32,48},{40,56},{48,64},{56,72},{64,... | collective-permute-start | bytes 786440 | tf_op jit(solution)/shard_map/ppermute | solution.py:338
  33.4 11.2 %collective-permute-start.20 = (f32[2,8,4096]{2,1,0:T(8,128)S(1)}, f32[2,8,4096]{2,1,0:T(8,128)S(1)}, u32[]{:S(2)}, u32[]{:S(2)}) collective-permute-start(f32[2,8,4096]{2,1,0:T(8,128)S(1)} %shard_map.128), channel_id=1, source_target_pairs={{0,112},{8,120},{16,0},{24,8},{32,16},{40,24},{48,32},{56,40},{64,... | collective-permute-start | bytes 786440 | tf_op jit(solution)/shard_map/ppermute | solution.py:339
  38.9 10.7 %collective-permute-start.7 = (f32[2,8,4096]{2,1,0:T(8,128)S(1)}, f32[2,8,4096]{2,1,0:T(8,128)S(1)}, u32[]{:S(2)}, u32[]{:S(2)}) collective-permute-start(f32[2,8,4096]{2,1,0:T(8,128)S(1)} %shard_map.119), channel_id=1, source_target_pairs={{0,16},{8,24},{16,32},{24,40},{32,48},{40,56},{48,64},{56,72},{64,... | collective-permute-start | bytes 786440 | tf_op jit(solution)/shard_map/ppermute | solution.py:338
  39.6 10.0 %collective-permute-start.11 = (f32[2,8,4096]{2,1,0:T(8,128)S(1)}, f32[2,8,4096]{2,1,0:T(8,128)S(1)}, u32[]{:S(2)}, u32[]{:S(2)}) collective-permute-start(f32[2,8,4096]{2,1,0:T(8,128)S(1)} %shard_map.122), channel_id=1, source_target_pairs={{0,112},{8,120},{16,0},{24,8},{32,16},{40,24},{48,32},{56,40},{64,... | collective-permute-start | bytes 786440 | tf_op jit(solution)/shard_map/ppermute | solution.py:339
  44.6 11.1 %collective-permute-start.17 = (f32[2,8,4096]{2,1,0:T(8,128)S(1)}, f32[2,8,4096]{2,1,0:T(8,128)S(1)}, u32[]{:S(2)}, u32[]{:S(2)}) collective-permute-start(f32[2,8,4096]{2,1,0:T(8,128)S(1)} %shard_map.126), channel_id=1, source_target_pairs={{0,16},{8,24},{16,32},{24,40},{32,48},{40,56},{48,64},{56,72},{64,... | collective-permute-start | bytes 786440 | tf_op jit(solution)/shard_map/ppermute | solution.py:338
  45.2 10.4 %collective-permute-start.21 = (f32[2,8,4096]{2,1,0:T(8,128)S(1)}, f32[2,8,4096]{2,1,0:T(8,128)S(1)}, u32[]{:S(2)}, u32[]{:S(2)}) collective-permute-start(f32[2,8,4096]{2,1,0:T(8,128)S(1)} %shard_map.129), channel_id=1, source_target_pairs={{0,112},{8,120},{16,0},{24,8},{32,16},{40,24},{48,32},{56,40},{64,... | collective-permute-start | bytes 786440 | tf_op jit(solution)/shard_map/ppermute | solution.py:339
  50.2 8.3 %collective-permute-start.12 = (f32[2,8,3072]{2,1,0:T(8,128)S(1)}, f32[2,8,3072]{2,1,0:T(8,128)S(1)}, u32[]{:S(2)}, u32[]{:S(2)}) collective-permute-start(f32[2,8,3072]{2,1,0:T(8,128)S(1)} %get-tuple-element.16), channel_id=1, source_target_pairs={{0,1},{1,2},{2,3},{3,4},{4,5},{5,6},{6,7},{7,0},{8,9},{9,10},{10,1... | collective-permute-start | bytes 589832 | tf_op jit(solution)/shard_map/ppermute | solution.py:345
  60.2 14.6 %collective-permute-start.22 = (f32[2,8,4096]{2,1,0:T(8,128)S(1)}, f32[2,8,4096]{2,1,0:T(8,128)}, u32[]{:S(2)}, u32[]{:S(2)}) collective-permute-start(f32[2,8,4096]{2,1,0:T(8,128)S(1)} %shard_map.131), channel_id=1, source_target_pairs={{0,128},{8,136},{16,144},{24,152},{32,160},{40,168},{48,176},{56,1... | collective-permute-start | bytes 786440 | tf_op jit(solution)/shard_map/ppermute | solution.py:371
  62.7 22.5 %collective-permute-start.2 = (f32[8,8,3072]{2,1,0:T(8,128)}, f32[8,8,3072]{2,1,0:T(8,128)}, u32[]{:S(2)}, u32[]{:S(2)}) collective-permute-start(f32[8,8,3072]{2,1,0:T(8,128)} %get-tuple-element.13), channel_id=1, source_target_pairs={{0,1},{1,2},{2,3},{3,4},{4,5},{5,6},{6,7},{7,0},{8,9},{9,10},{10,1... | collective-permute-start | bytes 2359304 | tf_op jit(solution)/shard_map/ppermute | solution.py:345
  65.1 34.9 %collective-permute-start.3 = (f32[8,8,3072]{2,1,0:T(8,128)}, f32[8,8,3072]{2,1,0:T(8,128)}, u32[]{:S(2)}, u32[]{:S(2)}) collective-permute-start(f32[8,8,3072]{2,1,0:T(8,128)} %get-tuple-element.14), channel_id=1, source_target_pairs={{1,0},{2,1},{3,2},{4,3},{5,4},{6,5},{7,6},{0,7},{9,8},{10,9},{11,1... | collective-permute-start | bytes 2359304 | tf_op jit(solution)/shard_map/ppermute | solution.py:346
  69.7 49.1 %collective-permute-start = (f32[8,8,3072]{2,1,0:T(8,128)}, f32[8,8,3072]{2,1,0:T(8,128)S(1)}, u32[]{:S(2)}, u32[]{:S(2)}) collective-permute-start(f32[8,8,3072]{2,1,0:T(8,128)} %get-tuple-element.11), channel_id=1, source_target_pairs={{0,1},{1,2},{2,3},{3,4},{4,5},{5,6},{6,7},{7,0},{8,9},{9,10},{10,1... | collective-permute-start | bytes 2359304 | tf_op jit(solution)/shard_map/ppermute | solution.py:345
  69.7 64.0 %collective-permute-start.1 = (f32[8,8,3072]{2,1,0:T(8,128)}, f32[8,8,3072]{2,1,0:T(8,128)}, u32[]{:S(2)}, u32[]{:S(2)}) collective-permute-start(f32[8,8,3072]{2,1,0:T(8,128)} %get-tuple-element.12), channel_id=1, source_target_pairs={{1,0},{2,1},{3,2},{4,3},{5,4},{6,5},{7,6},{0,7},{9,8},{10,9},{11,1... | collective-permute-start | bytes 2359304 | tf_op jit(solution)/shard_map/ppermute | solution.py:346
  74.8 12.9 %collective-permute-start.23 = (f32[2,8,4096]{2,1,0:T(8,128)S(1)}, f32[2,8,4096]{2,1,0:T(8,128)S(1)}, u32[]{:S(2)}, u32[]{:S(2)}) collective-permute-start(f32[2,8,4096]{2,1,0:T(8,128)S(1)} %broadcast_select_fusion.rest_0_), channel_id=1, source_target_pairs={{0,16},{8,24},{16,32},{24,40},{32,48},{40,56},{48,64},{56,72},{64,... | collective-permute-start | bytes 786440 | tf_op jit(solution)/shard_map/ppermute | solution.py:380
  91.0 48.8 %collective-permute-start.26 = (f32[2,8,4096]{2,1,0:T(8,128)S(1)}, f32[2,8,4096]{2,1,0:T(8,128)}, u32[]{:S(2)}, u32[]{:S(2)}) collective-permute-start(f32[2,8,4096]{2,1,0:T(8,128)S(1)} %collective-permute-done.24.rest_2_), channel_id=1, source_target_pairs={{0,112},{8,120},{16,0},{24,8},{32,16},{40,24},{48,32},{56,40},{64,... | collective-permute-start | bytes 786440 | tf_op jit(solution)/shard_map/ppermute | solution.py:381
  94.6 48.2 %collective-permute-start.27 = (f32[2,8,4096]{2,1,0:T(8,128)}, f32[2,8,4096]{2,1,0:T(8,128)}, u32[]{:S(2)}, u32[]{:S(2)}) collective-permute-start(f32[2,8,4096]{2,1,0:T(8,128)} %collective-permute-done.25.rest_3_), channel_id=1, source_target_pairs={{0,16},{8,24},{16,32},{24,40},{32,48},{40,56},{48,64},{56,72},{64,... | collective-permute-start | bytes 786440 | tf_op jit(solution)/shard_map/ppermute | solution.py:380
  100.0 42.8 %collective-permute-start.30 = (f32[2,8,4096]{2,1,0:T(8,128)S(1)}, f32[2,8,4096]{2,1,0:T(8,128)S(1)}, u32[]{:S(2)}, u32[]{:S(2)}) collective-permute-start(f32[2,8,4096]{2,1,0:T(8,128)S(1)} %broadcast_select_fusion.rest_0_), channel_id=1, source_target_pairs={{0,8},{8,0},{16,24},{24,16},{32,40},{40,32},{48,56},{56,48},{64,72... | collective-permute-start | bytes 786440 | tf_op jit(solution)/shard_map/ppermute | solution.py:386
  118.8 25.0 %collective-permute-start.32 = (f32[2,8,4096]{2,1,0:T(8,128)S(1)}, f32[2,8,4096]{2,1,0:T(8,128)S(1)}, u32[]{:S(2)}, u32[]{:S(2)}) collective-permute-start(f32[2,8,4096]{2,1,0:T(8,128)S(1)} %collective-permute-done.24.rest_2_), channel_id=1, source_target_pairs={{0,8},{8,0},{16,24},{24,16},{32,40},{40,32},{48,56},{56,48},{64,72... | collective-permute-start | bytes 786440 | tf_op jit(solution)/shard_map/ppermute | solution.py:386
  133.7 11.0 %collective-permute-start.31 = (f32[2,8,4096]{2,1,0:T(8,128)S(1)}, f32[2,8,4096]{2,1,0:T(8,128)S(1)}, u32[]{:S(2)}, u32[]{:S(2)}) collective-permute-start(f32[2,8,4096]{2,1,0:T(8,128)S(1)} %collective-permute-done.23.rest_1_), channel_id=1, source_target_pairs={{0,8},{8,0},{16,24},{24,16},{32,40},{40,32},{48,56},{56,48},{64,72... | collective-permute-start | bytes 786440 | tf_op jit(solution)/shard_map/ppermute | solution.py:386
  139.9 8.9 %collective-permute-start.28 = (f32[2,8,4096]{2,1,0:T(8,128)}, f32[2,8,4096]{2,1,0:T(8,128)}, u32[]{:S(2)}, u32[]{:S(2)}) collective-permute-start(f32[2,8,4096]{2,1,0:T(8,128)} %collective-permute-done.26.rest_4_), channel_id=1, source_target_pairs={{0,112},{8,120},{16,0},{24,8},{32,16},{40,24},{48,32},{56,40},{64,... | collective-permute-start | bytes 786440 | tf_op jit(solution)/shard_map/ppermute | solution.py:381
  142.8 9.1 %collective-permute-start.29 = (f32[2,8,4096]{2,1,0:T(8,128)}, f32[2,8,4096]{2,1,0:T(8,128)}, u32[]{:S(2)}, u32[]{:S(2)}) collective-permute-start(f32[2,8,4096]{2,1,0:T(8,128)} %collective-permute-done.27.rest_5_), channel_id=1, source_target_pairs={{0,16},{8,24},{16,32},{24,40},{32,48},{40,56},{48,64},{56,72},{64,... | collective-permute-start | bytes 786440 | tf_op jit(solution)/shard_map/ppermute | solution.py:384
  143.5 22.8 %collective-permute-start.34 = (f32[2,8,4096]{2,1,0:T(8,128)}, f32[2,8,4096]{2,1,0:T(8,128)}, u32[]{:S(2)}, u32[]{:S(2)}) collective-permute-start(f32[2,8,4096]{2,1,0:T(8,128)} %collective-permute-done.26.rest_4_), channel_id=1, source_target_pairs={{0,8},{8,0},{16,24},{24,16},{32,40},{40,32},{48,56},{56,48},{64,72... | collective-permute-start | bytes 786440 | tf_op jit(solution)/shard_map/ppermute | solution.py:386
  144.5 21.8 %collective-permute-start.33 = (f32[2,8,4096]{2,1,0:T(8,128)}, f32[2,8,4096]{2,1,0:T(8,128)}, u32[]{:S(2)}, u32[]{:S(2)}) collective-permute-start(f32[2,8,4096]{2,1,0:T(8,128)} %collective-permute-done.25.rest_3_), channel_id=1, source_target_pairs={{0,8},{8,0},{16,24},{24,16},{32,40},{40,32},{48,56},{56,48},{64,72... | collective-permute-start | bytes 786440 | tf_op jit(solution)/shard_map/ppermute | solution.py:386
  145.4 20.9 %collective-permute-start.35 = (f32[2,8,4096]{2,1,0:T(8,128)}, f32[2,8,4096]{2,1,0:T(8,128)}, u32[]{:S(2)}, u32[]{:S(2)}) collective-permute-start(f32[2,8,4096]{2,1,0:T(8,128)} %collective-permute-done.27.rest_5_), channel_id=1, source_target_pairs={{0,8},{8,0},{16,24},{24,16},{32,40},{40,32},{48,56},{56,48},{64,72... | collective-permute-start | bytes 786440 | tf_op jit(solution)/shard_map/ppermute | solution.py:386
  148.7 17.6 %collective-permute-start.36 = (f32[2,8,4096]{2,1,0:T(8,128)}, f32[2,8,4096]{2,1,0:T(8,128)}, u32[]{:S(2)}, u32[]{:S(2)}) collective-permute-start(f32[2,8,4096]{2,1,0:T(8,128)} %collective-permute-done.28.rest_6_), channel_id=1, source_target_pairs={{0,8},{8,0},{16,24},{24,16},{32,40},{40,32},{48,56},{56,48},{64,72... | collective-permute-start | bytes 786440 | tf_op jit(solution)/shard_map/ppermute | solution.py:386
  151.9 14.5 %collective-permute-start.37 = (f32[2,8,4096]{2,1,0:T(8,128)}, f32[2,8,4096]{2,1,0:T(8,128)}, u32[]{:S(2)}, u32[]{:S(2)}) collective-permute-start(f32[2,8,4096]{2,1,0:T(8,128)} %collective-permute-done.29.rest_7_), channel_id=1, source_target_pairs={{0,8},{8,0},{16,24},{24,16},{32,40},{40,32},{48,56},{56,48},{64,72... | collective-permute-start | bytes 786440 | tf_op jit(solution)/shard_map/ppermute | solution.py:386
  (26 other events, 204.5 us)

commit v2 on v1

--- a/solution.py
+++ b/solution.py
@@ -1,3 +1,5 @@
+import math
+
 import numpy as np
 import jax
 import jax.numpy as jnp
@@ -69,7 +71,7 @@
     n = n or orb.shape[0]
     planes, cells = orb.shape[1:]
     thin = cells * WIDTH // planes
-    step = min(n, 4)
+    step = math.gcd(4, n, first)
     return pl.pallas_call(
         pack_body,
         grid=(n // step,),
@@ -134,20 +136,20 @@
         filter_one(i, orb, low, high, prev, pot, mat, *rest[-4:])
 
 
-def apply_filter(orb, low, high, prev, pot, first=0, into=None):
-    total, planes, cells = orb.shape
-    n = low.shape[0]
+def apply_filter(orb, low, high, prev, pot, first=0, n=None, side=0, out=0, into=None, total=None):
+    planes, cells = orb.shape[1:]
+    n = n or low.shape[0]
+    total = total or orb.shape[0]
     tiles = cells // LANES
     thin = cells * WIDTH // planes
-    step = min(n, 4)
-    whole = pl.BlockSpec((step, planes, cells), lambda i: (i + first // step, 0, 0))
-    side = pl.BlockSpec((step, planes, thin), lambda i: (i, 0, 0))
+    step = math.gcd(4, n, first, side, out)
+    block = lambda start, width: pl.BlockSpec((step, planes, width), lambda i: (i + start // step, 0, 0))
     args = [orb, low, high, prev, pot, jnp.asarray(row_matrix())]
     specs = [
-        whole,
-        side,
-        side,
-        whole,
+        block(first, cells),
+        block(side, thin),
+        block(side, thin),
+        block(first, cells),
         pl.BlockSpec((planes, cells), lambda i: (0, 0)),
         pl.BlockSpec((LANES, LANES), lambda i: (0, 0)),
     ]
@@ -158,7 +160,7 @@
         filter_body,
         grid=(n // step,),
         in_specs=specs,
-        out_specs=whole,
+        out_specs=block(out, cells),
         out_shape=jax.ShapeDtypeStruct((total, planes, cells), jnp.float32),
         input_output_aliases={} if into is None else {6: 0},
         scratch_shapes=[
@@ -325,6 +327,41 @@
     )(place, block, up, down)
 
 
+def keep_body(flag, mine, other, out):
+    out[...] = jnp.where(flag[0] == 1, mine[...], other[...])
+
+
+def keep(flag, mine, other):
+    whole = pl.BlockSpec(memory_space=pltpu.VMEM)
+    return pl.pallas_call(
+        keep_body,
+        in_specs=[pl.BlockSpec(memory_space=pltpu.SMEM), whole, whole],
+        out_specs=whole,
+        out_shape=jax.ShapeDtypeStruct(mine.shape, jnp.float32),
+        compiler_params=room(2),
+        cost_estimate=pl.CostEstimate(flops=0, bytes_accessed=12 * mine.size, transcendentals=0),
+    )(flag, mine, other)
+
+
+def stack_body(*refs):
+    out = refs[-1]
+    for i, ref in enumerate(refs[:-1]):
+        out[i] = ref[0]
+
+
+def stacked(blocks):
+    whole = pl.BlockSpec(memory_space=pltpu.VMEM)
+    shape = (len(blocks),) + blocks[0].shape[1:]
+    return pl.pallas_call(
+        stack_body,
+        in_specs=[whole] * len(blocks),
+        out_specs=whole,
+        out_shape=jax.ShapeDtypeStruct(shape, jnp.float32),
+        compiler_params=room(3),
+        cost_estimate=pl.CostEstimate(flops=0, bytes_accessed=8 * math.prod(shape), transcendentals=0),
+    )(*blocks)
+
+
 def relay(block, place, packed):
     share = block.shape[0] // RING
     half = share // 2
@@ -357,7 +394,7 @@
 
     offset = (z - root_z) & (RING - 1)
 
-    early = count // 2
+    early = count * 5 // 8
     ends = pack(orbitals, 0, early)
     sides_early = halo(*ends)
     ends = pack(orbitals, early, count - early)
@@ -367,23 +404,32 @@
     piece, *ends = relay(orbitals, place, True)
     (before,) = relay(previous, place, False)
     below, above = halo(*ends)
-    piece = apply_filter(piece, below, above, before, potential)
-    other = lax.ppermute(piece, "band", ACROSS)
-    piece = jnp.where(x == root_x, piece, other)
     filtered = apply_filter(orbitals, *sides_early, previous, potential)
-    filtered = apply_filter(orbitals, *sides_late, previous, potential, early, filtered)
-
-    blocks = [piece]
-    plan = [(0, 0), (0, 1)]
-    up = down = piece
-    for hop in (1, 2, 3):
-        up = lax.ppermute(up, "band", ONWARD)
-        down = lax.ppermute(down, "band", BACK)
-        blocks += [up, down]
-        plan += [(-hop, 0), (-hop, 1), (hop, 0), (hop, 1)]
-    blocks += [lax.ppermute(up, "band", ONWARD)]
-    plan += [(-4, 0), (-4, 1)]
-    blocks += [lax.ppermute(b, "band", PARTNER) for b in blocks]
+    filtered = apply_filter(orbitals, *sides_late, previous, potential, early, out=early, into=filtered)
+
+    flag = (x == root_x).astype(jnp.int32)[None]
+    chains = []
+    for m in range(share):
+        mine = apply_filter(piece, below, above, before, potential, m, 1, m, total=1)
+        other = lax.ppermute(mine, "band", ACROSS)
+        chains.append([keep(flag, mine, other)] * 2)
+    rounds = [[(chain[0], 0, m) for m, chain in enumerate(chains)]]
+    for hop in range(1, RING // 2 + 1):
+        rounds.append([])
+        for m, chain in enumerate(chains):
+            for way, pairs in enumerate((ONWARD, BACK)):
+                if hop == RING // 2 and way != m % 2:
+                    continue
+                chain[way] = lax.ppermute(chain[way], "band", pairs)
+                rounds[-1].append((chain[way], hop if way else -hop, m))
+    rounds[:2] = [rounds[0] + rounds[1]]
+    mine, theirs, plan = [], [], []
+    for arrived in rounds:
+        mine += [block for block, _, _ in arrived]
+        plan += [(off, m) for _, off, m in arrived]
+        group = stacked([block for block, _, _ in arrived])
+        theirs.append(lax.ppermute(group, "band", PARTNER))
+    blocks = mine + theirs
     plan = [(o, i, c) for c in range(CORES) for o, i in plan]
     coefficients = weights(rotation, plan, z, core, chip, share, orbitals.shape[1])
     rotated = add_panel(accumulated, blocks, *coefficients)

time: 172 us -> 154 us (0.90)
  waiting for transfers between devices: 50.2 us -> 35.3 us
  starting transfers between devices: 83.8 us -> 72.6 us
  Pallas kernels: 25.8 us -> 34.4 us
    ppermute x16 -> x20, waiting for transfers between devices: 8.65 us -> 19.8 us  [the longest x2 15.9 us: step(): other = lax.ppermute(mine, 'band', ACROSS)]
    ppermute x16 -> x20, starting transfers between devices: 41.2 us -> 30.4 us  [the longest x14 18.9 us: step(): chain[way] = lax.ppermute(chain[way], 'band', pairs)]
    ppermute x3, waiting for transfers between devices: 21 us -> 11 us  [halo(): lax.ppermute(tail, 'domain', [(i, (i + 1) % size) for i in range(size)])]
    ppermute x2, waiting for transfers between devices: 6.9 us -> 1.29 us  [relay(): lax.ppermute(lax.dynamic_slice(block, (start, 0, 0), size), 'band', ONWARD)]
    ppermute x3, waiting for transfers between devices: 8.38 us -> 3.12 us  [halo(): lax.ppermute(head, 'domain', [((i + 1) % size, i) for i in range(size)])]
    pallas_call x0 -> x6, Pallas kernels: none -> 5.24 us  [the longest x4 3.33 us: stacked(): pl.pallas_call(stack_body, in_specs=[whole] * len(blocks), out_specs=whol...]
    ppermute x6, waiting for transfers between devices: 5.3 us -> 0.08 us  [relay(): up = lax.ppermute(up, 'band', ONWARD)]
    ppermute x6, starting transfers between devices: 16.6 us -> 13.3 us  [relay(): down = lax.ppermute(down, 'band', BACK)]
  transfers between devices with their start and end apart: 38 -> 42, of which waited for: 14 -> 7; matrix products, arithmetic and copies ran while one was open for 0% -> 1% of each run, Pallas kernels for 12% -> 19%
where the time goes in v2:
time: 154 us; the launch traced here: 153 us
  starting transfers between devices  72.6 us (47%)
  waiting for transfers between devices  35.3 us (23%)
  Pallas kernels  34.4 us (22%)
  local copies, waits for them, and re-layouts  8.9 us (6%)
  between operations  1.98 us (1%)
    ppermute x14, starting transfers between devices, step(): chain[way] = lax.ppermute(chain[way], 'band', pairs)  18.9 us
    ppermute x2, waiting for transfers between devices, step(): other = lax.ppermute(mine, 'band', ACROSS)  15.9 us
    ppermute x6, starting transfers between devices, relay(): down = lax.ppermute(down, 'band', BACK)  13.3 us
    pallas_call x4, Pallas kernels, apply_filter(): pl.pallas_call(filter_body, grid=(n // step,), in_specs=specs, out_specs=...  12 us
    ppermute x4, starting transfers between devices, step(): theirs.append(lax.ppermute(group, 'band', PARTNER))  11.1 us
    ppermute x3, waiting for transfers between devices, halo(): lax.ppermute(tail, 'domain', [(i, (i + 1) % size) for i in range(size)])  11 us
    ppermute x3, starting transfers between devices, halo(): lax.ppermute(head, 'domain', [((i + 1) % size, i) for i in range(size)])  10.7 us
    unnamed x80, local copies, waits for them, and re-layouts  6.92 us
  transfers between devices with their start and end apart: 42, of which 7 were waited for; matrix products, arithmetic and copies ran while one was open for 1% of the time, Pallas kernels for 19%

profile of v2, /device:TPU:1, one launch (start us, length us, event | category | flops | bytes accessed | tf_op | source)
XLA Modules:
  0.0 153.3 jit_solution(18117117729266819298)
XLA Ops:
  1.6 2.5 %collective-permute-start.4 = (f32[1,8,4096]{2,1,0:T(8,128)S(1)}, f32[1,8,4096]{2,1,0:T(8,128)S(1)}, u32[]{:S(2)}, u32[]{:S(2)}) collective-permute-start(f32[1,8,4096]{2,1,0:T(8,128)S(1)} %get-tuple-element.23), channel_id=1, source_target_pairs={{0,16},{8,24},{16,32},{24,40},{32,48},{40,56},{48,64},{56,72},{64,... | collective-permute-start | bytes 393224 | tf_op jit(solution)/shard_map/ppermute | solution.py:370
  5.2 1.7 %collective-permute-start.14 = (f32[1,8,4096]{2,1,0:T(8,128)S(1)}, f32[1,8,4096]{2,1,0:T(8,128)S(1)}, u32[]{:S(2)}, u32[]{:S(2)}) collective-permute-start(f32[1,8,4096]{2,1,0:T(8,128)S(1)} %get-tuple-element.21), channel_id=1, source_target_pairs={{0,16},{8,24},{16,32},{24,40},{32,48},{40,56},{48,64},{56,72},{64,... | collective-permute-start | bytes 393224 | tf_op jit(solution)/shard_map/ppermute | solution.py:370
  6.9 2.4 %collective-permute-start.8 = (f32[1,8,4096]{2,1,0:T(8,128)S(1)}, f32[1,8,4096]{2,1,0:T(8,128)S(1)}, u32[]{:S(2)}, u32[]{:S(2)}) collective-permute-start(f32[1,8,4096]{2,1,0:T(8,128)S(1)} %get-tuple-element.22), channel_id=1, source_target_pairs={{0,112},{8,120},{16,0},{24,8},{32,16},{40,24},{48,32},{56,40},{64,... | collective-permute-start | bytes 393224 | tf_op jit(solution)/shard_map/ppermute | solution.py:371
  11.3 1.6 %copy-done = f32[16,8,4096]{2,1,0:T(8,128)S(1)} copy-done((f32[16,8,4096]{2,1,0:T(8,128)S(1)}, f32[16,8,4096]{2,1,0:T(8,128)}, u32[]{:S(2)}) %copy-start) | copy-done | bytes 2097176
  13.6 2.7 %collective-permute-start.18 = (f32[1,8,4096]{2,1,0:T(8,128)S(1)}, f32[1,8,4096]{2,1,0:T(8,128)S(1)}, u32[]{:S(2)}, u32[]{:S(2)}) collective-permute-start(f32[1,8,4096]{2,1,0:T(8,128)S(1)} %get-tuple-element.20), channel_id=1, source_target_pairs={{0,112},{8,120},{16,0},{24,8},{32,16},{40,24},{48,32},{56,40},{64,... | collective-permute-start | bytes 393224 | tf_op jit(solution)/shard_map/ppermute | solution.py:371
  19.6 2.3 %collective-permute-start.19 = (f32[2,8,4096]{2,1,0:T(8,128)S(1)}, f32[2,8,4096]{2,1,0:T(8,128)S(1)}, u32[]{:S(2)}, u32[]{:S(2)}) collective-permute-start(f32[2,8,4096]{2,1,0:T(8,128)S(1)} %shard_map.136), channel_id=1, source_target_pairs={{0,112},{8,120},{16,0},{24,8},{32,16},{40,24},{48,32},{56,40},{64,... | collective-permute-start | bytes 786440 | tf_op jit(solution)/shard_map/ppermute | solution.py:376
  22.6 2.3 %shard_map.123 = (f32[10,8,3072]{2,1,0:T(8,128)}, f32[10,8,3072]{2,1,0:T(8,128)}) custom-call(f32[16,8,4096]{2,1,0:T(8,128)S(1)} %copy-done.1), custom_call_target="tpu_custom_call" | custom-call | bytes 3276800 | tf_op jit(solution)/shard_map/pallas_call | solution.py:75
  24.9 2.7 %collective-permute-start.2 = (f32[10,8,3072]{2,1,0:T(8,128)}, f32[10,8,3072]{2,1,0:T(8,128)S(1)}, u32[]{:S(2)}, u32[]{:S(2)}) collective-permute-start(f32[10,8,3072]{2,1,0:T(8,128)} %get-tuple-element.13), channel_id=1, source_target_pairs={{0,1},{1,2},{2,3},{3,4},{4,5},{5,6},{6,7},{7,0},{8,9},{9,10},{10,1... | collective-permute-start | bytes 2949128 | tf_op jit(solution)/shard_map/ppermute | solution.py:382
  28.2 2.7 %collective-permute-start.10 = (f32[2,8,4096]{2,1,0:T(8,128)S(1)}, f32[2,8,4096]{2,1,0:T(8,128)S(1)}, u32[]{:S(2)}, u32[]{:S(2)}) collective-permute-start(f32[2,8,4096]{2,1,0:T(8,128)S(1)} %shard_map.130), channel_id=1, source_target_pairs={{0,112},{8,120},{16,0},{24,8},{32,16},{40,24},{48,32},{56,40},{64,... | collective-permute-start | bytes 786440 | tf_op jit(solution)/shard_map/ppermute | solution.py:376
  32.2 2.7 %collective-permute-start.20 = (f32[2,8,4096]{2,1,0:T(8,128)S(1)}, f32[2,8,4096]{2,1,0:T(8,128)S(1)}, u32[]{:S(2)}, u32[]{:S(2)}) collective-permute-start(f32[2,8,4096]{2,1,0:T(8,128)S(1)} %shard_map.137), channel_id=1, source_target_pairs={{0,112},{8,120},{16,0},{24,8},{32,16},{40,24},{48,32},{56,40},{64,... | collective-permute-start | bytes 786440 | tf_op jit(solution)/shard_map/ppermute | solution.py:376
  36.2 2.7 %collective-permute-start.11 = (f32[2,8,4096]{2,1,0:T(8,128)S(1)}, f32[2,8,4096]{2,1,0:T(8,128)S(1)}, u32[]{:S(2)}, u32[]{:S(2)}) collective-permute-start(f32[2,8,4096]{2,1,0:T(8,128)S(1)} %shard_map.131), channel_id=1, source_target_pairs={{0,112},{8,120},{16,0},{24,8},{32,16},{40,24},{48,32},{56,40},{64,... | collective-permute-start | bytes 786440 | tf_op jit(solution)/shard_map/ppermute | solution.py:376
  43.2 2.7 %collective-permute-start.21 = (f32[2,8,4096]{2,1,0:T(8,128)S(1)}, f32[2,8,4096]{2,1,0:T(8,128)S(1)}, u32[]{:S(2)}, u32[]{:S(2)}) collective-permute-start(f32[2,8,4096]{2,1,0:T(8,128)S(1)} %shard_map.138), channel_id=1, source_target_pairs={{0,112},{8,120},{16,0},{24,8},{32,16},{40,24},{48,32},{56,40},{64,... | collective-permute-start | bytes 786440 | tf_op jit(solution)/shard_map/ppermute | solution.py:376
  46.6 2.7 %collective-permute-start.12 = (f32[2,8,3072]{2,1,0:T(8,128)S(1)}, f32[2,8,3072]{2,1,0:T(8,128)S(1)}, u32[]{:S(2)}, u32[]{:S(2)}) collective-permute-start(f32[2,8,3072]{2,1,0:T(8,128)S(1)} %get-tuple-element.16), channel_id=1, source_target_pairs={{0,1},{1,2},{2,3},{3,4},{4,5},{5,6},{6,7},{7,0},{8,9},{9,10},{10,1... | collective-permute-start | bytes 589832 | tf_op jit(solution)/shard_map/ppermute | solution.py:382
  49.3 3.8 %collective-permute-start.13 = (f32[2,8,3072]{2,1,0:T(8,128)S(1)}, f32[2,8,3072]{2,1,0:T(8,128)S(1)}, u32[]{:S(2)}, u32[]{:S(2)}) collective-permute-start(f32[2,8,3072]{2,1,0:T(8,128)S(1)} %get-tuple-element.17), channel_id=1, source_target_pairs={{1,0},{2,1},{3,2},{4,3},{5,4},{6,5},{7,6},{0,7},{9,8},{10,9},{11,1... | collective-permute-start | bytes 589832 | tf_op jit(solution)/shard_map/ppermute | solution.py:383
  53.8 11.0 %collective-permute-done.12.low = f32[2,8,3072]{2,1,0:T(8,128)S(1)} collective-permute-done((f32[2,8,3072]{2,1,0:T(8,128)S(1)}, f32[2,8,3072]{2,1,0:T(8,128)S(1)}, u32[]{:S(2)}, u32[]{:S(2)}) %collective-permute-start.12) | collective-permute-done | bytes 196640 | tf_op jit(solution)/shard_map/ppermute | solution.py:382
  64.7 3.1 %collective-permute-done.13.high = f32[2,8,3072]{2,1,0:T(8,128)S(1)} collective-permute-done((f32[2,8,3072]{2,1,0:T(8,128)S(1)}, f32[2,8,3072]{2,1,0:T(8,128)S(1)}, u32[]{:S(2)}, u32[]{:S(2)}) %collective-permute-start.13) | collective-permute-done | bytes 196640 | tf_op jit(solution)/shard_map/ppermute | solution.py:383
  69.1 3.4 %collective-permute-start.3 = (f32[10,8,3072]{2,1,0:T(8,128)}, f32[10,8,3072]{2,1,0:T(8,128)}, u32[]{:S(2)}, u32[]{:S(2)}) collective-permute-start(f32[10,8,3072]{2,1,0:T(8,128)} %get-tuple-element.14), channel_id=1, source_target_pairs={{1,0},{2,1},{3,2},{4,3},{5,4},{6,5},{7,6},{0,7},{9,8},{10,9},{11,1... | collective-permute-start | bytes 2949128 | tf_op jit(solution)/shard_map/ppermute | solution.py:383
  74.6 2.7 %collective-permute-start.25 = (f32[1,8,4096]{2,1,0:T(8,128)S(1)}, f32[1,8,4096]{2,1,0:T(8,128)S(1)}, u32[]{:S(2)}, u32[]{:S(2)}) collective-permute-start(f32[1,8,4096]{2,1,0:T(8,128)S(1)} %shard_map.141.refs_0_.rest_0_), channel_id=1, source_target_pairs={{0,112},{8,120},{16,0},{24,8},{32,16},{40,24},{48,32},{56,40},{64,... | collective-permute-start | bytes 393224 | tf_op jit(solution)/shard_map/ppermute | solution.py:423
  77.3 15.9 %collective-permute-done.23.other = f32[1,8,4096]{2,1,0:T(8,128)S(1)} collective-permute-done((f32[1,8,4096]{2,1,0:T(8,128)}, f32[1,8,4096]{2,1,0:T(8,128)S(1)}, u32[]{:S(2)}, u32[]{:S(2)}) %collective-permute-start.23) | collective-permute-done | bytes 131104 | tf_op jit(solution)/shard_map/ppermute | solution.py:414
  95.7 2.7 %collective-permute-start.27 = (f32[1,8,4096]{2,1,0:T(8,128)S(1)}, f32[1,8,4096]{2,1,0:T(8,128)S(1)}, u32[]{:S(2)}, u32[]{:S(2)}) collective-permute-start(f32[1,8,4096]{2,1,0:T(8,128)S(1)} %shard_map.143.refs_1_.rest_1_), channel_id=1, source_target_pairs={{0,112},{8,120},{16,0},{24,8},{32,16},{40,24},{48,32},{56,40},{64,... | collective-permute-start | bytes 393224 | tf_op jit(solution)/shard_map/ppermute | solution.py:423
  98.5 2.7 %collective-permute-start.29 = (f32[1,8,4096]{2,1,0:T(8,128)S(1)}, f32[1,8,4096]{2,1,0:T(8,128)S(1)}, u32[]{:S(2)}, u32[]{:S(2)}) collective-permute-start(f32[1,8,4096]{2,1,0:T(8,128)S(1)} %collective-permute-done.25.refs_3_.rest_3_), channel_id=1, source_target_pairs={{0,112},{8,120},{16,0},{24,8},{32,16},{40,24},{48,32},{56,40},{64,... | collective-permute-start | bytes 393224 | tf_op jit(solution)/shard_map/ppermute | solution.py:423
  101.2 2.7 %collective-permute-start.31 = (f32[1,8,4096]{2,1,0:T(8,128)S(1)}, f32[1,8,4096]{2,1,0:T(8,128)S(1)}, u32[]{:S(2)}, u32[]{:S(2)}) collective-permute-start(f32[1,8,4096]{2,1,0:T(8,128)S(1)} %collective-permute-done.27.refs_5_.rest_5_), channel_id=1, source_target_pairs={{0,112},{8,120},{16,0},{24,8},{32,16},{40,24},{48,32},{56,40},{64,... | collective-permute-start | bytes 393224 | tf_op jit(solution)/shard_map/ppermute | solution.py:423
  103.8 2.7 %collective-permute-start.33 = (f32[1,8,4096]{2,1,0:T(8,128)S(1)}, f32[1,8,4096]{2,1,0:T(8,128)S(1)}, u32[]{:S(2)}, u32[]{:S(2)}) collective-permute-start(f32[1,8,4096]{2,1,0:T(8,128)S(1)} %collective-permute-done.29.refs_1_.rest_7_), channel_id=1, source_target_pairs={{0,112},{8,120},{16,0},{24,8},{32,16},{40,24},{48,32},{56,40},{64,... | collective-permute-start | bytes 393224 | tf_op jit(solution)/shard_map/ppermute | solution.py:423
  106.9 2.7 %collective-permute-start.35 = (f32[1,8,4096]{2,1,0:T(8,128)S(1)}, f32[1,8,4096]{2,1,0:T(8,128)S(1)}, u32[]{:S(2)}, u32[]{:S(2)}) collective-permute-start(f32[1,8,4096]{2,1,0:T(8,128)S(1)} %collective-permute-done.31.refs_3_.rest_9_), channel_id=1, source_target_pairs={{0,112},{8,120},{16,0},{24,8},{32,16},{40,24},{48,32},{56,40},{64,... | collective-permute-start | bytes 393224 | tf_op jit(solution)/shard_map/ppermute | solution.py:423
  111.2 8.8 %collective-permute-start.38 = (f32[6,8,4096]{2,1,0:T(8,128)}, f32[6,8,4096]{2,1,0:T(8,128)}, u32[]{:S(2)}, u32[]{:S(2)}) collective-permute-start(f32[6,8,4096]{2,1,0:T(8,128)} %shard_map.144), channel_id=1, source_target_pairs={{0,8},{8,0},{16,24},{24,16},{32,40},{40,32},{48,56},{56,48},{64,72... | collective-permute-start | bytes 2359304 | tf_op jit(solution)/shard_map/ppermute | solution.py:431
  120.2 2.6 %collective-permute-start.37 = (f32[1,8,4096]{2,1,0:T(8,128)S(1)}, f32[1,8,4096]{2,1,0:T(8,128)S(1)}, u32[]{:S(2)}, u32[]{:S(2)}) collective-permute-start(f32[1,8,4096]{2,1,0:T(8,128)S(1)} %collective-permute-done.35.refs_3_.rest_13_), channel_id=1, source_target_pairs={{0,112},{8,120},{16,0},{24,8},{32,16},{40,24},{48,32},{56,40},{64,... | collective-permute-start | bytes 393224 | tf_op jit(solution)/shard_map/ppermute | solution.py:423
  122.8 3.4 %collective-permute-done.34.refs_2_.rest_12_ = f32[1,8,4096]{2,1,0:T(8,128)S(1)} collective-permute-done((f32[1,8,4096]{2,1,0:T(8,128)S(1)}, f32[1,8,4096]{2,1,0:T(8,128)S(1)}, u32[]{:S(2)}, u32[]{:S(2)}) %collective-permute-start.34) | collective-permute-done | bytes 131104 | tf_op jit(solution)/shard_map/ppermute | solution.py:423
  126.2 3.4 %collective-permute-start.1 = (f32[6,8,3072]{2,1,0:T(8,128)}, f32[6,8,3072]{2,1,0:T(8,128)}, u32[]{:S(2)}, u32[]{:S(2)}) collective-permute-start(f32[6,8,3072]{2,1,0:T(8,128)} %copy-done.39), channel_id=1, source_target_pairs={{1,0},{2,1},{3,2},{4,3},{5,4},{6,5},{7,6},{0,7},{9,8},{10,9},{11,1... | collective-permute-start | bytes 1769480 | tf_op jit(solution)/shard_map/ppermute | solution.py:383
  131.3 1.7 %collective-permute-start.39 = (f32[4,8,4096]{2,1,0:T(8,128)}, f32[4,8,4096]{2,1,0:T(8,128)}, u32[]{:S(2)}, u32[]{:S(2)}) collective-permute-start(f32[4,8,4096]{2,1,0:T(8,128)} %shard_map.145), channel_id=1, source_target_pairs={{0,8},{8,0},{16,24},{24,16},{32,40},{40,32},{48,56},{56,48},{64,72... | collective-permute-start | bytes 1572872 | tf_op jit(solution)/shard_map/ppermute | solution.py:431
  138.3 5.7 %shard_map.124.rest_0_ = f32[16,8,4096]{2,1,0:T(8,128)} custom-call(f32[16,8,4096]{2,1,0:T(8,128)S(1)} %copy-done.1, f32[10,8,3072]{2,1,0:T(8,128)S(1)} %collective-permute-done.2.low, f32[10,8,3072]{2,1,0:T(8,128)} %collective-permute-done.3.high, f32[16,8,4096]{2,1,0:T(8,128)S(1)} %copy-done.3, f32[8,4096]{1,0:T(8,128)S(1)} %copy-done.4, ...), custom_call_target="tpu_custom_call" | custom-call | flops 524288000 | bytes 6225920 | tf_op jit(solution)/shard_map/pallas_call | solution.py:159
  144.1 4.4 %shard_map.125 = f32[16,8,4096]{2,1,0:T(8,128)} custom-call(f32[16,8,4096]{2,1,0:T(8,128)S(1)} %copy-done.1, f32[6,8,3072]{2,1,0:T(8,128)} %collective-permute-done.low, f32[6,8,3072]{2,1,0:T(8,128)} %collective-permute-done.1.high, f32[16,8,4096]{2,1,0:T(8,128)S(1)} %copy-done.3, f32[8,4096]{1,0:T(8,128)S(1)} %copy-done.4, ...), custom_call_target="tpu_custom_call", output_to_operand_aliasing={{}: (6, {})} | custom-call | flops 314572800 | bytes 3735552 | tf_op jit(solution)/shard_map/pallas_call | solution.py:159
  148.7 4.6 %shard_map.149 = f32[16,8,4096]{2,1,0:T(8,128)} custom-call(f32[16,8,4096]{2,1,0:T(8,128)S(1)} %copy-done.5, f32[1,8,4096]{2,1,0:T(8,128)S(1)} %shard_map.141.refs_0_.rest_0_, f32[1,8,4096]{2,1,0:T(8,128)S(1)} %shard_map.143.refs_1_.rest_1_, f32[1,8,4096]{2,1,0:T(8,128)S(1)} %copy-done.10, f32[1,8,4096]{2,1,0:T(8,128)S(1)} %copy-done.8, ...), custom_call_target="tpu_custom_call" | custom-call | flops 805306368 | bytes 8388608 | tf_op jit(solution)/shard_map/pallas_call | solution.py:244
  (164 shorter events, 31.5 us)
Async XLA Ops:
  1.6 9.7 %collective-permute-start.4 = (f32[1,8,4096]{2,1,0:T(8,128)S(1)}, f32[1,8,4096]{2,1,0:T(8,128)S(1)}, u32[]{:S(2)}, u32[]{:S(2)}) collective-permute-start(f32[1,8,4096]{2,1,0:T(8,128)S(1)} %get-tuple-element.23), channel_id=1, source_target_pairs={{0,16},{8,24},{16,32},{24,40},{32,48},{40,56},{48,64},{56,72},{64,... | collective-permute-start | bytes 393224 | tf_op jit(solution)/shard_map/ppermute | solution.py:370
  5.2 11.8 %collective-permute-start.14 = (f32[1,8,4096]{2,1,0:T(8,128)S(1)}, f32[1,8,4096]{2,1,0:T(8,128)S(1)}, u32[]{:S(2)}, u32[]{:S(2)}) collective-permute-start(f32[1,8,4096]{2,1,0:T(8,128)S(1)} %get-tuple-element.21), channel_id=1, source_target_pairs={{0,16},{8,24},{16,32},{24,40},{32,48},{40,56},{48,64},{56,72},{64,... | collective-permute-start | bytes 393224 | tf_op jit(solution)/shard_map/ppermute | solution.py:370
  6.9 9.4 %collective-permute-start.8 = (f32[1,8,4096]{2,1,0:T(8,128)S(1)}, f32[1,8,4096]{2,1,0:T(8,128)S(1)}, u32[]{:S(2)}, u32[]{:S(2)}) collective-permute-start(f32[1,8,4096]{2,1,0:T(8,128)S(1)} %get-tuple-element.22), channel_id=1, source_target_pairs={{0,112},{8,120},{16,0},{24,8},{32,16},{40,24},{48,32},{56,40},{64,... | collective-permute-start | bytes 393224 | tf_op jit(solution)/shard_map/ppermute | solution.py:371
  13.5 8.4 %collective-permute-start.5 = (f32[2,8,4096]{2,1,0:T(8,128)S(1)}, f32[2,8,4096]{2,1,0:T(8,128)S(1)}, u32[]{:S(2)}, u32[]{:S(2)}) collective-permute-start(f32[2,8,4096]{2,1,0:T(8,128)S(1)} %shard_map.126), channel_id=1, source_target_pairs={{0,16},{8,24},{16,32},{24,40},{32,48},{40,56},{48,64},{56,72},{64,... | collective-permute-start | bytes 786440 | tf_op jit(solution)/shard_map/ppermute | solution.py:375
  16.8 10.9 %collective-permute-start.9 = (f32[2,8,4096]{2,1,0:T(8,128)S(1)}, f32[2,8,4096]{2,1,0:T(8,128)S(1)}, u32[]{:S(2)}, u32[]{:S(2)}) collective-permute-start(f32[2,8,4096]{2,1,0:T(8,128)S(1)} %shard_map.129), channel_id=1, source_target_pairs={{0,112},{8,120},{16,0},{24,8},{32,16},{40,24},{48,32},{56,40},{64,... | collective-permute-start | bytes 786440 | tf_op jit(solution)/shard_map/ppermute | solution.py:376
  17.5 13.5 %collective-permute-start.15 = (f32[2,8,4096]{2,1,0:T(8,128)S(1)}, f32[2,8,4096]{2,1,0:T(8,128)S(1)}, u32[]{:S(2)}, u32[]{:S(2)}) collective-permute-start(f32[2,8,4096]{2,1,0:T(8,128)S(1)} %shard_map.133), channel_id=1, source_target_pairs={{0,16},{8,24},{16,32},{24,40},{32,48},{40,56},{48,64},{56,72},{64,... | collective-permute-start | bytes 786440 | tf_op jit(solution)/shard_map/ppermute | solution.py:375
  19.6 12.0 %collective-permute-start.19 = (f32[2,8,4096]{2,1,0:T(8,128)S(1)}, f32[2,8,4096]{2,1,0:T(8,128)S(1)}, u32[]{:S(2)}, u32[]{:S(2)}) collective-permute-start(f32[2,8,4096]{2,1,0:T(8,128)S(1)} %shard_map.136), channel_id=1, source_target_pairs={{0,112},{8,120},{16,0},{24,8},{32,16},{40,24},{48,32},{56,40},{64,... | collective-permute-start | bytes 786440 | tf_op jit(solution)/shard_map/ppermute | solution.py:376
  22.5 12.5 %collective-permute-start.6 = (f32[2,8,4096]{2,1,0:T(8,128)S(1)}, f32[2,8,4096]{2,1,0:T(8,128)S(1)}, u32[]{:S(2)}, u32[]{:S(2)}) collective-permute-start(f32[2,8,4096]{2,1,0:T(8,128)S(1)} %shard_map.127), channel_id=1, source_target_pairs={{0,16},{8,24},{16,32},{24,40},{32,48},{40,56},{48,64},{56,72},{64,... | collective-permute-start | bytes 786440 | tf_op jit(solution)/shard_map/ppermute | solution.py:375
  24.9 73.5 %collective-permute-start.2 = (f32[10,8,3072]{2,1,0:T(8,128)}, f32[10,8,3072]{2,1,0:T(8,128)S(1)}, u32[]{:S(2)}, u32[]{:S(2)}) collective-permute-start(f32[10,8,3072]{2,1,0:T(8,128)} %get-tuple-element.13), channel_id=1, source_target_pairs={{0,1},{1,2},{2,3},{3,4},{4,5},{5,6},{6,7},{7,0},{8,9},{9,10},{10,1... | collective-permute-start | bytes 2949128 | tf_op jit(solution)/shard_map/ppermute | solution.py:382
  28.2 7.4 %collective-permute-start.10 = (f32[2,8,4096]{2,1,0:T(8,128)S(1)}, f32[2,8,4096]{2,1,0:T(8,128)S(1)}, u32[]{:S(2)}, u32[]{:S(2)}) collective-permute-start(f32[2,8,4096]{2,1,0:T(8,128)S(1)} %shard_map.130), channel_id=1, source_target_pairs={{0,112},{8,120},{16,0},{24,8},{32,16},{40,24},{48,32},{56,40},{64,... | collective-permute-start | bytes 786440 | tf_op jit(solution)/shard_map/ppermute | solution.py:376
  31.5 7.4 %collective-permute-start.16 = (f32[2,8,4096]{2,1,0:T(8,128)S(1)}, f32[2,8,4096]{2,1,0:T(8,128)S(1)}, u32[]{:S(2)}, u32[]{:S(2)}) collective-permute-start(f32[2,8,4096]{2,1,0:T(8,128)S(1)} %shard_map.134), channel_id=1, source_target_pairs={{0,16},{8,24},{16,32},{24,40},{32,48},{40,56},{48,64},{56,72},{64,... | collective-permute-start | bytes 786440 | tf_op jit(solution)/shard_map/ppermute | solution.py:375
  32.2 9.0 %collective-permute-start.20 = (f32[2,8,4096]{2,1,0:T(8,128)S(1)}, f32[2,8,4096]{2,1,0:T(8,128)S(1)}, u32[]{:S(2)}, u32[]{:S(2)}) collective-permute-start(f32[2,8,4096]{2,1,0:T(8,128)S(1)} %shard_map.137), channel_id=1, source_target_pairs={{0,112},{8,120},{16,0},{24,8},{32,16},{40,24},{48,32},{56,40},{64,... | collective-permute-start | bytes 786440 | tf_op jit(solution)/shard_map/ppermute | solution.py:376
  35.5 7.7 %collective-permute-start.7 = (f32[2,8,4096]{2,1,0:T(8,128)S(1)}, f32[2,8,4096]{2,1,0:T(8,128)S(1)}, u32[]{:S(2)}, u32[]{:S(2)}) collective-permute-start(f32[2,8,4096]{2,1,0:T(8,128)S(1)} %shard_map.128), channel_id=1, source_target_pairs={{0,16},{8,24},{16,32},{24,40},{32,48},{40,56},{48,64},{56,72},{64,... | collective-permute-start | bytes 786440 | tf_op jit(solution)/shard_map/ppermute | solution.py:375
  36.2 9.7 %collective-permute-start.11 = (f32[2,8,4096]{2,1,0:T(8,128)S(1)}, f32[2,8,4096]{2,1,0:T(8,128)S(1)}, u32[]{:S(2)}, u32[]{:S(2)}) collective-permute-start(f32[2,8,4096]{2,1,0:T(8,128)S(1)} %shard_map.131), channel_id=1, source_target_pairs={{0,112},{8,120},{16,0},{24,8},{32,16},{40,24},{48,32},{56,40},{64,... | collective-permute-start | bytes 786440 | tf_op jit(solution)/shard_map/ppermute | solution.py:376
  39.5 9.8 %collective-permute-start.17 = (f32[2,8,4096]{2,1,0:T(8,128)S(1)}, f32[2,8,4096]{2,1,0:T(8,128)S(1)}, u32[]{:S(2)}, u32[]{:S(2)}) collective-permute-start(f32[2,8,4096]{2,1,0:T(8,128)S(1)} %shard_map.135), channel_id=1, source_target_pairs={{0,16},{8,24},{16,32},{24,40},{32,48},{40,56},{48,64},{56,72},{64,... | collective-permute-start | bytes 786440 | tf_op jit(solution)/shard_map/ppermute | solution.py:375
  41.2 54.5 %collective-permute-start = (f32[6,8,3072]{2,1,0:T(8,128)}, f32[6,8,3072]{2,1,0:T(8,128)}, u32[]{:S(2)}, u32[]{:S(2)}) collective-permute-start(f32[6,8,3072]{2,1,0:T(8,128)} %get-tuple-element.11), channel_id=1, source_target_pairs={{0,1},{1,2},{2,3},{3,4},{4,5},{5,6},{6,7},{7,0},{8,9},{9,10},{10,1... | collective-permute-start | bytes 1769480 | tf_op jit(solution)/shard_map/ppermute | solution.py:382
  43.2 10.0 %collective-permute-start.21 = (f32[2,8,4096]{2,1,0:T(8,128)S(1)}, f32[2,8,4096]{2,1,0:T(8,128)S(1)}, u32[]{:S(2)}, u32[]{:S(2)}) collective-permute-start(f32[2,8,4096]{2,1,0:T(8,128)S(1)} %shard_map.138), channel_id=1, source_target_pairs={{0,112},{8,120},{16,0},{24,8},{32,16},{40,24},{48,32},{56,40},{64,... | collective-permute-start | bytes 786440 | tf_op jit(solution)/shard_map/ppermute | solution.py:376
  46.6 18.1 %collective-permute-start.12 = (f32[2,8,3072]{2,1,0:T(8,128)S(1)}, f32[2,8,3072]{2,1,0:T(8,128)S(1)}, u32[]{:S(2)}, u32[]{:S(2)}) collective-permute-start(f32[2,8,3072]{2,1,0:T(8,128)S(1)} %get-tuple-element.16), channel_id=1, source_target_pairs={{0,1},{1,2},{2,3},{3,4},{4,5},{5,6},{6,7},{7,0},{8,9},{9,10},{10,1... | collective-permute-start | bytes 589832 | tf_op jit(solution)/shard_map/ppermute | solution.py:382
  49.3 18.5 %collective-permute-start.13 = (f32[2,8,3072]{2,1,0:T(8,128)S(1)}, f32[2,8,3072]{2,1,0:T(8,128)S(1)}, u32[]{:S(2)}, u32[]{:S(2)}) collective-permute-start(f32[2,8,3072]{2,1,0:T(8,128)S(1)} %get-tuple-element.17), channel_id=1, source_target_pairs={{1,0},{2,1},{3,2},{4,3},{5,4},{6,5},{7,6},{0,7},{9,8},{10,9},{11,1... | collective-permute-start | bytes 589832 | tf_op jit(solution)/shard_map/ppermute | solution.py:383
  69.1 65.4 %collective-permute-start.3 = (f32[10,8,3072]{2,1,0:T(8,128)}, f32[10,8,3072]{2,1,0:T(8,128)}, u32[]{:S(2)}, u32[]{:S(2)}) collective-permute-start(f32[10,8,3072]{2,1,0:T(8,128)} %get-tuple-element.14), channel_id=1, source_target_pairs={{1,0},{2,1},{3,2},{4,3},{5,4},{6,5},{7,6},{0,7},{9,8},{10,9},{11,1... | collective-permute-start | bytes 2949128 | tf_op jit(solution)/shard_map/ppermute | solution.py:383
  73.6 19.6 %collective-permute-start.23 = (f32[1,8,4096]{2,1,0:T(8,128)}, f32[1,8,4096]{2,1,0:T(8,128)S(1)}, u32[]{:S(2)}, u32[]{:S(2)}) collective-permute-start(f32[1,8,4096]{2,1,0:T(8,128)} %shard_map.142.mine), channel_id=1, source_target_pairs={{0,128},{8,136},{16,144},{24,152},{32,160},{40,168},{48,176},{56,1... | collective-permute-start | bytes 393224 | tf_op jit(solution)/shard_map/ppermute | solution.py:414
  74.6 23.9 %collective-permute-start.25 = (f32[1,8,4096]{2,1,0:T(8,128)S(1)}, f32[1,8,4096]{2,1,0:T(8,128)S(1)}, u32[]{:S(2)}, u32[]{:S(2)}) collective-permute-start(f32[1,8,4096]{2,1,0:T(8,128)S(1)} %shard_map.141.refs_0_.rest_0_), channel_id=1, source_target_pairs={{0,112},{8,120},{16,0},{24,8},{32,16},{40,24},{48,32},{56,40},{64,... | collective-permute-start | bytes 393224 | tf_op jit(solution)/shard_map/ppermute | solution.py:423
  103.8 16.1 %collective-permute-start.33 = (f32[1,8,4096]{2,1,0:T(8,128)S(1)}, f32[1,8,4096]{2,1,0:T(8,128)S(1)}, u32[]{:S(2)}, u32[]{:S(2)}) collective-permute-start(f32[1,8,4096]{2,1,0:T(8,128)S(1)} %collective-permute-done.29.refs_1_.rest_7_), channel_id=1, source_target_pairs={{0,112},{8,120},{16,0},{24,8},{32,16},{40,24},{48,32},{56,40},{64,... | collective-permute-start | bytes 393224 | tf_op jit(solution)/shard_map/ppermute | solution.py:423
  106.9 13.1 %collective-permute-start.32 = (f32[1,8,4096]{2,1,0:T(8,128)S(1)}, f32[1,8,4096]{2,1,0:T(8,128)S(1)}, u32[]{:S(2)}, u32[]{:S(2)}) collective-permute-start(f32[1,8,4096]{2,1,0:T(8,128)S(1)} %collective-permute-done.28.refs_0_.rest_6_), channel_id=1, source_target_pairs={{0,16},{8,24},{16,32},{24,40},{32,48},{40,56},{48,64},{56,72},{64,... | collective-permute-start | bytes 393224 | tf_op jit(solution)/shard_map/ppermute | solution.py:423
  106.9 13.2 %collective-permute-start.35 = (f32[1,8,4096]{2,1,0:T(8,128)S(1)}, f32[1,8,4096]{2,1,0:T(8,128)S(1)}, u32[]{:S(2)}, u32[]{:S(2)}) collective-permute-start(f32[1,8,4096]{2,1,0:T(8,128)S(1)} %collective-permute-done.31.refs_3_.rest_9_), channel_id=1, source_target_pairs={{0,112},{8,120},{16,0},{24,8},{32,16},{40,24},{48,32},{56,40},{64,... | collective-permute-start | bytes 393224 | tf_op jit(solution)/shard_map/ppermute | solution.py:423
  111.2 37.3 %collective-permute-start.38 = (f32[6,8,4096]{2,1,0:T(8,128)}, f32[6,8,4096]{2,1,0:T(8,128)}, u32[]{:S(2)}, u32[]{:S(2)}) collective-permute-start(f32[6,8,4096]{2,1,0:T(8,128)} %shard_map.144), channel_id=1, source_target_pairs={{0,8},{8,0},{16,24},{24,16},{32,40},{40,32},{48,56},{56,48},{64,72... | collective-permute-start | bytes 2359304 | tf_op jit(solution)/shard_map/ppermute | solution.py:431
  120.1 11.3 %collective-permute-start.36 = (f32[1,8,4096]{2,1,0:T(8,128)S(1)}, f32[1,8,4096]{2,1,0:T(8,128)S(1)}, u32[]{:S(2)}, u32[]{:S(2)}) collective-permute-start(f32[1,8,4096]{2,1,0:T(8,128)S(1)} %collective-permute-done.32.refs_0_.rest_10_), channel_id=1, source_target_pairs={{0,16},{8,24},{16,32},{24,40},{32,48},{40,56},{48,64},{56,72},{64,... | collective-permute-start | bytes 393224 | tf_op jit(solution)/shard_map/ppermute | solution.py:423
  120.2 12.8 %collective-permute-start.37 = (f32[1,8,4096]{2,1,0:T(8,128)S(1)}, f32[1,8,4096]{2,1,0:T(8,128)S(1)}, u32[]{:S(2)}, u32[]{:S(2)}) collective-permute-start(f32[1,8,4096]{2,1,0:T(8,128)S(1)} %collective-permute-done.35.refs_3_.rest_13_), channel_id=1, source_target_pairs={{0,112},{8,120},{16,0},{24,8},{32,16},{40,24},{48,32},{56,40},{64,... | collective-permute-start | bytes 393224 | tf_op jit(solution)/shard_map/ppermute | solution.py:423
  126.2 17.9 %collective-permute-start.1 = (f32[6,8,3072]{2,1,0:T(8,128)}, f32[6,8,3072]{2,1,0:T(8,128)}, u32[]{:S(2)}, u32[]{:S(2)}) collective-permute-start(f32[6,8,3072]{2,1,0:T(8,128)} %copy-done.39), channel_id=1, source_target_pairs={{1,0},{2,1},{3,2},{4,3},{5,4},{6,5},{7,6},{0,7},{9,8},{10,9},{11,1... | collective-permute-start | bytes 1769480 | tf_op jit(solution)/shard_map/ppermute | solution.py:383
  131.3 17.2 %collective-permute-start.39 = (f32[4,8,4096]{2,1,0:T(8,128)}, f32[4,8,4096]{2,1,0:T(8,128)}, u32[]{:S(2)}, u32[]{:S(2)}) collective-permute-start(f32[4,8,4096]{2,1,0:T(8,128)} %shard_map.145), channel_id=1, source_target_pairs={{0,8},{8,0},{16,24},{24,16},{32,40},{40,32},{48,56},{56,48},{64,72... | collective-permute-start | bytes 1572872 | tf_op jit(solution)/shard_map/ppermute | solution.py:431
  133.0 15.5 %collective-permute-start.40 = (f32[4,8,4096]{2,1,0:T(8,128)}, f32[4,8,4096]{2,1,0:T(8,128)}, u32[]{:S(2)}, u32[]{:S(2)}) collective-permute-start(f32[4,8,4096]{2,1,0:T(8,128)} %shard_map.146), channel_id=1, source_target_pairs={{0,8},{8,0},{16,24},{24,16},{32,40},{40,32},{48,56},{56,48},{64,72... | collective-permute-start | bytes 1572872 | tf_op jit(solution)/shard_map/ppermute | solution.py:431
  134.6 13.9 %collective-permute-start.41 = (f32[2,8,4096]{2,1,0:T(8,128)}, f32[2,8,4096]{2,1,0:T(8,128)}, u32[]{:S(2)}, u32[]{:S(2)}) collective-permute-start(f32[2,8,4096]{2,1,0:T(8,128)} %shard_map.147), channel_id=1, source_target_pairs={{0,8},{8,0},{16,24},{24,16},{32,40},{40,32},{48,56},{56,48},{64,72... | collective-permute-start | bytes 786440 | tf_op jit(solution)/shard_map/ppermute | solution.py:431
  (50 other events, 424.3 us)

commit v3 on v2

--- a/solution.py
+++ b/solution.py
@@ -27,6 +27,10 @@
 CORES = 2
 
 
+def split(*counts):
+    return max(d for d in range(1, 6) if math.gcd(*counts) % d == 0)
+
+
 def room(mib):
     return pltpu.CompilerParams(vmem_limit_bytes=mib << 20)
 
@@ -71,7 +75,7 @@
     n = n or orb.shape[0]
     planes, cells = orb.shape[1:]
     thin = cells * WIDTH // planes
-    step = math.gcd(4, n, first)
+    step = split(n, first)
     return pl.pallas_call(
         pack_body,
         grid=(n // step,),
@@ -81,6 +85,18 @@
         compiler_params=room(8),
         cost_estimate=pl.CostEstimate(flops=0, bytes_accessed=10 * n * planes * cells, transcendentals=0),
     )(orb)
+
+
+def halves(values):
+    high = values.astype(jnp.bfloat16)
+    return high, (values - high.astype(jnp.float32)).astype(jnp.bfloat16)
+
+
+def three_pass(left, right):
+    left_high, left_low = halves(left)
+    right_high, right_low = halves(right)
+    dot = lambda a, b: jnp.dot(a, b, preferred_element_type=jnp.float32)
+    return dot(left_high, right_high) + (dot(left_high, right_low) + dot(left_low, right_high))
 
 
 def filter_one(i, orb, low, high, prev, pot, mat, out, ext, half, rowsum):
@@ -105,7 +121,7 @@
         rolled = now
     half[(tiles - 1) * planes : tiles * planes, :] = jnp.where(lane < ROW, rolled, first)
     cells = jnp.concatenate([orb[i, :, t * LANES : (t + 1) * LANES] for t in range(tiles)], axis=0)
-    rowsum[...] = jnp.dot(cells, mat[...], precision=lax.Precision.HIGHEST, preferred_element_type=jnp.float32)
+    rowsum[...] = three_pass(cells, mat[...])
     for t in range(tiles):
         base = span * t + planes
         centre = orb[i, :, t * LANES : (t + 1) * LANES]
@@ -142,7 +158,7 @@
     total = total or orb.shape[0]
     tiles = cells // LANES
     thin = cells * WIDTH // planes
-    step = math.gcd(4, n, first, side, out)
+    step = split(n, first, side, out)
     block = lambda start, width: pl.BlockSpec((step, planes, width), lambda i: (i + start // step, 0, 0))
     args = [orb, low, high, prev, pot, jnp.asarray(row_matrix())]
     specs = [
@@ -270,30 +286,29 @@
 PARTNER = everywhere(lambda x, z, c: (x, z, 1 - c))
 
 
-def pick_body(place, hand, moved, out):
-    for m in range(out.shape[0]):
-        out[m] = jnp.where(place[1] == 0, hand[m], moved[min(m, moved.shape[0] - 1)])
-
-
-def pick(block, place, step, moved):
+def pick_body(place, hand_up, hand_down, up, down, out_up, out_down):
+    for hand, moved, out in ((hand_up, up, out_up), (hand_down, down, out_down)):
+        for m in range(out.shape[0]):
+            out[m] = jnp.where(place[1] == 0, hand[m], moved[min(m, moved.shape[0] - 1)])
+
+
+def pick(block, place, step, up, down):
     n, planes, cells = block.shape
     share = n // RING
-    hand = lambda index: pl.BlockSpec((share, planes, cells), index)
+    hand = lambda step: pl.BlockSpec((share, planes, cells), lambda i, s: ((s[0] + step) & (RING - 1), 0, 0))
+    still = pl.BlockSpec(memory_space=pltpu.VMEM)
     return pl.pallas_call(
         pick_body,
         grid_spec=pltpu.PrefetchScalarGridSpec(
             num_scalar_prefetch=1,
             grid=(1,),
-            in_specs=[
-                hand(lambda i, s: ((s[0] + step) & (RING - 1), 0, 0)),
-                pl.BlockSpec(memory_space=pltpu.VMEM),
-            ],
-            out_specs=pl.BlockSpec(memory_space=pltpu.VMEM),
+            in_specs=[hand(step), hand(RING - step), still, still],
+            out_specs=[still, still],
         ),
-        out_shape=jax.ShapeDtypeStruct((share, planes, cells), jnp.float32),
-        compiler_params=room(3),
-        cost_estimate=pl.CostEstimate(flops=0, bytes_accessed=12 * share * planes * cells, transcendentals=0),
-    )(place, block, moved)
+        out_shape=[jax.ShapeDtypeStruct((share, planes, cells), jnp.float32)] * 2,
+        compiler_params=room(5),
+        cost_estimate=pl.CostEstimate(flops=0, bytes_accessed=24 * share * planes * cells, transcendentals=0),
+    )(place, block, block, up, down)
 
 
 def settle_body(place, own, up, down, piece, *ends):
@@ -370,8 +385,7 @@
     up = lax.ppermute(lax.dynamic_slice(block, (start, 0, 0), size), "band", ONWARD)
     down = lax.ppermute(lax.dynamic_slice(block, (start + half, 0, 0), size), "band", BACK)
     for step in (3, 2, 1):
-        up = pick(block, place, step, up)
-        down = pick(block, place, RING - step, down)
+        up, down = pick(block, place, step, up, down)
         up = lax.ppermute(up, "band", ONWARD)
         down = lax.ppermute(down, "band", BACK)
     return settle(block, place, up, down, packed)

time: 154 us -> 155 us (level)
  starting transfers between devices: 72.6 us -> 79.3 us
  Pallas kernels: 34.4 us -> 29 us
    ppermute x2, starting transfers between devices: 4.25 us -> 0.01 us  [relay(): lax.ppermute(lax.dynamic_slice(block, (start, 0, 0), size), 'band', ONWARD)]
    ppermute x2, starting transfers between devices: 5.07 us -> 9.22 us  [relay(): lax.ppermute(lax.dynamic_slice(block, (start + half, 0, 0), size), 'band'...]
    ppermute x3, starting transfers between devices: 10.7 us -> 14.3 us  [halo(): lax.ppermute(head, 'domain', [((i + 1) % size, i) for i in range(size)])]
    ppermute x6, waiting for transfers between devices: 0.08 us -> 3.41 us  [relay(): up = lax.ppermute(up, 'band', ONWARD)]
    pallas_call x12 -> x6, Pallas kernels: 6.81 us -> 3.59 us  [pick(): pl.pallas_call(pick_body, grid_spec=pltpu.PrefetchScalarGridSpec(num_scal...]
    ppermute x6, starting transfers between devices: 13.3 us -> 16.1 us  [relay(): down = lax.ppermute(down, 'band', BACK)]
    ppermute x3, waiting for transfers between devices: 11 us -> 9.08 us  [halo(): lax.ppermute(tail, 'domain', [(i, (i + 1) % size) for i in range(size)])]
  transfers between devices with their start and end apart: 42 -> 42, of which waited for: 7 -> 12; matrix products, arithmetic and copies ran while one was open for 1% -> 1% of each run, Pallas kernels for 19% -> 16%
where the time goes in v3:
time: 155 us
  starting transfers between devices  79.3 us (51%)
  waiting for transfers between devices  35.7 us (23%)
  Pallas kernels  29 us (19%)
  local copies, waits for them, and re-layouts  8.89 us (6%)
  between operations  1.86 us (1%)
    ppermute x14, starting transfers between devices, step(): chain[way] = lax.ppermute(chain[way], 'band', pairs)  19.4 us
    ppermute x6, starting transfers between devices, relay(): down = lax.ppermute(down, 'band', BACK)  16.1 us
    ppermute x2, waiting for transfers between devices, step(): other = lax.ppermute(mine, 'band', ACROSS)  15.5 us
    ppermute x3, starting transfers between devices, halo(): lax.ppermute(head, 'domain', [((i + 1) % size, i) for i in range(size)])  14.3 us
    ppermute x4, starting transfers between devices, step(): theirs.append(lax.ppermute(group, 'band', PARTNER))  11.1 us
    pallas_call x4, Pallas kernels, apply_filter(): pl.pallas_call(filter_body, grid=(n // step,), in_specs=specs, out_specs=...  10.7 us
    ppermute x2, starting transfers between devices, relay(): lax.ppermute(lax.dynamic_slice(block, (start + half, 0, 0), size), 'band'...  9.22 us
    ppermute x3, waiting for transfers between devices, halo(): lax.ppermute(tail, 'domain', [(i, (i + 1) % size) for i in range(size)])  9.08 us
  transfers between devices with their start and end apart: 42, of which 12 were waited for; matrix products, arithmetic and copies ran while one was open for 1% of the time, Pallas kernels for 16%

profile of v3, /device:TPU:1, one launch (start us, length us, event | category | flops | bytes accessed | tf_op | source)
XLA Modules:
  0.0 154.9 jit_solution(5703489474665854159)
XLA Ops:
  1.6 6.5 %collective-permute-start.5 = (f32[1,8,4096]{2,1,0:T(8,128)S(1)}, f32[1,8,4096]{2,1,0:T(8,128)S(1)}, u32[]{:S(2)}, u32[]{:S(2)}) collective-permute-start(f32[1,8,4096]{2,1,0:T(8,128)S(1)} %get-tuple-element.46), channel_id=1, source_target_pairs={{0,112},{8,120},{16,0},{24,8},{32,16},{40,24},{48,32},{56,40},{64,... | collective-permute-start | bytes 393224 | tf_op jit(solution)/shard_map/ppermute | solution.py:386
  9.1 2.7 %collective-permute-start.15 = (f32[1,8,4096]{2,1,0:T(8,128)S(1)}, f32[1,8,4096]{2,1,0:T(8,128)S(1)}, u32[]{:S(2)}, u32[]{:S(2)}) collective-permute-start(f32[1,8,4096]{2,1,0:T(8,128)S(1)} %get-tuple-element.44), channel_id=1, source_target_pairs={{0,112},{8,120},{16,0},{24,8},{32,16},{40,24},{48,32},{56,40},{64,... | collective-permute-start | bytes 393224 | tf_op jit(solution)/shard_map/ppermute | solution.py:386
  13.1 1.6 %copy-done = f32[16,8,4096]{2,1,0:T(8,128)S(1)} copy-done((f32[16,8,4096]{2,1,0:T(8,128)S(1)}, f32[16,8,4096]{2,1,0:T(8,128)}, u32[]{:S(2)}) %copy-start) | copy-done | bytes 2097176
  15.4 2.7 %collective-permute-start.7 = (f32[2,8,4096]{2,1,0:T(8,128)S(1)}, f32[2,8,4096]{2,1,0:T(8,128)S(1)}, u32[]{:S(2)}, u32[]{:S(2)}) collective-permute-start(f32[2,8,4096]{2,1,0:T(8,128)S(1)} %get-tuple-element.28), channel_id=1, source_target_pairs={{0,112},{8,120},{16,0},{24,8},{32,16},{40,24},{48,32},{56,40},{64,... | collective-permute-start | bytes 786440 | tf_op jit(solution)/shard_map/ppermute | solution.py:390
  18.8 2.7 %collective-permute-start.17 = (f32[2,8,4096]{2,1,0:T(8,128)S(1)}, f32[2,8,4096]{2,1,0:T(8,128)S(1)}, u32[]{:S(2)}, u32[]{:S(2)}) collective-permute-start(f32[2,8,4096]{2,1,0:T(8,128)S(1)} %get-tuple-element.37), channel_id=1, source_target_pairs={{0,112},{8,120},{16,0},{24,8},{32,16},{40,24},{48,32},{56,40},{64,... | collective-permute-start | bytes 786440 | tf_op jit(solution)/shard_map/ppermute | solution.py:390
  23.1 2.7 %collective-permute-start.9 = (f32[2,8,4096]{2,1,0:T(8,128)S(1)}, f32[2,8,4096]{2,1,0:T(8,128)S(1)}, u32[]{:S(2)}, u32[]{:S(2)}) collective-permute-start(f32[2,8,4096]{2,1,0:T(8,128)S(1)} %get-tuple-element.30), channel_id=1, source_target_pairs={{0,112},{8,120},{16,0},{24,8},{32,16},{40,24},{48,32},{56,40},{64,... | collective-permute-start | bytes 786440 | tf_op jit(solution)/shard_map/ppermute | solution.py:390
  27.1 2.7 %collective-permute-start.2 = (f32[10,8,3072]{2,1,0:T(8,128)}, f32[10,8,3072]{2,1,0:T(8,128)S(1)}, u32[]{:S(2)}, u32[]{:S(2)}) collective-permute-start(f32[10,8,3072]{2,1,0:T(8,128)} %get-tuple-element.25), channel_id=1, source_target_pairs={{0,1},{1,2},{2,3},{3,4},{4,5},{5,6},{6,7},{7,0},{8,9},{9,10},{10,1... | collective-permute-start | bytes 2949128 | tf_op jit(solution)/shard_map/ppermute | solution.py:396
  30.5 2.7 %collective-permute-start.19 = (f32[2,8,4096]{2,1,0:T(8,128)S(1)}, f32[2,8,4096]{2,1,0:T(8,128)S(1)}, u32[]{:S(2)}, u32[]{:S(2)}) collective-permute-start(f32[2,8,4096]{2,1,0:T(8,128)S(1)} %get-tuple-element.39), channel_id=1, source_target_pairs={{0,112},{8,120},{16,0},{24,8},{32,16},{40,24},{48,32},{56,40},{64,... | collective-permute-start | bytes 786440 | tf_op jit(solution)/shard_map/ppermute | solution.py:390
  34.6 2.7 %collective-permute-start.11 = (f32[2,8,4096]{2,1,0:T(8,128)S(1)}, f32[2,8,4096]{2,1,0:T(8,128)S(1)}, u32[]{:S(2)}, u32[]{:S(2)}) collective-permute-start(f32[2,8,4096]{2,1,0:T(8,128)S(1)} %get-tuple-element.32), channel_id=1, source_target_pairs={{0,112},{8,120},{16,0},{24,8},{32,16},{40,24},{48,32},{56,40},{64,... | collective-permute-start | bytes 786440 | tf_op jit(solution)/shard_map/ppermute | solution.py:390
  41.0 2.9 %collective-permute-start = (f32[6,8,3072]{2,1,0:T(8,128)}, f32[6,8,3072]{2,1,0:T(8,128)}, u32[]{:S(2)}, u32[]{:S(2)}) collective-permute-start(f32[6,8,3072]{2,1,0:T(8,128)} %get-tuple-element.23), channel_id=1, source_target_pairs={{0,1},{1,2},{2,3},{3,4},{4,5},{5,6},{6,7},{7,0},{8,9},{9,10},{10,1... | collective-permute-start | bytes 1769480 | tf_op jit(solution)/shard_map/ppermute | solution.py:396
  43.9 2.7 %collective-permute-start.21 = (f32[2,8,4096]{2,1,0:T(8,128)S(1)}, f32[2,8,4096]{2,1,0:T(8,128)S(1)}, u32[]{:S(2)}, u32[]{:S(2)}) collective-permute-start(f32[2,8,4096]{2,1,0:T(8,128)S(1)} %get-tuple-element.41), channel_id=1, source_target_pairs={{0,112},{8,120},{16,0},{24,8},{32,16},{40,24},{48,32},{56,40},{64,... | collective-permute-start | bytes 786440 | tf_op jit(solution)/shard_map/ppermute | solution.py:390
  47.3 1.8 %collective-permute-start.12 = (f32[2,8,3072]{2,1,0:T(8,128)S(1)}, f32[2,8,3072]{2,1,0:T(8,128)S(1)}, u32[]{:S(2)}, u32[]{:S(2)}) collective-permute-start(f32[2,8,3072]{2,1,0:T(8,128)S(1)} %get-tuple-element.34), channel_id=1, source_target_pairs={{0,1},{1,2},{2,3},{3,4},{4,5},{5,6},{6,7},{7,0},{8,9},{9,10},{10,1... | collective-permute-start | bytes 589832 | tf_op jit(solution)/shard_map/ppermute | solution.py:396
  49.4 6.5 %collective-permute-start.13 = (f32[2,8,3072]{2,1,0:T(8,128)S(1)}, f32[2,8,3072]{2,1,0:T(8,128)S(1)}, u32[]{:S(2)}, u32[]{:S(2)}) collective-permute-start(f32[2,8,3072]{2,1,0:T(8,128)S(1)} %get-tuple-element.35), channel_id=1, source_target_pairs={{1,0},{2,1},{3,2},{4,3},{5,4},{6,5},{7,6},{0,7},{9,8},{10,9},{11,1... | collective-permute-start | bytes 589832 | tf_op jit(solution)/shard_map/ppermute | solution.py:397
  56.5 9.1 %collective-permute-done.12.low = f32[2,8,3072]{2,1,0:T(8,128)S(1)} collective-permute-done((f32[2,8,3072]{2,1,0:T(8,128)S(1)}, f32[2,8,3072]{2,1,0:T(8,128)S(1)}, u32[]{:S(2)}, u32[]{:S(2)}) %collective-permute-start.12) | collective-permute-done | bytes 196640 | tf_op jit(solution)/shard_map/ppermute | solution.py:396
  65.6 2.9 %collective-permute-done.13.high = f32[2,8,3072]{2,1,0:T(8,128)S(1)} collective-permute-done((f32[2,8,3072]{2,1,0:T(8,128)S(1)}, f32[2,8,3072]{2,1,0:T(8,128)S(1)}, u32[]{:S(2)}, u32[]{:S(2)}) %collective-permute-start.13) | collective-permute-done | bytes 196640 | tf_op jit(solution)/shard_map/ppermute | solution.py:397
  70.7 3.1 %collective-permute-start.3 = (f32[10,8,3072]{2,1,0:T(8,128)}, f32[10,8,3072]{2,1,0:T(8,128)}, u32[]{:S(2)}, u32[]{:S(2)}) collective-permute-start(f32[10,8,3072]{2,1,0:T(8,128)} %get-tuple-element.26), channel_id=1, source_target_pairs={{1,0},{2,1},{3,2},{4,3},{5,4},{6,5},{7,6},{0,7},{9,8},{10,9},{11,1... | collective-permute-start | bytes 2949128 | tf_op jit(solution)/shard_map/ppermute | solution.py:397
  76.1 1.8 %collective-permute-start.25 = (f32[1,8,4096]{2,1,0:T(8,128)S(1)}, f32[1,8,4096]{2,1,0:T(8,128)S(1)}, u32[]{:S(2)}, u32[]{:S(2)}) collective-permute-start(f32[1,8,4096]{2,1,0:T(8,128)S(1)} %shard_map.135.refs_0_.rest_0_), channel_id=1, source_target_pairs={{0,112},{8,120},{16,0},{24,8},{32,16},{40,24},{48,32},{56,40},{64,... | collective-permute-start | bytes 393224 | tf_op jit(solution)/shard_map/ppermute | solution.py:437
  77.9 15.1 %collective-permute-done.23.other = f32[1,8,4096]{2,1,0:T(8,128)S(1)} collective-permute-done((f32[1,8,4096]{2,1,0:T(8,128)}, f32[1,8,4096]{2,1,0:T(8,128)S(1)}, u32[]{:S(2)}, u32[]{:S(2)}) %collective-permute-start.23) | collective-permute-done | bytes 131104 | tf_op jit(solution)/shard_map/ppermute | solution.py:428
  93.7 3.3 %collective-permute-start.24 = (f32[1,8,4096]{2,1,0:T(8,128)S(1)}, f32[1,8,4096]{2,1,0:T(8,128)S(1)}, u32[]{:S(2)}, u32[]{:S(2)}) collective-permute-start(f32[1,8,4096]{2,1,0:T(8,128)S(1)} %shard_map.135.refs_0_.rest_0_), channel_id=1, source_target_pairs={{0,16},{8,24},{16,32},{24,40},{32,48},{40,56},{48,64},{56,72},{64,... | collective-permute-start | bytes 393224 | tf_op jit(solution)/shard_map/ppermute | solution.py:437
  100.7 1.9 %collective-permute-start.29 = (f32[1,8,4096]{2,1,0:T(8,128)S(1)}, f32[1,8,4096]{2,1,0:T(8,128)S(1)}, u32[]{:S(2)}, u32[]{:S(2)}) collective-permute-start(f32[1,8,4096]{2,1,0:T(8,128)S(1)} %collective-permute-done.25.refs_3_.rest_3_), channel_id=1, source_target_pairs={{0,112},{8,120},{16,0},{24,8},{32,16},{40,24},{48,32},{56,40},{64,... | collective-permute-start | bytes 393224 | tf_op jit(solution)/shard_map/ppermute | solution.py:437
  102.9 2.4 %collective-permute-start.31 = (f32[1,8,4096]{2,1,0:T(8,128)S(1)}, f32[1,8,4096]{2,1,0:T(8,128)S(1)}, u32[]{:S(2)}, u32[]{:S(2)}) collective-permute-start(f32[1,8,4096]{2,1,0:T(8,128)S(1)} %collective-permute-done.27.refs_5_.rest_5_), channel_id=1, source_target_pairs={{0,112},{8,120},{16,0},{24,8},{32,16},{40,24},{48,32},{56,40},{64,... | collective-permute-start | bytes 393224 | tf_op jit(solution)/shard_map/ppermute | solution.py:437
  105.3 2.7 %collective-permute-start.33 = (f32[1,8,4096]{2,1,0:T(8,128)S(1)}, f32[1,8,4096]{2,1,0:T(8,128)S(1)}, u32[]{:S(2)}, u32[]{:S(2)}) collective-permute-start(f32[1,8,4096]{2,1,0:T(8,128)S(1)} %collective-permute-done.29.refs_1_.rest_7_), channel_id=1, source_target_pairs={{0,112},{8,120},{16,0},{24,8},{32,16},{40,24},{48,32},{56,40},{64,... | collective-permute-start | bytes 393224 | tf_op jit(solution)/shard_map/ppermute | solution.py:437
  108.4 2.7 %collective-permute-start.35 = (f32[1,8,4096]{2,1,0:T(8,128)S(1)}, f32[1,8,4096]{2,1,0:T(8,128)S(1)}, u32[]{:S(2)}, u32[]{:S(2)}) collective-permute-start(f32[1,8,4096]{2,1,0:T(8,128)S(1)} %collective-permute-done.31.refs_3_.rest_9_), channel_id=1, source_target_pairs={{0,112},{8,120},{16,0},{24,8},{32,16},{40,24},{48,32},{56,40},{64,... | collective-permute-start | bytes 393224 | tf_op jit(solution)/shard_map/ppermute | solution.py:437
  112.7 8.8 %collective-permute-start.38 = (f32[6,8,4096]{2,1,0:T(8,128)}, f32[6,8,4096]{2,1,0:T(8,128)}, u32[]{:S(2)}, u32[]{:S(2)}) collective-permute-start(f32[6,8,4096]{2,1,0:T(8,128)} %shard_map.138), channel_id=1, source_target_pairs={{0,8},{8,0},{16,24},{24,16},{32,40},{40,32},{48,56},{56,48},{64,72... | collective-permute-start | bytes 2359304 | tf_op jit(solution)/shard_map/ppermute | solution.py:445
  121.7 2.6 %collective-permute-start.37 = (f32[1,8,4096]{2,1,0:T(8,128)S(1)}, f32[1,8,4096]{2,1,0:T(8,128)S(1)}, u32[]{:S(2)}, u32[]{:S(2)}) collective-permute-start(f32[1,8,4096]{2,1,0:T(8,128)S(1)} %collective-permute-done.35.refs_3_.rest_13_), channel_id=1, source_target_pairs={{0,112},{8,120},{16,0},{24,8},{32,16},{40,24},{48,32},{56,40},{64,... | collective-permute-start | bytes 393224 | tf_op jit(solution)/shard_map/ppermute | solution.py:437
  124.3 3.4 %collective-permute-done.34.refs_2_.rest_12_ = f32[1,8,4096]{2,1,0:T(8,128)S(1)} collective-permute-done((f32[1,8,4096]{2,1,0:T(8,128)S(1)}, f32[1,8,4096]{2,1,0:T(8,128)S(1)}, u32[]{:S(2)}, u32[]{:S(2)}) %collective-permute-start.34) | collective-permute-done | bytes 131104 | tf_op jit(solution)/shard_map/ppermute | solution.py:437
  127.8 4.6 %collective-permute-start.1 = (f32[6,8,3072]{2,1,0:T(8,128)}, f32[6,8,3072]{2,1,0:T(8,128)}, u32[]{:S(2)}, u32[]{:S(2)}) collective-permute-start(f32[6,8,3072]{2,1,0:T(8,128)} %copy-done.39), channel_id=1, source_target_pairs={{1,0},{2,1},{3,2},{4,3},{5,4},{6,5},{7,6},{0,7},{9,8},{10,9},{11,1... | collective-permute-start | bytes 1769480 | tf_op jit(solution)/shard_map/ppermute | solution.py:397
  134.0 1.7 %collective-permute-start.39 = (f32[4,8,4096]{2,1,0:T(8,128)}, f32[4,8,4096]{2,1,0:T(8,128)}, u32[]{:S(2)}, u32[]{:S(2)}) collective-permute-start(f32[4,8,4096]{2,1,0:T(8,128)} %shard_map.139), channel_id=1, source_target_pairs={{0,8},{8,0},{16,24},{24,16},{32,40},{40,32},{48,56},{56,48},{64,72... | collective-permute-start | bytes 1572872 | tf_op jit(solution)/shard_map/ppermute | solution.py:445
  139.5 1.6 %copy-done.3 = f32[16,8,4096]{2,1,0:T(8,128)S(1)} copy-done((f32[16,8,4096]{2,1,0:T(8,128)S(1)}, f32[16,8,4096]{2,1,0:T(8,128)}, u32[]{:S(2)}) %copy-start.3) | copy-done | bytes 2097176
  141.1 4.7 %shard_map.124.rest_0_ = f32[16,8,4096]{2,1,0:T(8,128)} custom-call(f32[16,8,4096]{2,1,0:T(8,128)S(1)} %copy-done.1, f32[10,8,3072]{2,1,0:T(8,128)S(1)} %collective-permute-done.2.low, f32[10,8,3072]{2,1,0:T(8,128)} %collective-permute-done.3.high, f32[16,8,4096]{2,1,0:T(8,128)S(1)} %copy-done.3, f32[8,4096]{1,0:T(8,128)S(1)} %copy-done.4, ...), custom_call_target="tpu_custom_call" | custom-call | flops 524288000 | bytes 6225920 | tf_op jit(solution)/shard_map/pallas_call | solution.py:175
  145.9 4.2 %shard_map.125 = f32[16,8,4096]{2,1,0:T(8,128)} custom-call(f32[16,8,4096]{2,1,0:T(8,128)S(1)} %copy-done.1, f32[6,8,3072]{2,1,0:T(8,128)} %collective-permute-done.low, f32[6,8,3072]{2,1,0:T(8,128)} %collective-permute-done.1.high, f32[16,8,4096]{2,1,0:T(8,128)S(1)} %copy-done.3, f32[8,4096]{1,0:T(8,128)S(1)} %copy-done.4, ...), custom_call_target="tpu_custom_call", output_to_operand_aliasing={{}: (6, {})} | custom-call | flops 314572800 | bytes 3735552 | tf_op jit(solution)/shard_map/pallas_call | solution.py:175
  150.2 4.6 %shard_map.143 = f32[16,8,4096]{2,1,0:T(8,128)} custom-call(f32[16,8,4096]{2,1,0:T(8,128)S(1)} %copy-done.5, f32[1,8,4096]{2,1,0:T(8,128)S(1)} %shard_map.135.refs_0_.rest_0_, f32[1,8,4096]{2,1,0:T(8,128)S(1)} %shard_map.137.refs_1_.rest_1_, f32[1,8,4096]{2,1,0:T(8,128)S(1)} %copy-done.10, f32[1,8,4096]{2,1,0:T(8,128)S(1)} %copy-done.8, ...), custom_call_target="tpu_custom_call" | custom-call | flops 805306368 | bytes 8388608 | tf_op jit(solution)/shard_map/pallas_call | solution.py:260
  (158 shorter events, 31.0 us)
Async XLA Ops:
  1.6 11.0 %collective-permute-start.5 = (f32[1,8,4096]{2,1,0:T(8,128)S(1)}, f32[1,8,4096]{2,1,0:T(8,128)S(1)}, u32[]{:S(2)}, u32[]{:S(2)}) collective-permute-start(f32[1,8,4096]{2,1,0:T(8,128)S(1)} %get-tuple-element.46), channel_id=1, source_target_pairs={{0,112},{8,120},{16,0},{24,8},{32,16},{40,24},{48,32},{56,40},{64,... | collective-permute-start | bytes 393224 | tf_op jit(solution)/shard_map/ppermute | solution.py:386
  9.1 9.0 %collective-permute-start.15 = (f32[1,8,4096]{2,1,0:T(8,128)S(1)}, f32[1,8,4096]{2,1,0:T(8,128)S(1)}, u32[]{:S(2)}, u32[]{:S(2)}) collective-permute-start(f32[1,8,4096]{2,1,0:T(8,128)S(1)} %get-tuple-element.44), channel_id=1, source_target_pairs={{0,112},{8,120},{16,0},{24,8},{32,16},{40,24},{48,32},{56,40},{64,... | collective-permute-start | bytes 393224 | tf_op jit(solution)/shard_map/ppermute | solution.py:386
  15.3 7.0 %collective-permute-start.6 = (f32[2,8,4096]{2,1,0:T(8,128)S(1)}, f32[2,8,4096]{2,1,0:T(8,128)S(1)}, u32[]{:S(2)}, u32[]{:S(2)}) collective-permute-start(f32[2,8,4096]{2,1,0:T(8,128)S(1)} %get-tuple-element.27), channel_id=1, source_target_pairs={{0,16},{8,24},{16,32},{24,40},{32,48},{40,56},{48,64},{56,72},{64,... | collective-permute-start | bytes 786440 | tf_op jit(solution)/shard_map/ppermute | solution.py:389
  18.7 11.1 %collective-permute-start.16 = (f32[2,8,4096]{2,1,0:T(8,128)S(1)}, f32[2,8,4096]{2,1,0:T(8,128)S(1)}, u32[]{:S(2)}, u32[]{:S(2)}) collective-permute-start(f32[2,8,4096]{2,1,0:T(8,128)S(1)} %get-tuple-element.36), channel_id=1, source_target_pairs={{0,16},{8,24},{16,32},{24,40},{32,48},{40,56},{48,64},{56,72},{64,... | collective-permute-start | bytes 786440 | tf_op jit(solution)/shard_map/ppermute | solution.py:389
  18.8 11.0 %collective-permute-start.17 = (f32[2,8,4096]{2,1,0:T(8,128)S(1)}, f32[2,8,4096]{2,1,0:T(8,128)S(1)}, u32[]{:S(2)}, u32[]{:S(2)}) collective-permute-start(f32[2,8,4096]{2,1,0:T(8,128)S(1)} %get-tuple-element.37), channel_id=1, source_target_pairs={{0,112},{8,120},{16,0},{24,8},{32,16},{40,24},{48,32},{56,40},{64,... | collective-permute-start | bytes 786440 | tf_op jit(solution)/shard_map/ppermute | solution.py:390
  23.0 10.9 %collective-permute-start.8 = (f32[2,8,4096]{2,1,0:T(8,128)S(1)}, f32[2,8,4096]{2,1,0:T(8,128)S(1)}, u32[]{:S(2)}, u32[]{:S(2)}) collective-permute-start(f32[2,8,4096]{2,1,0:T(8,128)S(1)} %get-tuple-element.29), channel_id=1, source_target_pairs={{0,16},{8,24},{16,32},{24,40},{32,48},{40,56},{48,64},{56,72},{64,... | collective-permute-start | bytes 786440 | tf_op jit(solution)/shard_map/ppermute | solution.py:389
  23.1 10.8 %collective-permute-start.9 = (f32[2,8,4096]{2,1,0:T(8,128)S(1)}, f32[2,8,4096]{2,1,0:T(8,128)S(1)}, u32[]{:S(2)}, u32[]{:S(2)}) collective-permute-start(f32[2,8,4096]{2,1,0:T(8,128)S(1)} %get-tuple-element.30), channel_id=1, source_target_pairs={{0,112},{8,120},{16,0},{24,8},{32,16},{40,24},{48,32},{56,40},{64,... | collective-permute-start | bytes 786440 | tf_op jit(solution)/shard_map/ppermute | solution.py:390
  27.1 72.8 %collective-permute-start.2 = (f32[10,8,3072]{2,1,0:T(8,128)}, f32[10,8,3072]{2,1,0:T(8,128)S(1)}, u32[]{:S(2)}, u32[]{:S(2)}) collective-permute-start(f32[10,8,3072]{2,1,0:T(8,128)} %get-tuple-element.25), channel_id=1, source_target_pairs={{0,1},{1,2},{2,3},{3,4},{4,5},{5,6},{6,7},{7,0},{8,9},{9,10},{10,1... | collective-permute-start | bytes 2949128 | tf_op jit(solution)/shard_map/ppermute | solution.py:396
  30.4 8.3 %collective-permute-start.18 = (f32[2,8,4096]{2,1,0:T(8,128)S(1)}, f32[2,8,4096]{2,1,0:T(8,128)S(1)}, u32[]{:S(2)}, u32[]{:S(2)}) collective-permute-start(f32[2,8,4096]{2,1,0:T(8,128)S(1)} %get-tuple-element.38), channel_id=1, source_target_pairs={{0,16},{8,24},{16,32},{24,40},{32,48},{40,56},{48,64},{56,72},{64,... | collective-permute-start | bytes 786440 | tf_op jit(solution)/shard_map/ppermute | solution.py:389
  30.5 8.2 %collective-permute-start.19 = (f32[2,8,4096]{2,1,0:T(8,128)S(1)}, f32[2,8,4096]{2,1,0:T(8,128)S(1)}, u32[]{:S(2)}, u32[]{:S(2)}) collective-permute-start(f32[2,8,4096]{2,1,0:T(8,128)S(1)} %get-tuple-element.39), channel_id=1, source_target_pairs={{0,112},{8,120},{16,0},{24,8},{32,16},{40,24},{48,32},{56,40},{64,... | collective-permute-start | bytes 786440 | tf_op jit(solution)/shard_map/ppermute | solution.py:390
  34.5 9.4 %collective-permute-start.10 = (f32[2,8,4096]{2,1,0:T(8,128)S(1)}, f32[2,8,4096]{2,1,0:T(8,128)S(1)}, u32[]{:S(2)}, u32[]{:S(2)}) collective-permute-start(f32[2,8,4096]{2,1,0:T(8,128)S(1)} %get-tuple-element.31), channel_id=1, source_target_pairs={{0,16},{8,24},{16,32},{24,40},{32,48},{40,56},{48,64},{56,72},{64,... | collective-permute-start | bytes 786440 | tf_op jit(solution)/shard_map/ppermute | solution.py:389
  34.6 12.0 %collective-permute-start.11 = (f32[2,8,4096]{2,1,0:T(8,128)S(1)}, f32[2,8,4096]{2,1,0:T(8,128)S(1)}, u32[]{:S(2)}, u32[]{:S(2)}) collective-permute-start(f32[2,8,4096]{2,1,0:T(8,128)S(1)} %get-tuple-element.32), channel_id=1, source_target_pairs={{0,112},{8,120},{16,0},{24,8},{32,16},{40,24},{48,32},{56,40},{64,... | collective-permute-start | bytes 786440 | tf_op jit(solution)/shard_map/ppermute | solution.py:390
  39.3 10.1 %collective-permute-start.20 = (f32[2,8,4096]{2,1,0:T(8,128)S(1)}, f32[2,8,4096]{2,1,0:T(8,128)S(1)}, u32[]{:S(2)}, u32[]{:S(2)}) collective-permute-start(f32[2,8,4096]{2,1,0:T(8,128)S(1)} %get-tuple-element.40), channel_id=1, source_target_pairs={{0,16},{8,24},{16,32},{24,40},{32,48},{40,56},{48,64},{56,72},{64,... | collective-permute-start | bytes 786440 | tf_op jit(solution)/shard_map/ppermute | solution.py:389
  41.0 57.9 %collective-permute-start = (f32[6,8,3072]{2,1,0:T(8,128)}, f32[6,8,3072]{2,1,0:T(8,128)}, u32[]{:S(2)}, u32[]{:S(2)}) collective-permute-start(f32[6,8,3072]{2,1,0:T(8,128)} %get-tuple-element.23), channel_id=1, source_target_pairs={{0,1},{1,2},{2,3},{3,4},{4,5},{5,6},{6,7},{7,0},{8,9},{9,10},{10,1... | collective-permute-start | bytes 1769480 | tf_op jit(solution)/shard_map/ppermute | solution.py:396
  43.9 12.0 %collective-permute-start.21 = (f32[2,8,4096]{2,1,0:T(8,128)S(1)}, f32[2,8,4096]{2,1,0:T(8,128)S(1)}, u32[]{:S(2)}, u32[]{:S(2)}) collective-permute-start(f32[2,8,4096]{2,1,0:T(8,128)S(1)} %get-tuple-element.41), channel_id=1, source_target_pairs={{0,112},{8,120},{16,0},{24,8},{32,16},{40,24},{48,32},{56,40},{64,... | collective-permute-start | bytes 786440 | tf_op jit(solution)/shard_map/ppermute | solution.py:390
  47.3 18.4 %collective-permute-start.12 = (f32[2,8,3072]{2,1,0:T(8,128)S(1)}, f32[2,8,3072]{2,1,0:T(8,128)S(1)}, u32[]{:S(2)}, u32[]{:S(2)}) collective-permute-start(f32[2,8,3072]{2,1,0:T(8,128)S(1)} %get-tuple-element.34), channel_id=1, source_target_pairs={{0,1},{1,2},{2,3},{3,4},{4,5},{5,6},{6,7},{7,0},{8,9},{9,10},{10,1... | collective-permute-start | bytes 589832 | tf_op jit(solution)/shard_map/ppermute | solution.py:396
  49.4 19.1 %collective-permute-start.13 = (f32[2,8,3072]{2,1,0:T(8,128)S(1)}, f32[2,8,3072]{2,1,0:T(8,128)S(1)}, u32[]{:S(2)}, u32[]{:S(2)}) collective-permute-start(f32[2,8,3072]{2,1,0:T(8,128)S(1)} %get-tuple-element.35), channel_id=1, source_target_pairs={{1,0},{2,1},{3,2},{4,3},{5,4},{6,5},{7,6},{0,7},{9,8},{10,9},{11,1... | collective-permute-start | bytes 589832 | tf_op jit(solution)/shard_map/ppermute | solution.py:397
  70.7 66.6 %collective-permute-start.3 = (f32[10,8,3072]{2,1,0:T(8,128)}, f32[10,8,3072]{2,1,0:T(8,128)}, u32[]{:S(2)}, u32[]{:S(2)}) collective-permute-start(f32[10,8,3072]{2,1,0:T(8,128)} %get-tuple-element.26), channel_id=1, source_target_pairs={{1,0},{2,1},{3,2},{4,3},{5,4},{6,5},{7,6},{0,7},{9,8},{10,9},{11,1... | collective-permute-start | bytes 2949128 | tf_op jit(solution)/shard_map/ppermute | solution.py:397
  74.7 18.3 %collective-permute-start.23 = (f32[1,8,4096]{2,1,0:T(8,128)}, f32[1,8,4096]{2,1,0:T(8,128)S(1)}, u32[]{:S(2)}, u32[]{:S(2)}) collective-permute-start(f32[1,8,4096]{2,1,0:T(8,128)} %shard_map.136.mine), channel_id=1, source_target_pairs={{0,128},{8,136},{16,144},{24,152},{32,160},{40,168},{48,176},{56,1... | collective-permute-start | bytes 393224 | tf_op jit(solution)/shard_map/ppermute | solution.py:428
  76.1 24.6 %collective-permute-start.25 = (f32[1,8,4096]{2,1,0:T(8,128)S(1)}, f32[1,8,4096]{2,1,0:T(8,128)S(1)}, u32[]{:S(2)}, u32[]{:S(2)}) collective-permute-start(f32[1,8,4096]{2,1,0:T(8,128)S(1)} %shard_map.135.refs_0_.rest_0_), channel_id=1, source_target_pairs={{0,112},{8,120},{16,0},{24,8},{32,16},{40,24},{48,32},{56,40},{64,... | collective-permute-start | bytes 393224 | tf_op jit(solution)/shard_map/ppermute | solution.py:437
  93.7 8.9 %collective-permute-start.24 = (f32[1,8,4096]{2,1,0:T(8,128)S(1)}, f32[1,8,4096]{2,1,0:T(8,128)S(1)}, u32[]{:S(2)}, u32[]{:S(2)}) collective-permute-start(f32[1,8,4096]{2,1,0:T(8,128)S(1)} %shard_map.135.refs_0_.rest_0_), channel_id=1, source_target_pairs={{0,16},{8,24},{16,32},{24,40},{32,48},{40,56},{48,64},{56,72},{64,... | collective-permute-start | bytes 393224 | tf_op jit(solution)/shard_map/ppermute | solution.py:437
  105.3 7.4 %collective-permute-start.30 = (f32[1,8,4096]{2,1,0:T(8,128)S(1)}, f32[1,8,4096]{2,1,0:T(8,128)S(1)}, u32[]{:S(2)}, u32[]{:S(2)}) collective-permute-start(f32[1,8,4096]{2,1,0:T(8,128)S(1)} %collective-permute-done.26.refs_4_.rest_4_), channel_id=1, source_target_pairs={{0,16},{8,24},{16,32},{24,40},{32,48},{40,56},{48,64},{56,72},{64,... | collective-permute-start | bytes 393224 | tf_op jit(solution)/shard_map/ppermute | solution.py:437
  105.3 16.2 %collective-permute-start.33 = (f32[1,8,4096]{2,1,0:T(8,128)S(1)}, f32[1,8,4096]{2,1,0:T(8,128)S(1)}, u32[]{:S(2)}, u32[]{:S(2)}) collective-permute-start(f32[1,8,4096]{2,1,0:T(8,128)S(1)} %collective-permute-done.29.refs_1_.rest_7_), channel_id=1, source_target_pairs={{0,112},{8,120},{16,0},{24,8},{32,16},{40,24},{48,32},{56,40},{64,... | collective-permute-start | bytes 393224 | tf_op jit(solution)/shard_map/ppermute | solution.py:437
  108.4 13.1 %collective-permute-start.32 = (f32[1,8,4096]{2,1,0:T(8,128)S(1)}, f32[1,8,4096]{2,1,0:T(8,128)S(1)}, u32[]{:S(2)}, u32[]{:S(2)}) collective-permute-start(f32[1,8,4096]{2,1,0:T(8,128)S(1)} %collective-permute-done.28.refs_0_.rest_6_), channel_id=1, source_target_pairs={{0,16},{8,24},{16,32},{24,40},{32,48},{40,56},{48,64},{56,72},{64,... | collective-permute-start | bytes 393224 | tf_op jit(solution)/shard_map/ppermute | solution.py:437
  108.4 13.2 %collective-permute-start.35 = (f32[1,8,4096]{2,1,0:T(8,128)S(1)}, f32[1,8,4096]{2,1,0:T(8,128)S(1)}, u32[]{:S(2)}, u32[]{:S(2)}) collective-permute-start(f32[1,8,4096]{2,1,0:T(8,128)S(1)} %collective-permute-done.31.refs_3_.rest_9_), channel_id=1, source_target_pairs={{0,112},{8,120},{16,0},{24,8},{32,16},{40,24},{48,32},{56,40},{64,... | collective-permute-start | bytes 393224 | tf_op jit(solution)/shard_map/ppermute | solution.py:437
  112.7 37.4 %collective-permute-start.38 = (f32[6,8,4096]{2,1,0:T(8,128)}, f32[6,8,4096]{2,1,0:T(8,128)}, u32[]{:S(2)}, u32[]{:S(2)}) collective-permute-start(f32[6,8,4096]{2,1,0:T(8,128)} %shard_map.138), channel_id=1, source_target_pairs={{0,8},{8,0},{16,24},{24,16},{32,40},{40,32},{48,56},{56,48},{64,72... | collective-permute-start | bytes 2359304 | tf_op jit(solution)/shard_map/ppermute | solution.py:445
  121.6 12.5 %collective-permute-start.36 = (f32[1,8,4096]{2,1,0:T(8,128)S(1)}, f32[1,8,4096]{2,1,0:T(8,128)S(1)}, u32[]{:S(2)}, u32[]{:S(2)}) collective-permute-start(f32[1,8,4096]{2,1,0:T(8,128)S(1)} %collective-permute-done.32.refs_0_.rest_10_), channel_id=1, source_target_pairs={{0,16},{8,24},{16,32},{24,40},{32,48},{40,56},{48,64},{56,72},{64,... | collective-permute-start | bytes 393224 | tf_op jit(solution)/shard_map/ppermute | solution.py:437
  121.7 14.0 %collective-permute-start.37 = (f32[1,8,4096]{2,1,0:T(8,128)S(1)}, f32[1,8,4096]{2,1,0:T(8,128)S(1)}, u32[]{:S(2)}, u32[]{:S(2)}) collective-permute-start(f32[1,8,4096]{2,1,0:T(8,128)S(1)} %collective-permute-done.35.refs_3_.rest_13_), channel_id=1, source_target_pairs={{0,112},{8,120},{16,0},{24,8},{32,16},{40,24},{48,32},{56,40},{64,... | collective-permute-start | bytes 393224 | tf_op jit(solution)/shard_map/ppermute | solution.py:437
  127.8 18.1 %collective-permute-start.1 = (f32[6,8,3072]{2,1,0:T(8,128)}, f32[6,8,3072]{2,1,0:T(8,128)}, u32[]{:S(2)}, u32[]{:S(2)}) collective-permute-start(f32[6,8,3072]{2,1,0:T(8,128)} %copy-done.39), channel_id=1, source_target_pairs={{1,0},{2,1},{3,2},{4,3},{5,4},{6,5},{7,6},{0,7},{9,8},{10,9},{11,1... | collective-permute-start | bytes 1769480 | tf_op jit(solution)/shard_map/ppermute | solution.py:397
  134.0 16.0 %collective-permute-start.39 = (f32[4,8,4096]{2,1,0:T(8,128)}, f32[4,8,4096]{2,1,0:T(8,128)}, u32[]{:S(2)}, u32[]{:S(2)}) collective-permute-start(f32[4,8,4096]{2,1,0:T(8,128)} %shard_map.139), channel_id=1, source_target_pairs={{0,8},{8,0},{16,24},{24,16},{32,40},{40,32},{48,56},{56,48},{64,72... | collective-permute-start | bytes 1572872 | tf_op jit(solution)/shard_map/ppermute | solution.py:445
  135.7 14.4 %collective-permute-start.40 = (f32[4,8,4096]{2,1,0:T(8,128)}, f32[4,8,4096]{2,1,0:T(8,128)}, u32[]{:S(2)}, u32[]{:S(2)}) collective-permute-start(f32[4,8,4096]{2,1,0:T(8,128)} %shard_map.140), channel_id=1, source_target_pairs={{0,8},{8,0},{16,24},{24,16},{32,40},{40,32},{48,56},{56,48},{64,72... | collective-permute-start | bytes 1572872 | tf_op jit(solution)/shard_map/ppermute | solution.py:445
  137.3 12.8 %collective-permute-start.41 = (f32[2,8,4096]{2,1,0:T(8,128)}, f32[2,8,4096]{2,1,0:T(8,128)}, u32[]{:S(2)}, u32[]{:S(2)}) collective-permute-start(f32[2,8,4096]{2,1,0:T(8,128)} %shard_map.141), channel_id=1, source_target_pairs={{0,8},{8,0},{16,24},{24,16},{32,40},{40,32},{48,56},{56,48},{64,72... | collective-permute-start | bytes 786440 | tf_op jit(solution)/shard_map/ppermute | solution.py:445
  (50 other events, 438.8 us)

commit v4 on v3

--- a/solution.py
+++ b/solution.py
@@ -50,15 +50,20 @@
     return jnp.where(sub < limit, full, spare) if below else jnp.where(sub >= limit, full, spare)
 
 
+def pack_one(i, orb, head, tail):
+    for g in range(orb.shape[2] // (4 * LANES)):
+        tiles = [orb[i, :, (4 * g + m) * LANES : (4 * g + m + 1) * LANES] for m in range(4)]
+        for m in range(3):
+            spare = pltpu.roll(tiles[3], 6 - 2 * m, 0)
+            span = slice((3 * g + m) * LANES, (3 * g + m + 1) * LANES)
+            head[i, :, span] = mixed(tiles[m], spare, WIDTH, True)
+            tail[i, :, span] = mixed(tiles[m], spare, 2, False)
+
+
 def pack_body(orb, head, tail):
-    for i in range(orb.shape[0]):
-        for g in range(orb.shape[2] // (4 * LANES)):
-            tiles = [orb[i, :, (4 * g + m) * LANES : (4 * g + m + 1) * LANES] for m in range(4)]
-            for m in range(3):
-                spare = pltpu.roll(tiles[3], 6 - 2 * m, 0)
-                span = slice((3 * g + m) * LANES, (3 * g + m + 1) * LANES)
-                head[i, :, span] = mixed(tiles[m], spare, WIDTH, True)
-                tail[i, :, span] = mixed(tiles[m], spare, 2, False)
+    @pl.loop(0, head.shape[0])
+    def _(i):
+        pack_one(i, orb, head, tail)
 
 
 def unpacked(side, i, first):
@@ -286,6 +291,47 @@
 PARTNER = everywhere(lambda x, z, c: (x, z, 1 - c))
 
 
+def open_body(place, orb, head, tail, first, second, held, hand, sems):
+    share, half = hand.shape[0], first.shape[0]
+    start = ((place[0] + RING // 2) & (RING - 1)) * share
+    step = split(held.shape[0])
+    copies = [pltpu.make_async_copy(orb.at[pl.ds(start, share)], hand, sems.at[0])]
+    for i in range(0, held.shape[0], step):
+        part = pl.ds(i, step)
+        copies.append(pltpu.make_async_copy(orb.at[part], held.at[part], sems.at[len(copies)]))
+    for copy in copies:
+        copy.start()
+    copies[0].wait()
+    first[...] = hand[:half]
+    second[...] = hand[half:]
+    for i, copy in enumerate(copies[1:]):
+        copy.wait()
+
+        @pl.loop(i * step, i * step + step)
+        def _(m):
+            pack_one(m, held, head, tail)
+
+
+def opening(orb, place, early):
+    n, planes, cells = orb.shape
+    share = n // RING
+    shapes = [(early, planes, cells * WIDTH // planes)] * 2 + [(share // 2, planes, cells)] * 2
+    still = pl.BlockSpec(memory_space=pltpu.VMEM)
+    return pl.pallas_call(
+        open_body,
+        in_specs=[pl.BlockSpec(memory_space=pltpu.SMEM), pl.BlockSpec(memory_space=pltpu.HBM)],
+        out_specs=[still] * 4,
+        out_shape=[jax.ShapeDtypeStruct(shape, jnp.float32) for shape in shapes],
+        scratch_shapes=[
+            pltpu.VMEM((early, planes, cells), jnp.float32),
+            pltpu.VMEM((share, planes, cells), jnp.float32),
+            pltpu.SemaphoreType.DMA((early // split(early) + 1,)),
+        ],
+        compiler_params=room(60),
+        cost_estimate=pl.CostEstimate(flops=0, bytes_accessed=8 * n * planes * cells, transcendentals=0),
+    )(place, orb)
+
+
 def pick_body(place, hand_up, hand_down, up, down, out_up, out_down):
     for hand, moved, out in ((hand_up, up, out_up), (hand_down, down, out_down)):
         for m in range(out.shape[0]):
@@ -342,22 +388,6 @@
     )(place, block, up, down)
 
 
-def keep_body(flag, mine, other, out):
-    out[...] = jnp.where(flag[0] == 1, mine[...], other[...])
-
-
-def keep(flag, mine, other):
-    whole = pl.BlockSpec(memory_space=pltpu.VMEM)
-    return pl.pallas_call(
-        keep_body,
-        in_specs=[pl.BlockSpec(memory_space=pltpu.SMEM), whole, whole],
-        out_specs=whole,
-        out_shape=jax.ShapeDtypeStruct(mine.shape, jnp.float32),
-        compiler_params=room(2),
-        cost_estimate=pl.CostEstimate(flops=0, bytes_accessed=12 * mine.size, transcendentals=0),
-    )(flag, mine, other)
-
-
 def stack_body(*refs):
     out = refs[-1]
     for i, ref in enumerate(refs[:-1]):
@@ -377,13 +407,9 @@
     )(*blocks)
 
 
-def relay(block, place, packed):
-    share = block.shape[0] // RING
-    half = share // 2
-    start = ((place[0] + 4) & (RING - 1)) * share
-    size = (half,) + block.shape[1:]
-    up = lax.ppermute(lax.dynamic_slice(block, (start, 0, 0), size), "band", ONWARD)
-    down = lax.ppermute(lax.dynamic_slice(block, (start + half, 0, 0), size), "band", BACK)
+def relay(block, place, packed, opposite):
+    up = lax.ppermute(opposite[0], "band", ONWARD)
+    down = lax.ppermute(opposite[1], "band", BACK)
     for step in (3, 2, 1):
         up, down = pick(block, place, step, up, down)
         up = lax.ppermute(up, "band", ONWARD)
@@ -408,25 +434,27 @@
 
     offset = (z - root_z) & (RING - 1)
 
-    early = count * 5 // 8
-    ends = pack(orbitals, 0, early)
+    early = count * 9 // 16
+    place = jnp.stack([z, offset])
+    *ends, first, second = opening(orbitals, place, early)
     sides_early = halo(*ends)
     ends = pack(orbitals, early, count - early)
     sides_late = halo(*ends)
 
-    place = jnp.stack([z, offset])
-    piece, *ends = relay(orbitals, place, True)
-    (before,) = relay(previous, place, False)
+    piece, *ends = relay(orbitals, place, True, (first, second))
+    start = ((z + RING // 2) & (RING - 1)) * share
+    size = (share // 2,) + previous.shape[1:]
+    opposite = [lax.dynamic_slice(previous, (start + m * size[0], 0, 0), size) for m in range(2)]
+    (before,) = relay(previous, place, False, opposite)
     below, above = halo(*ends)
     filtered = apply_filter(orbitals, *sides_early, previous, potential)
     filtered = apply_filter(orbitals, *sides_late, previous, potential, early, out=early, into=filtered)
 
-    flag = (x == root_x).astype(jnp.int32)[None]
     chains = []
     for m in range(share):
         mine = apply_filter(piece, below, above, before, potential, m, 1, m, total=1)
         other = lax.ppermute(mine, "band", ACROSS)
-        chains.append([keep(flag, mine, other)] * 2)
+        chains.append([jnp.where(x == root_x, mine, other)] * 2)
     rounds = [[(chain[0], 0, m) for m, chain in enumerate(chains)]]
     for hop in range(1, RING // 2 + 1):
         rounds.append([])

time: 155 us -> 177 us (1.14)
  waiting for transfers between devices: 35.7 us -> 71 us
  starting transfers between devices: 79.3 us -> 69.4 us
  local copies, waits for them, and re-layouts: 8.89 us -> 2.4 us
    ppermute x2, waiting for transfers between devices: 15.5 us -> 44.4 us  [step(): other = lax.ppermute(mine, 'band', ACROSS)]
    ppermute x4, waiting for transfers between devices: 0.55 us -> 8.5 us  [the longest x2 8.5 us: relay(): up = lax.ppermute(opposite[0], 'band', ONWARD)]
    ppermute x3, waiting for transfers between devices: 9.08 us -> 2.38 us  [halo(): lax.ppermute(tail, 'domain', [(i, (i + 1) % size) for i in range(size)])]
    ppermute x3, starting transfers between devices: 14.3 us -> 9.1 us  [halo(): lax.ppermute(head, 'domain', [((i + 1) % size, i) for i in range(size)])]
    ppermute x14, starting transfers between devices: 19.4 us -> 14.4 us  [step(): chain[way] = lax.ppermute(chain[way], 'band', pairs)]
    unnamed x80 -> x70, local copies, waits for them, and re-layouts: 6.92 us -> 2.39 us
    ppermute x6, waiting for transfers between devices: 3.41 us -> 7.7 us  [relay(): up = lax.ppermute(up, 'band', ONWARD)]
    ppermute x14, waiting for transfers between devices: 4.23 us -> 7.07 us  [step(): chain[way] = lax.ppermute(chain[way], 'band', pairs)]
  transfers between devices with their start and end apart: 42 -> 42, of which waited for: 12 -> 15; matrix products, arithmetic and copies ran while one was open for 1% -> 0% of each run, Pallas kernels for 16% -> 12%
where the time goes in v4:
time: 177 us; the launch traced here: 176 us
  waiting for transfers between devices  71 us (40%)
  starting transfers between devices  69.4 us (39%)
  Pallas kernels  30.7 us (17%)
  local copies, waits for them, and re-layouts  2.4 us (1%)
  between operations  1.98 us (1%)
    ppermute x2, waiting for transfers between devices, step(): other = lax.ppermute(mine, 'band', ACROSS)  44.4 us
    ppermute x14, starting transfers between devices, step(): chain[way] = lax.ppermute(chain[way], 'band', pairs)  14.4 us
    ppermute x6, starting transfers between devices, relay(): down = lax.ppermute(down, 'band', BACK)  13.5 us
    ppermute x4, starting transfers between devices, step(): theirs.append(lax.ppermute(group, 'band', PARTNER))  12.9 us
    pallas_call x4, Pallas kernels, apply_filter(): pl.pallas_call(filter_body, grid=(n // step,), in_specs=specs, out_specs=...  11.2 us
    ppermute x3, starting transfers between devices, halo(): lax.ppermute(head, 'domain', [((i + 1) % size, i) for i in range(size)])  9.1 us
    ppermute x2, waiting for transfers between devices, relay(): up = lax.ppermute(opposite[0], 'band', ONWARD)  8.5 us
    ppermute x6, waiting for transfers between devices, relay(): up = lax.ppermute(up, 'band', ONWARD)  7.7 us
  transfers between devices with their start and end apart: 42, of which 15 were waited for; matrix products, arithmetic and copies ran while one was open for 0% of the time, Pallas kernels for 12%

profile of v4, /device:TPU:1, one launch (start us, length us, event | category | flops | bytes accessed | tf_op | source)
XLA Modules:
  0.0 176.2 jit_solution(14427644918586182601)
XLA Ops:
  2.1 3.4 %shard_map.123 = (f32[9,8,3072]{2,1,0:T(8,128)}, f32[9,8,3072]{2,1,0:T(8,128)}, f32[1,8,4096]{2,1,0:T(8,128)}, f32[1,8,4096]{2,1,0:T(8,128)}) custom-call(s32[2]{0:T(128)} %pad_add_fusion.place, f32[16,8,4096]{2,1,0:T(8,128)} %own.2), custom_call_target="tpu_custom_call" | custom-call | bytes 4194304 | tf_op jit(solution)/shard_map/pallas_call | solution.py:320
  5.5 2.5 %collective-permute-start.4 = (f32[1,8,4096]{2,1,0:T(8,128)}, f32[1,8,4096]{2,1,0:T(8,128)S(1)}, u32[]{:S(2)}, u32[]{:S(2)}) collective-permute-start(f32[1,8,4096]{2,1,0:T(8,128)} %get-tuple-element.29), channel_id=1, source_target_pairs={{0,16},{8,24},{16,32},{24,40},{32,48},{40,56},{48,64},{56,72},{64,... | collective-permute-start | bytes 393224 | tf_op jit(solution)/shard_map/ppermute | solution.py:411
  8.0 4.0 %collective-permute-start.5 = (f32[1,8,4096]{2,1,0:T(8,128)}, f32[1,8,4096]{2,1,0:T(8,128)S(1)}, u32[]{:S(2)}, u32[]{:S(2)}) collective-permute-start(f32[1,8,4096]{2,1,0:T(8,128)} %get-tuple-element.30), channel_id=1, source_target_pairs={{0,112},{8,120},{16,0},{24,8},{32,16},{40,24},{48,32},{56,40},{64,... | collective-permute-start | bytes 393224 | tf_op jit(solution)/shard_map/ppermute | solution.py:412
  12.0 3.3 %collective-permute-done.4.up = f32[1,8,4096]{2,1,0:T(8,128)S(1)} collective-permute-done((f32[1,8,4096]{2,1,0:T(8,128)}, f32[1,8,4096]{2,1,0:T(8,128)S(1)}, u32[]{:S(2)}, u32[]{:S(2)}) %collective-permute-start.4) | collective-permute-done | bytes 131104 | tf_op jit(solution)/shard_map/ppermute | solution.py:411
  16.0 2.7 %collective-permute-start.7 = (f32[2,8,4096]{2,1,0:T(8,128)S(1)}, f32[2,8,4096]{2,1,0:T(8,128)S(1)}, u32[]{:S(2)}, u32[]{:S(2)}) collective-permute-start(f32[2,8,4096]{2,1,0:T(8,128)S(1)} %get-tuple-element.32), channel_id=1, source_target_pairs={{0,112},{8,120},{16,0},{24,8},{32,16},{40,24},{48,32},{56,40},{64,... | collective-permute-start | bytes 786440 | tf_op jit(solution)/shard_map/ppermute | solution.py:416
  18.8 2.7 %collective-permute-start.15 = (f32[1,8,4096]{2,1,0:T(8,128)S(1)}, f32[1,8,4096]{2,1,0:T(8,128)S(1)}, u32[]{:S(2)}, u32[]{:S(2)}) collective-permute-start(f32[1,8,4096]{2,1,0:T(8,128)S(1)} %get-tuple-element.48), channel_id=1, source_target_pairs={{0,112},{8,120},{16,0},{24,8},{32,16},{40,24},{48,32},{56,40},{64,... | collective-permute-start | bytes 393224 | tf_op jit(solution)/shard_map/ppermute | solution.py:412
  21.5 5.2 %collective-permute-done.14.up = f32[1,8,4096]{2,1,0:T(8,128)S(1)} collective-permute-done((f32[1,8,4096]{2,1,0:T(8,128)S(1)}, f32[1,8,4096]{2,1,0:T(8,128)S(1)}, u32[]{:S(2)}, u32[]{:S(2)}) %collective-permute-start.14) | collective-permute-done | bytes 131104 | tf_op jit(solution)/shard_map/ppermute | solution.py:411
  27.8 2.2 %collective-permute-start.17 = (f32[2,8,4096]{2,1,0:T(8,128)S(1)}, f32[2,8,4096]{2,1,0:T(8,128)S(1)}, u32[]{:S(2)}, u32[]{:S(2)}) collective-permute-start(f32[2,8,4096]{2,1,0:T(8,128)S(1)} %get-tuple-element.41), channel_id=1, source_target_pairs={{0,112},{8,120},{16,0},{24,8},{32,16},{40,24},{48,32},{56,40},{64,... | collective-permute-start | bytes 786440 | tf_op jit(solution)/shard_map/ppermute | solution.py:416
  30.7 2.7 %collective-permute-start.9 = (f32[2,8,4096]{2,1,0:T(8,128)S(1)}, f32[2,8,4096]{2,1,0:T(8,128)S(1)}, u32[]{:S(2)}, u32[]{:S(2)}) collective-permute-start(f32[2,8,4096]{2,1,0:T(8,128)S(1)} %get-tuple-element.34), channel_id=1, source_target_pairs={{0,112},{8,120},{16,0},{24,8},{32,16},{40,24},{48,32},{56,40},{64,... | collective-permute-start | bytes 786440 | tf_op jit(solution)/shard_map/ppermute | solution.py:416
  37.7 2.6 %collective-permute-done.8.up = f32[2,8,4096]{2,1,0:T(8,128)S(1)} collective-permute-done((f32[2,8,4096]{2,1,0:T(8,128)S(1)}, f32[2,8,4096]{2,1,0:T(8,128)S(1)}, u32[]{:S(2)}, u32[]{:S(2)}) %collective-permute-start.8) | collective-permute-done | bytes 262176 | tf_op jit(solution)/shard_map/ppermute | solution.py:415
  41.4 2.3 %collective-permute-start.11 = (f32[2,8,4096]{2,1,0:T(8,128)S(1)}, f32[2,8,4096]{2,1,0:T(8,128)S(1)}, u32[]{:S(2)}, u32[]{:S(2)}) collective-permute-start(f32[2,8,4096]{2,1,0:T(8,128)S(1)} %get-tuple-element.36), channel_id=1, source_target_pairs={{0,112},{8,120},{16,0},{24,8},{32,16},{40,24},{48,32},{56,40},{64,... | collective-permute-start | bytes 786440 | tf_op jit(solution)/shard_map/ppermute | solution.py:416
  43.7 2.0 %collective-permute-done.18.up = f32[2,8,4096]{2,1,0:T(8,128)S(1)} collective-permute-done((f32[2,8,4096]{2,1,0:T(8,128)S(1)}, f32[2,8,4096]{2,1,0:T(8,128)S(1)}, u32[]{:S(2)}, u32[]{:S(2)}) %collective-permute-start.18) | collective-permute-done | bytes 262176 | tf_op jit(solution)/shard_map/ppermute | solution.py:415
  47.0 2.1 %collective-permute-start.21 = (f32[2,8,4096]{2,1,0:T(8,128)S(1)}, f32[2,8,4096]{2,1,0:T(8,128)S(1)}, u32[]{:S(2)}, u32[]{:S(2)}) collective-permute-start(f32[2,8,4096]{2,1,0:T(8,128)S(1)} %get-tuple-element.45), channel_id=1, source_target_pairs={{0,112},{8,120},{16,0},{24,8},{32,16},{40,24},{48,32},{56,40},{64,... | collective-permute-start | bytes 786440 | tf_op jit(solution)/shard_map/ppermute | solution.py:416
  49.1 2.2 %collective-permute-done.10.up = f32[2,8,4096]{2,1,0:T(8,128)S(1)} collective-permute-done((f32[2,8,4096]{2,1,0:T(8,128)S(1)}, f32[2,8,4096]{2,1,0:T(8,128)S(1)}, u32[]{:S(2)}, u32[]{:S(2)}) %collective-permute-start.10) | collective-permute-done | bytes 262176 | tf_op jit(solution)/shard_map/ppermute | solution.py:415
  52.0 2.8 %collective-permute-start.12 = (f32[2,8,3072]{2,1,0:T(8,128)S(1)}, f32[2,8,3072]{2,1,0:T(8,128)S(1)}, u32[]{:S(2)}, u32[]{:S(2)}) collective-permute-start(f32[2,8,3072]{2,1,0:T(8,128)S(1)} %get-tuple-element.38), channel_id=1, source_target_pairs={{0,1},{1,2},{2,3},{3,4},{4,5},{5,6},{6,7},{7,0},{8,9},{9,10},{10,1... | collective-permute-start | bytes 589832 | tf_op jit(solution)/shard_map/ppermute | solution.py:422
  54.8 2.5 %collective-permute-start.13 = (f32[2,8,3072]{2,1,0:T(8,128)S(1)}, f32[2,8,3072]{2,1,0:T(8,128)S(1)}, u32[]{:S(2)}, u32[]{:S(2)}) collective-permute-start(f32[2,8,3072]{2,1,0:T(8,128)S(1)} %get-tuple-element.39), channel_id=1, source_target_pairs={{1,0},{2,1},{3,2},{4,3},{5,4},{6,5},{7,6},{0,7},{9,8},{10,9},{11,1... | collective-permute-start | bytes 589832 | tf_op jit(solution)/shard_map/ppermute | solution.py:423
  57.9 2.4 %collective-permute-done.12.low = f32[2,8,3072]{2,1,0:T(8,128)S(1)} collective-permute-done((f32[2,8,3072]{2,1,0:T(8,128)S(1)}, f32[2,8,3072]{2,1,0:T(8,128)S(1)}, u32[]{:S(2)}, u32[]{:S(2)}) %collective-permute-start.12) | collective-permute-done | bytes 196640 | tf_op jit(solution)/shard_map/ppermute | solution.py:422
  62.8 2.4 %collective-permute-start.2 = (f32[9,8,3072]{2,1,0:T(8,128)}, f32[9,8,3072]{2,1,0:T(8,128)}, u32[]{:S(2)}, u32[]{:S(2)}) collective-permute-start(f32[9,8,3072]{2,1,0:T(8,128)} %get-tuple-element.27), channel_id=1, source_target_pairs={{0,1},{1,2},{2,3},{3,4},{4,5},{5,6},{6,7},{7,0},{8,9},{9,10},{10,1... | collective-permute-start | bytes 2654216 | tf_op jit(solution)/shard_map/ppermute | solution.py:422
  65.2 2.6 %collective-permute-start.3 = (f32[9,8,3072]{2,1,0:T(8,128)}, f32[9,8,3072]{2,1,0:T(8,128)}, u32[]{:S(2)}, u32[]{:S(2)}) collective-permute-start(f32[9,8,3072]{2,1,0:T(8,128)} %get-tuple-element.28), channel_id=1, source_target_pairs={{1,0},{2,1},{3,2},{4,3},{5,4},{6,5},{7,6},{0,7},{9,8},{10,9},{11,1... | collective-permute-start | bytes 2654216 | tf_op jit(solution)/shard_map/ppermute | solution.py:423
  67.9 2.8 %shard_map.122 = (f32[7,8,3072]{2,1,0:T(8,128)}, f32[7,8,3072]{2,1,0:T(8,128)}) custom-call(f32[16,8,4096]{2,1,0:T(8,128)S(1)} %copy-done), custom_call_target="tpu_custom_call" | custom-call | bytes 2293760 | tf_op jit(solution)/shard_map/pallas_call | solution.py:84
  71.4 2.5 %collective-permute-start.27 = (f32[1,8,4096]{2,1,0:T(8,128)S(1)}, f32[1,8,4096]{2,1,0:T(8,128)S(1)}, u32[]{:S(2)}, u32[]{:S(2)}) collective-permute-start(f32[1,8,4096]{2,1,0:T(8,128)S(1)} %broadcast_select_fusion.refs_1_.rest_1_), channel_id=1, source_target_pairs={{0,112},{8,120},{16,0},{24,8},{32,16},{40,24},{48,32},{56,40},{64,... | collective-permute-start | bytes 393224 | tf_op jit(solution)/shard_map/ppermute | solution.py:465
  73.9 44.4 %collective-permute-done.22 = f32[1,8,4096]{2,1,0:T(8,128)S(1)} collective-permute-done((f32[1,8,4096]{2,1,0:T(8,128)S(1)}, f32[1,8,4096]{2,1,0:T(8,128)S(1)}, u32[]{:S(2)}, u32[]{:S(2)}) %collective-permute-start.22) | collective-permute-done | bytes 131104 | tf_op jit(solution)/shard_map/ppermute | solution.py:456
  118.5 1.6 collective-permute-start.26
  125.3 2.7 %collective-permute-start.29 = (f32[1,8,4096]{2,1,0:T(8,128)S(1)}, f32[1,8,4096]{2,1,0:T(8,128)S(1)}, u32[]{:S(2)}, u32[]{:S(2)}) collective-permute-start(f32[1,8,4096]{2,1,0:T(8,128)S(1)} %collective-permute-done.25.refs_3_.rest_3_), channel_id=1, source_target_pairs={{0,112},{8,120},{16,0},{24,8},{32,16},{40,24},{48,32},{56,40},{64,... | collective-permute-start | bytes 393224 | tf_op jit(solution)/shard_map/ppermute | solution.py:465
  129.5 2.2 %collective-permute-done.30.refs_2_.rest_8_ = f32[1,8,4096]{2,1,0:T(8,128)S(1)} collective-permute-done((f32[1,8,4096]{2,1,0:T(8,128)S(1)}, f32[1,8,4096]{2,1,0:T(8,128)S(1)}, u32[]{:S(2)}, u32[]{:S(2)}) %collective-permute-start.30) | collective-permute-done | bytes 131104 | tf_op jit(solution)/shard_map/ppermute | solution.py:465
  131.7 2.7 %collective-permute-start.33 = (f32[1,8,4096]{2,1,0:T(8,128)S(1)}, f32[1,8,4096]{2,1,0:T(8,128)S(1)}, u32[]{:S(2)}, u32[]{:S(2)}) collective-permute-start(f32[1,8,4096]{2,1,0:T(8,128)S(1)} %collective-permute-done.29.refs_1_.rest_7_), channel_id=1, source_target_pairs={{0,112},{8,120},{16,0},{24,8},{32,16},{40,24},{48,32},{56,40},{64,... | collective-permute-start | bytes 393224 | tf_op jit(solution)/shard_map/ppermute | solution.py:465
  135.3 9.6 %collective-permute-start.38 = (f32[6,8,4096]{2,1,0:T(8,128)}, f32[6,8,4096]{2,1,0:T(8,128)S(1)}, u32[]{:S(2)}, u32[]{:S(2)}) collective-permute-start(f32[6,8,4096]{2,1,0:T(8,128)} %shard_map.136), channel_id=1, source_target_pairs={{0,8},{8,0},{16,24},{24,16},{32,40},{40,32},{48,56},{56,48},{64,72... | collective-permute-start | bytes 2359304 | tf_op jit(solution)/shard_map/ppermute | solution.py:473
  144.9 3.9 %collective-permute-start.1 = (f32[7,8,3072]{2,1,0:T(8,128)}, f32[7,8,3072]{2,1,0:T(8,128)}, u32[]{:S(2)}, u32[]{:S(2)}) collective-permute-start(f32[7,8,3072]{2,1,0:T(8,128)} %get-tuple-element.26), channel_id=1, source_target_pairs={{1,0},{2,1},{3,2},{4,3},{5,4},{6,5},{7,6},{0,7},{9,8},{10,9},{11,1... | collective-permute-start | bytes 2064392 | tf_op jit(solution)/shard_map/ppermute | solution.py:423
  153.0 1.9 %collective-permute-start.39 = (f32[4,8,4096]{2,1,0:T(8,128)}, f32[4,8,4096]{2,1,0:T(8,128)}, u32[]{:S(2)}, u32[]{:S(2)}) collective-permute-start(f32[4,8,4096]{2,1,0:T(8,128)} %shard_map.137), channel_id=1, source_target_pairs={{0,8},{8,0},{16,24},{24,16},{32,40},{40,32},{48,56},{56,48},{64,72... | collective-permute-start | bytes 1572872 | tf_op jit(solution)/shard_map/ppermute | solution.py:473
  160.7 4.7 %shard_map.124.rest_0_ = f32[16,8,4096]{2,1,0:T(8,128)} custom-call(f32[16,8,4096]{2,1,0:T(8,128)S(1)} %copy-done, f32[9,8,3072]{2,1,0:T(8,128)} %collective-permute-done.2.low, f32[9,8,3072]{2,1,0:T(8,128)} %collective-permute-done.3.high, f32[16,8,4096]{2,1,0:T(8,128)S(1)} %copy-done.2, f32[8,4096]{1,0:T(8,128)S(1)} %copy-done.3, f32[128,128]{1,0:T(8,128)S(1)} %copy-done.5), custom_call_target="tpu_custom_call" | custom-call | flops 471859200 | bytes 5603328 | tf_op jit(solution)/shard_map/pallas_call | solution.py:180
  165.5 6.0 %shard_map.125 = f32[16,8,4096]{2,1,0:T(8,128)} custom-call(f32[16,8,4096]{2,1,0:T(8,128)S(1)} %copy-done, f32[7,8,3072]{2,1,0:T(8,128)} %collective-permute-done.low, f32[7,8,3072]{2,1,0:T(8,128)} %collective-permute-done.1.high, f32[16,8,4096]{2,1,0:T(8,128)S(1)} %copy-done.2, f32[8,4096]{1,0:T(8,128)S(1)} %copy-done.3, ...), custom_call_target="tpu_custom_call", output_to_operand_aliasing={{}: (6, {})} | custom-call | flops 367001600 | bytes 4358144 | tf_op jit(solution)/shard_map/pallas_call | solution.py:180
  171.7 4.5 %shard_map.141 = f32[16,8,4096]{2,1,0:T(8,128)} custom-call(f32[16,8,4096]{2,1,0:T(8,128)S(1)} %copy-done.4, f32[1,8,4096]{2,1,0:T(8,128)S(1)} %broadcast_select_fusion.1.refs_0_.rest_0_, f32[1,8,4096]{2,1,0:T(8,128)S(1)} %broadcast_select_fusion.refs_1_.rest_1_, f32[1,8,4096]{2,1,0:T(8,128)S(1)} %copy-done.7, f32[1,8,4096]{2,1,0:T(8,128)S(1)} %copy-done.11, ...), custom_call_target="tpu_custom_call" | custom-call | flops 805306368 | bytes 8388608 | tf_op jit(solution)/shard_map/pallas_call | solution.py:265
  (147 shorter events, 32.2 us)
Async XLA Ops:
  5.5 9.9 %collective-permute-start.4 = (f32[1,8,4096]{2,1,0:T(8,128)}, f32[1,8,4096]{2,1,0:T(8,128)S(1)}, u32[]{:S(2)}, u32[]{:S(2)}) collective-permute-start(f32[1,8,4096]{2,1,0:T(8,128)} %get-tuple-element.29), channel_id=1, source_target_pairs={{0,16},{8,24},{16,32},{24,40},{32,48},{40,56},{48,64},{56,72},{64,... | collective-permute-start | bytes 393224 | tf_op jit(solution)/shard_map/ppermute | solution.py:411
  8.0 7.4 %collective-permute-start.5 = (f32[1,8,4096]{2,1,0:T(8,128)}, f32[1,8,4096]{2,1,0:T(8,128)S(1)}, u32[]{:S(2)}, u32[]{:S(2)}) collective-permute-start(f32[1,8,4096]{2,1,0:T(8,128)} %get-tuple-element.30), channel_id=1, source_target_pairs={{0,112},{8,120},{16,0},{24,8},{32,16},{40,24},{48,32},{56,40},{64,... | collective-permute-start | bytes 393224 | tf_op jit(solution)/shard_map/ppermute | solution.py:412
  16.0 14.1 %collective-permute-start.6 = (f32[2,8,4096]{2,1,0:T(8,128)S(1)}, f32[2,8,4096]{2,1,0:T(8,128)S(1)}, u32[]{:S(2)}, u32[]{:S(2)}) collective-permute-start(f32[2,8,4096]{2,1,0:T(8,128)S(1)} %get-tuple-element.31), channel_id=1, source_target_pairs={{0,16},{8,24},{16,32},{24,40},{32,48},{40,56},{48,64},{56,72},{64,... | collective-permute-start | bytes 786440 | tf_op jit(solution)/shard_map/ppermute | solution.py:415
  16.0 14.0 %collective-permute-start.7 = (f32[2,8,4096]{2,1,0:T(8,128)S(1)}, f32[2,8,4096]{2,1,0:T(8,128)S(1)}, u32[]{:S(2)}, u32[]{:S(2)}) collective-permute-start(f32[2,8,4096]{2,1,0:T(8,128)S(1)} %get-tuple-element.32), channel_id=1, source_target_pairs={{0,112},{8,120},{16,0},{24,8},{32,16},{40,24},{48,32},{56,40},{64,... | collective-permute-start | bytes 786440 | tf_op jit(solution)/shard_map/ppermute | solution.py:416
  18.7 7.9 %collective-permute-start.14 = (f32[1,8,4096]{2,1,0:T(8,128)S(1)}, f32[1,8,4096]{2,1,0:T(8,128)S(1)}, u32[]{:S(2)}, u32[]{:S(2)}) collective-permute-start(f32[1,8,4096]{2,1,0:T(8,128)S(1)} %get-tuple-element.49), channel_id=1, source_target_pairs={{0,16},{8,24},{16,32},{24,40},{32,48},{40,56},{48,64},{56,72},{64,... | collective-permute-start | bytes 393224 | tf_op jit(solution)/shard_map/ppermute | solution.py:411
  18.8 7.8 %collective-permute-start.15 = (f32[1,8,4096]{2,1,0:T(8,128)S(1)}, f32[1,8,4096]{2,1,0:T(8,128)S(1)}, u32[]{:S(2)}, u32[]{:S(2)}) collective-permute-start(f32[1,8,4096]{2,1,0:T(8,128)S(1)} %get-tuple-element.48), channel_id=1, source_target_pairs={{0,112},{8,120},{16,0},{24,8},{32,16},{40,24},{48,32},{56,40},{64,... | collective-permute-start | bytes 393224 | tf_op jit(solution)/shard_map/ppermute | solution.py:412
  27.3 7.0 %collective-permute-start.16 = (f32[2,8,4096]{2,1,0:T(8,128)S(1)}, f32[2,8,4096]{2,1,0:T(8,128)S(1)}, u32[]{:S(2)}, u32[]{:S(2)}) collective-permute-start(f32[2,8,4096]{2,1,0:T(8,128)S(1)} %get-tuple-element.40), channel_id=1, source_target_pairs={{0,16},{8,24},{16,32},{24,40},{32,48},{40,56},{48,64},{56,72},{64,... | collective-permute-start | bytes 786440 | tf_op jit(solution)/shard_map/ppermute | solution.py:415
  30.6 9.6 %collective-permute-start.8 = (f32[2,8,4096]{2,1,0:T(8,128)S(1)}, f32[2,8,4096]{2,1,0:T(8,128)S(1)}, u32[]{:S(2)}, u32[]{:S(2)}) collective-permute-start(f32[2,8,4096]{2,1,0:T(8,128)S(1)} %get-tuple-element.33), channel_id=1, source_target_pairs={{0,16},{8,24},{16,32},{24,40},{32,48},{40,56},{48,64},{56,72},{64,... | collective-permute-start | bytes 786440 | tf_op jit(solution)/shard_map/ppermute | solution.py:415
  30.7 9.5 %collective-permute-start.9 = (f32[2,8,4096]{2,1,0:T(8,128)S(1)}, f32[2,8,4096]{2,1,0:T(8,128)S(1)}, u32[]{:S(2)}, u32[]{:S(2)}) collective-permute-start(f32[2,8,4096]{2,1,0:T(8,128)S(1)} %get-tuple-element.34), channel_id=1, source_target_pairs={{0,112},{8,120},{16,0},{24,8},{32,16},{40,24},{48,32},{56,40},{64,... | collective-permute-start | bytes 786440 | tf_op jit(solution)/shard_map/ppermute | solution.py:416
  34.9 10.8 %collective-permute-start.18 = (f32[2,8,4096]{2,1,0:T(8,128)S(1)}, f32[2,8,4096]{2,1,0:T(8,128)S(1)}, u32[]{:S(2)}, u32[]{:S(2)}) collective-permute-start(f32[2,8,4096]{2,1,0:T(8,128)S(1)} %get-tuple-element.42), channel_id=1, source_target_pairs={{0,16},{8,24},{16,32},{24,40},{32,48},{40,56},{48,64},{56,72},{64,... | collective-permute-start | bytes 786440 | tf_op jit(solution)/shard_map/ppermute | solution.py:415
  36.1 9.6 %collective-permute-start.19 = (f32[2,8,4096]{2,1,0:T(8,128)S(1)}, f32[2,8,4096]{2,1,0:T(8,128)S(1)}, u32[]{:S(2)}, u32[]{:S(2)}) collective-permute-start(f32[2,8,4096]{2,1,0:T(8,128)S(1)} %get-tuple-element.43), channel_id=1, source_target_pairs={{0,112},{8,120},{16,0},{24,8},{32,16},{40,24},{48,32},{56,40},{64,... | collective-permute-start | bytes 786440 | tf_op jit(solution)/shard_map/ppermute | solution.py:416
  40.9 10.5 %collective-permute-start.10 = (f32[2,8,4096]{2,1,0:T(8,128)S(1)}, f32[2,8,4096]{2,1,0:T(8,128)S(1)}, u32[]{:S(2)}, u32[]{:S(2)}) collective-permute-start(f32[2,8,4096]{2,1,0:T(8,128)S(1)} %get-tuple-element.35), channel_id=1, source_target_pairs={{0,16},{8,24},{16,32},{24,40},{32,48},{40,56},{48,64},{56,72},{64,... | collective-permute-start | bytes 786440 | tf_op jit(solution)/shard_map/ppermute | solution.py:415
  41.4 9.9 %collective-permute-start.11 = (f32[2,8,4096]{2,1,0:T(8,128)S(1)}, f32[2,8,4096]{2,1,0:T(8,128)S(1)}, u32[]{:S(2)}, u32[]{:S(2)}) collective-permute-start(f32[2,8,4096]{2,1,0:T(8,128)S(1)} %get-tuple-element.36), channel_id=1, source_target_pairs={{0,112},{8,120},{16,0},{24,8},{32,16},{40,24},{48,32},{56,40},{64,... | collective-permute-start | bytes 786440 | tf_op jit(solution)/shard_map/ppermute | solution.py:416
  46.3 11.0 %collective-permute-start.20 = (f32[2,8,4096]{2,1,0:T(8,128)S(1)}, f32[2,8,4096]{2,1,0:T(8,128)S(1)}, u32[]{:S(2)}, u32[]{:S(2)}) collective-permute-start(f32[2,8,4096]{2,1,0:T(8,128)S(1)} %get-tuple-element.44), channel_id=1, source_target_pairs={{0,16},{8,24},{16,32},{24,40},{32,48},{40,56},{48,64},{56,72},{64,... | collective-permute-start | bytes 786440 | tf_op jit(solution)/shard_map/ppermute | solution.py:415
  47.0 10.3 %collective-permute-start.21 = (f32[2,8,4096]{2,1,0:T(8,128)S(1)}, f32[2,8,4096]{2,1,0:T(8,128)S(1)}, u32[]{:S(2)}, u32[]{:S(2)}) collective-permute-start(f32[2,8,4096]{2,1,0:T(8,128)S(1)} %get-tuple-element.45), channel_id=1, source_target_pairs={{0,112},{8,120},{16,0},{24,8},{32,16},{40,24},{48,32},{56,40},{64,... | collective-permute-start | bytes 786440 | tf_op jit(solution)/shard_map/ppermute | solution.py:416
  52.0 8.3 %collective-permute-start.12 = (f32[2,8,3072]{2,1,0:T(8,128)S(1)}, f32[2,8,3072]{2,1,0:T(8,128)S(1)}, u32[]{:S(2)}, u32[]{:S(2)}) collective-permute-start(f32[2,8,3072]{2,1,0:T(8,128)S(1)} %get-tuple-element.38), channel_id=1, source_target_pairs={{0,1},{1,2},{2,3},{3,4},{4,5},{5,6},{6,7},{7,0},{8,9},{9,10},{10,1... | collective-permute-start | bytes 589832 | tf_op jit(solution)/shard_map/ppermute | solution.py:422
  61.5 9.9 %collective-permute-start.23 = (f32[1,8,4096]{2,1,0:T(8,128)S(1)}, f32[1,8,4096]{2,1,0:T(8,128)S(1)}, u32[]{:S(2)}, u32[]{:S(2)}) collective-permute-start(f32[1,8,4096]{2,1,0:T(8,128)S(1)} %shard_map.135), channel_id=1, source_target_pairs={{0,128},{8,136},{16,144},{24,152},{32,160},{40,168},{48,176},{56,1... | collective-permute-start | bytes 393224 | tf_op jit(solution)/shard_map/ppermute | solution.py:456
  62.8 57.3 %collective-permute-start.2 = (f32[9,8,3072]{2,1,0:T(8,128)}, f32[9,8,3072]{2,1,0:T(8,128)}, u32[]{:S(2)}, u32[]{:S(2)}) collective-permute-start(f32[9,8,3072]{2,1,0:T(8,128)} %get-tuple-element.27), channel_id=1, source_target_pairs={{0,1},{1,2},{2,3},{3,4},{4,5},{5,6},{6,7},{7,0},{8,9},{9,10},{10,1... | collective-permute-start | bytes 2654216 | tf_op jit(solution)/shard_map/ppermute | solution.py:422
  65.2 92.9 %collective-permute-start.3 = (f32[9,8,3072]{2,1,0:T(8,128)}, f32[9,8,3072]{2,1,0:T(8,128)}, u32[]{:S(2)}, u32[]{:S(2)}) collective-permute-start(f32[9,8,3072]{2,1,0:T(8,128)} %get-tuple-element.28), channel_id=1, source_target_pairs={{1,0},{2,1},{3,2},{4,3},{5,4},{6,5},{7,6},{0,7},{9,8},{10,9},{11,1... | collective-permute-start | bytes 2654216 | tf_op jit(solution)/shard_map/ppermute | solution.py:423
  70.7 47.8 %collective-permute-start = (f32[7,8,3072]{2,1,0:T(8,128)}, f32[7,8,3072]{2,1,0:T(8,128)}, u32[]{:S(2)}, u32[]{:S(2)}) collective-permute-start(f32[7,8,3072]{2,1,0:T(8,128)} %get-tuple-element.25), channel_id=1, source_target_pairs={{0,1},{1,2},{2,3},{3,4},{4,5},{5,6},{6,7},{7,0},{8,9},{9,10},{10,1... | collective-permute-start | bytes 2064392 | tf_op jit(solution)/shard_map/ppermute | solution.py:422
  71.3 47.1 %collective-permute-start.22 = (f32[1,8,4096]{2,1,0:T(8,128)S(1)}, f32[1,8,4096]{2,1,0:T(8,128)S(1)}, u32[]{:S(2)}, u32[]{:S(2)}) collective-permute-start(f32[1,8,4096]{2,1,0:T(8,128)S(1)} %shard_map.134), channel_id=1, source_target_pairs={{0,128},{8,136},{16,144},{24,152},{32,160},{40,168},{48,176},{56,1... | collective-permute-start | bytes 393224 | tf_op jit(solution)/shard_map/ppermute | solution.py:456
  71.4 49.8 %collective-permute-start.27 = (f32[1,8,4096]{2,1,0:T(8,128)S(1)}, f32[1,8,4096]{2,1,0:T(8,128)S(1)}, u32[]{:S(2)}, u32[]{:S(2)}) collective-permute-start(f32[1,8,4096]{2,1,0:T(8,128)S(1)} %broadcast_select_fusion.refs_1_.rest_1_), channel_id=1, source_target_pairs={{0,112},{8,120},{16,0},{24,8},{32,16},{40,24},{48,32},{56,40},{64,... | collective-permute-start | bytes 393224 | tf_op jit(solution)/shard_map/ppermute | solution.py:465
  118.5 6.8 %collective-permute-start.26 = (f32[1,8,4096]{2,1,0:T(8,128)S(1)}, f32[1,8,4096]{2,1,0:T(8,128)S(1)}, u32[]{:S(2)}, u32[]{:S(2)}) collective-permute-start(f32[1,8,4096]{2,1,0:T(8,128)S(1)} %broadcast_select_fusion.refs_1_.rest_1_), channel_id=1, source_target_pairs={{0,16},{8,24},{16,32},{24,40},{32,48},{40,56},{48,64},{56,72},{64,... | collective-permute-start | bytes 393224 | tf_op jit(solution)/shard_map/ppermute | solution.py:465
  128.0 7.3 %collective-permute-start.35 = (f32[1,8,4096]{2,1,0:T(8,128)S(1)}, f32[1,8,4096]{2,1,0:T(8,128)S(1)}, u32[]{:S(2)}, u32[]{:S(2)}) collective-permute-start(f32[1,8,4096]{2,1,0:T(8,128)S(1)} %collective-permute-done.31.refs_3_.rest_9_), channel_id=1, source_target_pairs={{0,112},{8,120},{16,0},{24,8},{32,16},{40,24},{48,32},{56,40},{64,... | collective-permute-start | bytes 393224 | tf_op jit(solution)/shard_map/ppermute | solution.py:465
  128.9 16.0 %collective-permute-start.32 = (f32[1,8,4096]{2,1,0:T(8,128)S(1)}, f32[1,8,4096]{2,1,0:T(8,128)S(1)}, u32[]{:S(2)}, u32[]{:S(2)}) collective-permute-start(f32[1,8,4096]{2,1,0:T(8,128)S(1)} %collective-permute-done.28.refs_0_.rest_6_), channel_id=1, source_target_pairs={{0,16},{8,24},{16,32},{24,40},{32,48},{40,56},{48,64},{56,72},{64,... | collective-permute-start | bytes 393224 | tf_op jit(solution)/shard_map/ppermute | solution.py:465
  131.7 17.1 %collective-permute-start.34 = (f32[1,8,4096]{2,1,0:T(8,128)S(1)}, f32[1,8,4096]{2,1,0:T(8,128)S(1)}, u32[]{:S(2)}, u32[]{:S(2)}) collective-permute-start(f32[1,8,4096]{2,1,0:T(8,128)S(1)} %collective-permute-done.30.refs_2_.rest_8_), channel_id=1, source_target_pairs={{0,16},{8,24},{16,32},{24,40},{32,48},{40,56},{48,64},{56,72},{64,... | collective-permute-start | bytes 393224 | tf_op jit(solution)/shard_map/ppermute | solution.py:465
  131.7 17.9 %collective-permute-start.33 = (f32[1,8,4096]{2,1,0:T(8,128)S(1)}, f32[1,8,4096]{2,1,0:T(8,128)S(1)}, u32[]{:S(2)}, u32[]{:S(2)}) collective-permute-start(f32[1,8,4096]{2,1,0:T(8,128)S(1)} %collective-permute-done.29.refs_1_.rest_7_), channel_id=1, source_target_pairs={{0,112},{8,120},{16,0},{24,8},{32,16},{40,24},{48,32},{56,40},{64,... | collective-permute-start | bytes 393224 | tf_op jit(solution)/shard_map/ppermute | solution.py:465
  135.3 36.2 %collective-permute-start.38 = (f32[6,8,4096]{2,1,0:T(8,128)}, f32[6,8,4096]{2,1,0:T(8,128)S(1)}, u32[]{:S(2)}, u32[]{:S(2)}) collective-permute-start(f32[6,8,4096]{2,1,0:T(8,128)} %shard_map.136), channel_id=1, source_target_pairs={{0,8},{8,0},{16,24},{24,16},{32,40},{40,32},{48,56},{56,48},{64,72... | collective-permute-start | bytes 2359304 | tf_op jit(solution)/shard_map/ppermute | solution.py:473
  144.9 20.6 %collective-permute-start.1 = (f32[7,8,3072]{2,1,0:T(8,128)}, f32[7,8,3072]{2,1,0:T(8,128)}, u32[]{:S(2)}, u32[]{:S(2)}) collective-permute-start(f32[7,8,3072]{2,1,0:T(8,128)} %get-tuple-element.26), channel_id=1, source_target_pairs={{1,0},{2,1},{3,2},{4,3},{5,4},{6,5},{7,6},{0,7},{9,8},{10,9},{11,1... | collective-permute-start | bytes 2064392 | tf_op jit(solution)/shard_map/ppermute | solution.py:423
  153.0 18.5 %collective-permute-start.39 = (f32[4,8,4096]{2,1,0:T(8,128)}, f32[4,8,4096]{2,1,0:T(8,128)}, u32[]{:S(2)}, u32[]{:S(2)}) collective-permute-start(f32[4,8,4096]{2,1,0:T(8,128)} %shard_map.137), channel_id=1, source_target_pairs={{0,8},{8,0},{16,24},{24,16},{32,40},{40,32},{48,56},{56,48},{64,72... | collective-permute-start | bytes 1572872 | tf_op jit(solution)/shard_map/ppermute | solution.py:473
  155.3 16.1 %collective-permute-start.40 = (f32[4,8,4096]{2,1,0:T(8,128)}, f32[4,8,4096]{2,1,0:T(8,128)}, u32[]{:S(2)}, u32[]{:S(2)}) collective-permute-start(f32[4,8,4096]{2,1,0:T(8,128)} %shard_map.138), channel_id=1, source_target_pairs={{0,8},{8,0},{16,24},{24,16},{32,40},{40,32},{48,56},{56,48},{64,72... | collective-permute-start | bytes 1572872 | tf_op jit(solution)/shard_map/ppermute | solution.py:473
  158.1 13.3 %collective-permute-start.41 = (f32[2,8,4096]{2,1,0:T(8,128)}, f32[2,8,4096]{2,1,0:T(8,128)}, u32[]{:S(2)}, u32[]{:S(2)}) collective-permute-start(f32[2,8,4096]{2,1,0:T(8,128)} %shard_map.139), channel_id=1, source_target_pairs={{0,8},{8,0},{16,24},{24,16},{32,40},{40,32},{48,56},{56,48},{64,72... | collective-permute-start | bytes 786440 | tf_op jit(solution)/shard_map/ppermute | solution.py:473
  (45 other events, 471.6 us)

commit v5 on v4

--- a/solution.py
+++ b/solution.py
@@ -291,43 +291,26 @@
 PARTNER = everywhere(lambda x, z, c: (x, z, 1 - c))
 
 
-def open_body(place, orb, head, tail, first, second, held, hand, sems):
-    share, half = hand.shape[0], first.shape[0]
+def open_body(place, orb, head, tail, first, second):
+    share = orb.shape[0] // RING
     start = ((place[0] + RING // 2) & (RING - 1)) * share
-    step = split(held.shape[0])
-    copies = [pltpu.make_async_copy(orb.at[pl.ds(start, share)], hand, sems.at[0])]
-    for i in range(0, held.shape[0], step):
-        part = pl.ds(i, step)
-        copies.append(pltpu.make_async_copy(orb.at[part], held.at[part], sems.at[len(copies)]))
-    for copy in copies:
-        copy.start()
-    copies[0].wait()
-    first[...] = hand[:half]
-    second[...] = hand[half:]
-    for i, copy in enumerate(copies[1:]):
-        copy.wait()
-
-        @pl.loop(i * step, i * step + step)
-        def _(m):
-            pack_one(m, held, head, tail)
+    for m in range(first.shape[0]):
+        first[m] = orb[start + m]
+        second[m] = orb[start + first.shape[0] + m]
+    pack_body(orb, head, tail)
 
 
 def opening(orb, place, early):
     n, planes, cells = orb.shape
-    share = n // RING
-    shapes = [(early, planes, cells * WIDTH // planes)] * 2 + [(share // 2, planes, cells)] * 2
+    half = n // RING // 2
+    shapes = [(early, planes, cells * WIDTH // planes)] * 2 + [(half, planes, cells)] * 2
     still = pl.BlockSpec(memory_space=pltpu.VMEM)
     return pl.pallas_call(
         open_body,
-        in_specs=[pl.BlockSpec(memory_space=pltpu.SMEM), pl.BlockSpec(memory_space=pltpu.HBM)],
+        in_specs=[pl.BlockSpec(memory_space=pltpu.SMEM), still],
         out_specs=[still] * 4,
         out_shape=[jax.ShapeDtypeStruct(shape, jnp.float32) for shape in shapes],
-        scratch_shapes=[
-            pltpu.VMEM((early, planes, cells), jnp.float32),
-            pltpu.VMEM((share, planes, cells), jnp.float32),
-            pltpu.SemaphoreType.DMA((early // split(early) + 1,)),
-        ],
-        compiler_params=room(60),
+        compiler_params=room(12),
         cost_estimate=pl.CostEstimate(flops=0, bytes_accessed=8 * n * planes * cells, transcendentals=0),
     )(place, orb)
 
@@ -434,9 +417,9 @@
 
     offset = (z - root_z) & (RING - 1)
 
-    early = count * 9 // 16
+    early = count * 5 // 8
     place = jnp.stack([z, offset])
-    *ends, first, second = opening(orbitals, place, early)
+    *ends, first, second = opening(orbitals, z[None], early)
     sides_early = halo(*ends)
     ends = pack(orbitals, early, count - early)
     sides_late = halo(*ends)

time: 177 us -> 175 us (0.989)
  Pallas kernels: 30.7 us -> 26 us
  local copies, waits for them, and re-layouts: 2.4 us -> 4.62 us
    ppermute x2, waiting for transfers between devices: 44.4 us -> 47.3 us  [step(): other = lax.ppermute(mine, 'band', ACROSS)]
    unnamed x70, local copies, waits for them, and re-layouts: 2.39 us -> 4.6 us
    pallas_call x1, Pallas kernels: 3.4 us -> 1.44 us  [opening(): pl.pallas_call(open_body, in_specs=[pl.BlockSpec(memory_space=pltpu.SMEM)...]
  transfers between devices with their start and end apart: 42 -> 42, of which waited for: 15 -> 15; matrix products, arithmetic and copies ran while one was open for 0% -> 0% of each run, Pallas kernels for 12% -> 11%
where the time goes in v5:
time: 175 us; the launch traced here: 174 us
  waiting for transfers between devices  72.4 us (41%)
  starting transfers between devices  69.6 us (40%)
  Pallas kernels  26 us (15%)
  local copies, waits for them, and re-layouts  4.62 us (3%)
  between operations  1.78 us (1%)
    ppermute x2, waiting for transfers between devices, step(): other = lax.ppermute(mine, 'band', ACROSS)  47.3 us
    ppermute x14, starting transfers between devices, step(): chain[way] = lax.ppermute(chain[way], 'band', pairs)  14.3 us
    ppermute x6, starting transfers between devices, relay(): down = lax.ppermute(down, 'band', BACK)  13.5 us
    ppermute x4, starting transfers between devices, step(): theirs.append(lax.ppermute(group, 'band', PARTNER))  13.4 us
    pallas_call x4, Pallas kernels, apply_filter(): pl.pallas_call(filter_body, grid=(n // step,), in_specs=specs, out_specs=...  9.57 us
    ppermute x3, starting transfers between devices, halo(): lax.ppermute(head, 'domain', [((i + 1) % size, i) for i in range(size)])  9.05 us
    ppermute x6, waiting for transfers between devices, relay(): up = lax.ppermute(up, 'band', ONWARD)  7.7 us
    ppermute x2, waiting for transfers between devices, relay(): up = lax.ppermute(opposite[0], 'band', ONWARD)  7.64 us
  transfers between devices with their start and end apart: 42, of which 15 were waited for; matrix products, arithmetic and copies ran while one was open for 0% of the time, Pallas kernels for 11%

profile of v5, /device:TPU:1, one launch (start us, length us, event | category | flops | bytes accessed | tf_op | source)
XLA Modules:
  0.0 174.5 jit_solution(18210315251916080165)
XLA Ops:
  0.6 1.6 copy-done
  3.7 2.5 %collective-permute-start.4 = (f32[1,8,4096]{2,1,0:T(8,128)S(1)}, f32[1,8,4096]{2,1,0:T(8,128)S(1)}, u32[]{:S(2)}, u32[]{:S(2)}) collective-permute-start(f32[1,8,4096]{2,1,0:T(8,128)S(1)} %get-tuple-element.29), channel_id=1, source_target_pairs={{0,16},{8,24},{16,32},{24,40},{32,48},{40,56},{48,64},{56,72},{64,... | collective-permute-start | bytes 393224 | tf_op jit(solution)/shard_map/ppermute | solution.py:394
  6.1 3.9 %collective-permute-start.5 = (f32[1,8,4096]{2,1,0:T(8,128)S(1)}, f32[1,8,4096]{2,1,0:T(8,128)S(1)}, u32[]{:S(2)}, u32[]{:S(2)}) collective-permute-start(f32[1,8,4096]{2,1,0:T(8,128)S(1)} %get-tuple-element.30), channel_id=1, source_target_pairs={{0,112},{8,120},{16,0},{24,8},{32,16},{40,24},{48,32},{56,40},{64,... | collective-permute-start | bytes 393224 | tf_op jit(solution)/shard_map/ppermute | solution.py:395
  10.8 2.5 %collective-permute-done.4.up = f32[1,8,4096]{2,1,0:T(8,128)S(1)} collective-permute-done((f32[1,8,4096]{2,1,0:T(8,128)S(1)}, f32[1,8,4096]{2,1,0:T(8,128)S(1)}, u32[]{:S(2)}, u32[]{:S(2)}) %collective-permute-start.4) | collective-permute-done | bytes 131104 | tf_op jit(solution)/shard_map/ppermute | solution.py:394
  14.0 2.7 %collective-permute-start.7 = (f32[2,8,4096]{2,1,0:T(8,128)S(1)}, f32[2,8,4096]{2,1,0:T(8,128)S(1)}, u32[]{:S(2)}, u32[]{:S(2)}) collective-permute-start(f32[2,8,4096]{2,1,0:T(8,128)S(1)} %get-tuple-element.32), channel_id=1, source_target_pairs={{0,112},{8,120},{16,0},{24,8},{32,16},{40,24},{48,32},{56,40},{64,... | collective-permute-start | bytes 786440 | tf_op jit(solution)/shard_map/ppermute | solution.py:399
  16.7 2.7 %collective-permute-start.15 = (f32[1,8,4096]{2,1,0:T(8,128)S(1)}, f32[1,8,4096]{2,1,0:T(8,128)S(1)}, u32[]{:S(2)}, u32[]{:S(2)}) collective-permute-start(f32[1,8,4096]{2,1,0:T(8,128)S(1)} %get-tuple-element.48), channel_id=1, source_target_pairs={{0,112},{8,120},{16,0},{24,8},{32,16},{40,24},{48,32},{56,40},{64,... | collective-permute-start | bytes 393224 | tf_op jit(solution)/shard_map/ppermute | solution.py:395
  19.4 5.2 %collective-permute-done.14.up = f32[1,8,4096]{2,1,0:T(8,128)S(1)} collective-permute-done((f32[1,8,4096]{2,1,0:T(8,128)S(1)}, f32[1,8,4096]{2,1,0:T(8,128)S(1)}, u32[]{:S(2)}, u32[]{:S(2)}) %collective-permute-start.14) | collective-permute-done | bytes 131104 | tf_op jit(solution)/shard_map/ppermute | solution.py:394
  25.7 2.2 %collective-permute-start.17 = (f32[2,8,4096]{2,1,0:T(8,128)S(1)}, f32[2,8,4096]{2,1,0:T(8,128)S(1)}, u32[]{:S(2)}, u32[]{:S(2)}) collective-permute-start(f32[2,8,4096]{2,1,0:T(8,128)S(1)} %get-tuple-element.41), channel_id=1, source_target_pairs={{0,112},{8,120},{16,0},{24,8},{32,16},{40,24},{48,32},{56,40},{64,... | collective-permute-start | bytes 786440 | tf_op jit(solution)/shard_map/ppermute | solution.py:399
  28.6 2.7 %collective-permute-start.9 = (f32[2,8,4096]{2,1,0:T(8,128)S(1)}, f32[2,8,4096]{2,1,0:T(8,128)S(1)}, u32[]{:S(2)}, u32[]{:S(2)}) collective-permute-start(f32[2,8,4096]{2,1,0:T(8,128)S(1)} %get-tuple-element.34), channel_id=1, source_target_pairs={{0,112},{8,120},{16,0},{24,8},{32,16},{40,24},{48,32},{56,40},{64,... | collective-permute-start | bytes 786440 | tf_op jit(solution)/shard_map/ppermute | solution.py:399
  34.0 1.6 collective-permute-start.19
  35.6 2.6 %collective-permute-done.8.up = f32[2,8,4096]{2,1,0:T(8,128)S(1)} collective-permute-done((f32[2,8,4096]{2,1,0:T(8,128)S(1)}, f32[2,8,4096]{2,1,0:T(8,128)S(1)}, u32[]{:S(2)}, u32[]{:S(2)}) %collective-permute-start.8) | collective-permute-done | bytes 262176 | tf_op jit(solution)/shard_map/ppermute | solution.py:398
  39.3 2.3 %collective-permute-start.11 = (f32[2,8,4096]{2,1,0:T(8,128)S(1)}, f32[2,8,4096]{2,1,0:T(8,128)S(1)}, u32[]{:S(2)}, u32[]{:S(2)}) collective-permute-start(f32[2,8,4096]{2,1,0:T(8,128)S(1)} %get-tuple-element.36), channel_id=1, source_target_pairs={{0,112},{8,120},{16,0},{24,8},{32,16},{40,24},{48,32},{56,40},{64,... | collective-permute-start | bytes 786440 | tf_op jit(solution)/shard_map/ppermute | solution.py:399
  41.6 2.0 %collective-permute-done.18.up = f32[2,8,4096]{2,1,0:T(8,128)S(1)} collective-permute-done((f32[2,8,4096]{2,1,0:T(8,128)S(1)}, f32[2,8,4096]{2,1,0:T(8,128)S(1)}, u32[]{:S(2)}, u32[]{:S(2)}) %collective-permute-start.18) | collective-permute-done | bytes 262176 | tf_op jit(solution)/shard_map/ppermute | solution.py:398
  44.9 2.1 %collective-permute-start.21 = (f32[2,8,4096]{2,1,0:T(8,128)S(1)}, f32[2,8,4096]{2,1,0:T(8,128)S(1)}, u32[]{:S(2)}, u32[]{:S(2)}) collective-permute-start(f32[2,8,4096]{2,1,0:T(8,128)S(1)} %get-tuple-element.45), channel_id=1, source_target_pairs={{0,112},{8,120},{16,0},{24,8},{32,16},{40,24},{48,32},{56,40},{64,... | collective-permute-start | bytes 786440 | tf_op jit(solution)/shard_map/ppermute | solution.py:399
  47.0 2.2 %collective-permute-done.10.up = f32[2,8,4096]{2,1,0:T(8,128)S(1)} collective-permute-done((f32[2,8,4096]{2,1,0:T(8,128)S(1)}, f32[2,8,4096]{2,1,0:T(8,128)S(1)}, u32[]{:S(2)}, u32[]{:S(2)}) %collective-permute-start.10) | collective-permute-done | bytes 262176 | tf_op jit(solution)/shard_map/ppermute | solution.py:398
  49.9 2.8 %collective-permute-start.12 = (f32[2,8,3072]{2,1,0:T(8,128)S(1)}, f32[2,8,3072]{2,1,0:T(8,128)S(1)}, u32[]{:S(2)}, u32[]{:S(2)}) collective-permute-start(f32[2,8,3072]{2,1,0:T(8,128)S(1)} %get-tuple-element.38), channel_id=1, source_target_pairs={{0,1},{1,2},{2,3},{3,4},{4,5},{5,6},{6,7},{7,0},{8,9},{9,10},{10,1... | collective-permute-start | bytes 589832 | tf_op jit(solution)/shard_map/ppermute | solution.py:405
  52.7 2.5 %collective-permute-start.13 = (f32[2,8,3072]{2,1,0:T(8,128)S(1)}, f32[2,8,3072]{2,1,0:T(8,128)S(1)}, u32[]{:S(2)}, u32[]{:S(2)}) collective-permute-start(f32[2,8,3072]{2,1,0:T(8,128)S(1)} %get-tuple-element.39), channel_id=1, source_target_pairs={{1,0},{2,1},{3,2},{4,3},{5,4},{6,5},{7,6},{0,7},{9,8},{10,9},{11,1... | collective-permute-start | bytes 589832 | tf_op jit(solution)/shard_map/ppermute | solution.py:406
  55.8 2.4 %collective-permute-done.12.low = f32[2,8,3072]{2,1,0:T(8,128)S(1)} collective-permute-done((f32[2,8,3072]{2,1,0:T(8,128)S(1)}, f32[2,8,3072]{2,1,0:T(8,128)S(1)}, u32[]{:S(2)}, u32[]{:S(2)}) %collective-permute-start.12) | collective-permute-done | bytes 196640 | tf_op jit(solution)/shard_map/ppermute | solution.py:405
  60.7 2.5 %collective-permute-start.2 = (f32[10,8,3072]{2,1,0:T(8,128)}, f32[10,8,3072]{2,1,0:T(8,128)}, u32[]{:S(2)}, u32[]{:S(2)}) collective-permute-start(f32[10,8,3072]{2,1,0:T(8,128)} %get-tuple-element.27), channel_id=1, source_target_pairs={{0,1},{1,2},{2,3},{3,4},{4,5},{5,6},{6,7},{7,0},{8,9},{9,10},{10,1... | collective-permute-start | bytes 2949128 | tf_op jit(solution)/shard_map/ppermute | solution.py:405
  63.1 2.6 %collective-permute-start.3 = (f32[10,8,3072]{2,1,0:T(8,128)}, f32[10,8,3072]{2,1,0:T(8,128)}, u32[]{:S(2)}, u32[]{:S(2)}) collective-permute-start(f32[10,8,3072]{2,1,0:T(8,128)} %get-tuple-element.28), channel_id=1, source_target_pairs={{1,0},{2,1},{3,2},{4,3},{5,4},{6,5},{7,6},{0,7},{9,8},{10,9},{11,1... | collective-permute-start | bytes 2949128 | tf_op jit(solution)/shard_map/ppermute | solution.py:406
  68.1 2.5 %collective-permute-start.27 = (f32[1,8,4096]{2,1,0:T(8,128)S(1)}, f32[1,8,4096]{2,1,0:T(8,128)S(1)}, u32[]{:S(2)}, u32[]{:S(2)}) collective-permute-start(f32[1,8,4096]{2,1,0:T(8,128)S(1)} %broadcast_select_fusion.refs_1_.rest_1_), channel_id=1, source_target_pairs={{0,112},{8,120},{16,0},{24,8},{32,16},{40,24},{48,32},{56,40},{64,... | collective-permute-start | bytes 393224 | tf_op jit(solution)/shard_map/ppermute | solution.py:448
  70.6 47.3 %collective-permute-done.22 = f32[1,8,4096]{2,1,0:T(8,128)S(1)} collective-permute-done((f32[1,8,4096]{2,1,0:T(8,128)S(1)}, f32[1,8,4096]{2,1,0:T(8,128)S(1)}, u32[]{:S(2)}, u32[]{:S(2)}) %collective-permute-start.22) | collective-permute-done | bytes 131104 | tf_op jit(solution)/shard_map/ppermute | solution.py:439
  118.2 2.0 %collective-permute-start.26 = (f32[1,8,4096]{2,1,0:T(8,128)S(1)}, f32[1,8,4096]{2,1,0:T(8,128)S(1)}, u32[]{:S(2)}, u32[]{:S(2)}) collective-permute-start(f32[1,8,4096]{2,1,0:T(8,128)S(1)} %broadcast_select_fusion.refs_1_.rest_1_), channel_id=1, source_target_pairs={{0,16},{8,24},{16,32},{24,40},{32,48},{40,56},{48,64},{56,72},{64,... | collective-permute-start | bytes 393224 | tf_op jit(solution)/shard_map/ppermute | solution.py:448
  125.4 2.1 %collective-permute-start.29 = (f32[1,8,4096]{2,1,0:T(8,128)S(1)}, f32[1,8,4096]{2,1,0:T(8,128)S(1)}, u32[]{:S(2)}, u32[]{:S(2)}) collective-permute-start(f32[1,8,4096]{2,1,0:T(8,128)S(1)} %collective-permute-done.25.refs_3_.rest_3_), channel_id=1, source_target_pairs={{0,112},{8,120},{16,0},{24,8},{32,16},{40,24},{48,32},{56,40},{64,... | collective-permute-start | bytes 393224 | tf_op jit(solution)/shard_map/ppermute | solution.py:448
  129.0 1.8 %collective-permute-done.30.refs_2_.rest_8_ = f32[1,8,4096]{2,1,0:T(8,128)S(1)} collective-permute-done((f32[1,8,4096]{2,1,0:T(8,128)S(1)}, f32[1,8,4096]{2,1,0:T(8,128)S(1)}, u32[]{:S(2)}, u32[]{:S(2)}) %collective-permute-start.30) | collective-permute-done | bytes 131104 | tf_op jit(solution)/shard_map/ppermute | solution.py:448
  131.8 9.4 %collective-permute-start.38 = (f32[6,8,4096]{2,1,0:T(8,128)}, f32[6,8,4096]{2,1,0:T(8,128)S(1)}, u32[]{:S(2)}, u32[]{:S(2)}) collective-permute-start(f32[6,8,4096]{2,1,0:T(8,128)} %shard_map.136), channel_id=1, source_target_pairs={{0,8},{8,0},{16,24},{24,16},{32,40},{40,32},{48,56},{56,48},{64,72... | collective-permute-start | bytes 2359304 | tf_op jit(solution)/shard_map/ppermute | solution.py:456
  141.2 3.0 %collective-permute-start.33 = (f32[1,8,4096]{2,1,0:T(8,128)S(1)}, f32[1,8,4096]{2,1,0:T(8,128)S(1)}, u32[]{:S(2)}, u32[]{:S(2)}) collective-permute-start(f32[1,8,4096]{2,1,0:T(8,128)S(1)} %collective-permute-done.29.refs_1_.rest_7_), channel_id=1, source_target_pairs={{0,112},{8,120},{16,0},{24,8},{32,16},{40,24},{48,32},{56,40},{64,... | collective-permute-start | bytes 393224 | tf_op jit(solution)/shard_map/ppermute | solution.py:448
  146.5 3.9 %collective-permute-start.1 = (f32[6,8,3072]{2,1,0:T(8,128)}, f32[6,8,3072]{2,1,0:T(8,128)}, u32[]{:S(2)}, u32[]{:S(2)}) collective-permute-start(f32[6,8,3072]{2,1,0:T(8,128)} %get-tuple-element.26), channel_id=1, source_target_pairs={{1,0},{2,1},{3,2},{4,3},{5,4},{6,5},{7,6},{0,7},{9,8},{10,9},{11,1... | collective-permute-start | bytes 1769480 | tf_op jit(solution)/shard_map/ppermute | solution.py:406
  152.7 3.4 %collective-permute-start.39 = (f32[4,8,4096]{2,1,0:T(8,128)}, f32[4,8,4096]{2,1,0:T(8,128)}, u32[]{:S(2)}, u32[]{:S(2)}) collective-permute-start(f32[4,8,4096]{2,1,0:T(8,128)} %shard_map.137), channel_id=1, source_target_pairs={{0,8},{8,0},{16,24},{24,16},{32,40},{40,32},{48,56},{56,48},{64,72... | collective-permute-start | bytes 1572872 | tf_op jit(solution)/shard_map/ppermute | solution.py:456
  160.6 4.9 %shard_map.124.rest_0_ = f32[16,8,4096]{2,1,0:T(8,128)} custom-call(f32[16,8,4096]{2,1,0:T(8,128)S(1)} %copy-done.1, f32[10,8,3072]{2,1,0:T(8,128)} %collective-permute-done.2.low, f32[10,8,3072]{2,1,0:T(8,128)} %collective-permute-done.3.high, f32[16,8,4096]{2,1,0:T(8,128)S(1)} %copy-done.3, f32[8,4096]{1,0:T(8,128)S(1)} %copy-done.4, f32[128,128]{1,0:T(8,128)S(1)} %copy-done.6), custom_call_target="tpu_custom_call" | custom-call | flops 524288000 | bytes 6225920 | tf_op jit(solution)/shard_map/pallas_call | solution.py:180
  165.6 4.2 %shard_map.125 = f32[16,8,4096]{2,1,0:T(8,128)} custom-call(f32[16,8,4096]{2,1,0:T(8,128)S(1)} %copy-done.1, f32[6,8,3072]{2,1,0:T(8,128)} %collective-permute-done.low, f32[6,8,3072]{2,1,0:T(8,128)} %collective-permute-done.1.high, f32[16,8,4096]{2,1,0:T(8,128)S(1)} %copy-done.3, f32[8,4096]{1,0:T(8,128)S(1)} %copy-done.4, ...), custom_call_target="tpu_custom_call", output_to_operand_aliasing={{}: (6, {})} | custom-call | flops 314572800 | bytes 3735552 | tf_op jit(solution)/shard_map/pallas_call | solution.py:180
  170.0 4.5 %shard_map.141 = f32[16,8,4096]{2,1,0:T(8,128)} custom-call(f32[16,8,4096]{2,1,0:T(8,128)S(1)} %copy-done.5, f32[1,8,4096]{2,1,0:T(8,128)S(1)} %broadcast_select_fusion.1.refs_0_.rest_0_, f32[1,8,4096]{2,1,0:T(8,128)S(1)} %broadcast_select_fusion.refs_1_.rest_1_, f32[1,8,4096]{2,1,0:T(8,128)S(1)} %copy-done.8, f32[1,8,4096]{2,1,0:T(8,128)S(1)} %copy-done.12, ...), custom_call_target="tpu_custom_call" | custom-call | flops 805306368 | bytes 8388608 | tf_op jit(solution)/shard_map/pallas_call | solution.py:265
  (147 shorter events, 32.3 us)
Async XLA Ops:
  3.7 9.6 %collective-permute-start.4 = (f32[1,8,4096]{2,1,0:T(8,128)S(1)}, f32[1,8,4096]{2,1,0:T(8,128)S(1)}, u32[]{:S(2)}, u32[]{:S(2)}) collective-permute-start(f32[1,8,4096]{2,1,0:T(8,128)S(1)} %get-tuple-element.29), channel_id=1, source_target_pairs={{0,16},{8,24},{16,32},{24,40},{32,48},{40,56},{48,64},{56,72},{64,... | collective-permute-start | bytes 393224 | tf_op jit(solution)/shard_map/ppermute | solution.py:394
  6.1 7.1 %collective-permute-start.5 = (f32[1,8,4096]{2,1,0:T(8,128)S(1)}, f32[1,8,4096]{2,1,0:T(8,128)S(1)}, u32[]{:S(2)}, u32[]{:S(2)}) collective-permute-start(f32[1,8,4096]{2,1,0:T(8,128)S(1)} %get-tuple-element.30), channel_id=1, source_target_pairs={{0,112},{8,120},{16,0},{24,8},{32,16},{40,24},{48,32},{56,40},{64,... | collective-permute-start | bytes 393224 | tf_op jit(solution)/shard_map/ppermute | solution.py:395
  13.9 14.1 %collective-permute-start.6 = (f32[2,8,4096]{2,1,0:T(8,128)S(1)}, f32[2,8,4096]{2,1,0:T(8,128)S(1)}, u32[]{:S(2)}, u32[]{:S(2)}) collective-permute-start(f32[2,8,4096]{2,1,0:T(8,128)S(1)} %get-tuple-element.31), channel_id=1, source_target_pairs={{0,16},{8,24},{16,32},{24,40},{32,48},{40,56},{48,64},{56,72},{64,... | collective-permute-start | bytes 786440 | tf_op jit(solution)/shard_map/ppermute | solution.py:398
  14.0 14.0 %collective-permute-start.7 = (f32[2,8,4096]{2,1,0:T(8,128)S(1)}, f32[2,8,4096]{2,1,0:T(8,128)S(1)}, u32[]{:S(2)}, u32[]{:S(2)}) collective-permute-start(f32[2,8,4096]{2,1,0:T(8,128)S(1)} %get-tuple-element.32), channel_id=1, source_target_pairs={{0,112},{8,120},{16,0},{24,8},{32,16},{40,24},{48,32},{56,40},{64,... | collective-permute-start | bytes 786440 | tf_op jit(solution)/shard_map/ppermute | solution.py:399
  16.6 7.9 %collective-permute-start.14 = (f32[1,8,4096]{2,1,0:T(8,128)S(1)}, f32[1,8,4096]{2,1,0:T(8,128)S(1)}, u32[]{:S(2)}, u32[]{:S(2)}) collective-permute-start(f32[1,8,4096]{2,1,0:T(8,128)S(1)} %get-tuple-element.49), channel_id=1, source_target_pairs={{0,16},{8,24},{16,32},{24,40},{32,48},{40,56},{48,64},{56,72},{64,... | collective-permute-start | bytes 393224 | tf_op jit(solution)/shard_map/ppermute | solution.py:394
  16.7 7.8 %collective-permute-start.15 = (f32[1,8,4096]{2,1,0:T(8,128)S(1)}, f32[1,8,4096]{2,1,0:T(8,128)S(1)}, u32[]{:S(2)}, u32[]{:S(2)}) collective-permute-start(f32[1,8,4096]{2,1,0:T(8,128)S(1)} %get-tuple-element.48), channel_id=1, source_target_pairs={{0,112},{8,120},{16,0},{24,8},{32,16},{40,24},{48,32},{56,40},{64,... | collective-permute-start | bytes 393224 | tf_op jit(solution)/shard_map/ppermute | solution.py:395
  25.2 7.0 %collective-permute-start.16 = (f32[2,8,4096]{2,1,0:T(8,128)S(1)}, f32[2,8,4096]{2,1,0:T(8,128)S(1)}, u32[]{:S(2)}, u32[]{:S(2)}) collective-permute-start(f32[2,8,4096]{2,1,0:T(8,128)S(1)} %get-tuple-element.40), channel_id=1, source_target_pairs={{0,16},{8,24},{16,32},{24,40},{32,48},{40,56},{48,64},{56,72},{64,... | collective-permute-start | bytes 786440 | tf_op jit(solution)/shard_map/ppermute | solution.py:398
  28.5 9.6 %collective-permute-start.8 = (f32[2,8,4096]{2,1,0:T(8,128)S(1)}, f32[2,8,4096]{2,1,0:T(8,128)S(1)}, u32[]{:S(2)}, u32[]{:S(2)}) collective-permute-start(f32[2,8,4096]{2,1,0:T(8,128)S(1)} %get-tuple-element.33), channel_id=1, source_target_pairs={{0,16},{8,24},{16,32},{24,40},{32,48},{40,56},{48,64},{56,72},{64,... | collective-permute-start | bytes 786440 | tf_op jit(solution)/shard_map/ppermute | solution.py:398
  28.6 9.5 %collective-permute-start.9 = (f32[2,8,4096]{2,1,0:T(8,128)S(1)}, f32[2,8,4096]{2,1,0:T(8,128)S(1)}, u32[]{:S(2)}, u32[]{:S(2)}) collective-permute-start(f32[2,8,4096]{2,1,0:T(8,128)S(1)} %get-tuple-element.34), channel_id=1, source_target_pairs={{0,112},{8,120},{16,0},{24,8},{32,16},{40,24},{48,32},{56,40},{64,... | collective-permute-start | bytes 786440 | tf_op jit(solution)/shard_map/ppermute | solution.py:399
  32.8 10.8 %collective-permute-start.18 = (f32[2,8,4096]{2,1,0:T(8,128)S(1)}, f32[2,8,4096]{2,1,0:T(8,128)S(1)}, u32[]{:S(2)}, u32[]{:S(2)}) collective-permute-start(f32[2,8,4096]{2,1,0:T(8,128)S(1)} %get-tuple-element.42), channel_id=1, source_target_pairs={{0,16},{8,24},{16,32},{24,40},{32,48},{40,56},{48,64},{56,72},{64,... | collective-permute-start | bytes 786440 | tf_op jit(solution)/shard_map/ppermute | solution.py:398
  34.0 9.6 %collective-permute-start.19 = (f32[2,8,4096]{2,1,0:T(8,128)S(1)}, f32[2,8,4096]{2,1,0:T(8,128)S(1)}, u32[]{:S(2)}, u32[]{:S(2)}) collective-permute-start(f32[2,8,4096]{2,1,0:T(8,128)S(1)} %get-tuple-element.43), channel_id=1, source_target_pairs={{0,112},{8,120},{16,0},{24,8},{32,16},{40,24},{48,32},{56,40},{64,... | collective-permute-start | bytes 786440 | tf_op jit(solution)/shard_map/ppermute | solution.py:399
  38.8 10.5 %collective-permute-start.10 = (f32[2,8,4096]{2,1,0:T(8,128)S(1)}, f32[2,8,4096]{2,1,0:T(8,128)S(1)}, u32[]{:S(2)}, u32[]{:S(2)}) collective-permute-start(f32[2,8,4096]{2,1,0:T(8,128)S(1)} %get-tuple-element.35), channel_id=1, source_target_pairs={{0,16},{8,24},{16,32},{24,40},{32,48},{40,56},{48,64},{56,72},{64,... | collective-permute-start | bytes 786440 | tf_op jit(solution)/shard_map/ppermute | solution.py:398
  39.3 9.9 %collective-permute-start.11 = (f32[2,8,4096]{2,1,0:T(8,128)S(1)}, f32[2,8,4096]{2,1,0:T(8,128)S(1)}, u32[]{:S(2)}, u32[]{:S(2)}) collective-permute-start(f32[2,8,4096]{2,1,0:T(8,128)S(1)} %get-tuple-element.36), channel_id=1, source_target_pairs={{0,112},{8,120},{16,0},{24,8},{32,16},{40,24},{48,32},{56,40},{64,... | collective-permute-start | bytes 786440 | tf_op jit(solution)/shard_map/ppermute | solution.py:399
  44.2 11.0 %collective-permute-start.20 = (f32[2,8,4096]{2,1,0:T(8,128)S(1)}, f32[2,8,4096]{2,1,0:T(8,128)S(1)}, u32[]{:S(2)}, u32[]{:S(2)}) collective-permute-start(f32[2,8,4096]{2,1,0:T(8,128)S(1)} %get-tuple-element.44), channel_id=1, source_target_pairs={{0,16},{8,24},{16,32},{24,40},{32,48},{40,56},{48,64},{56,72},{64,... | collective-permute-start | bytes 786440 | tf_op jit(solution)/shard_map/ppermute | solution.py:398
  44.9 10.3 %collective-permute-start.21 = (f32[2,8,4096]{2,1,0:T(8,128)S(1)}, f32[2,8,4096]{2,1,0:T(8,128)S(1)}, u32[]{:S(2)}, u32[]{:S(2)}) collective-permute-start(f32[2,8,4096]{2,1,0:T(8,128)S(1)} %get-tuple-element.45), channel_id=1, source_target_pairs={{0,112},{8,120},{16,0},{24,8},{32,16},{40,24},{48,32},{56,40},{64,... | collective-permute-start | bytes 786440 | tf_op jit(solution)/shard_map/ppermute | solution.py:399
  49.9 8.3 %collective-permute-start.12 = (f32[2,8,3072]{2,1,0:T(8,128)S(1)}, f32[2,8,3072]{2,1,0:T(8,128)S(1)}, u32[]{:S(2)}, u32[]{:S(2)}) collective-permute-start(f32[2,8,3072]{2,1,0:T(8,128)S(1)} %get-tuple-element.38), channel_id=1, source_target_pairs={{0,1},{1,2},{2,3},{3,4},{4,5},{5,6},{6,7},{7,0},{8,9},{9,10},{10,1... | collective-permute-start | bytes 589832 | tf_op jit(solution)/shard_map/ppermute | solution.py:405
  59.4 8.7 %collective-permute-start.23 = (f32[1,8,4096]{2,1,0:T(8,128)S(1)}, f32[1,8,4096]{2,1,0:T(8,128)S(1)}, u32[]{:S(2)}, u32[]{:S(2)}) collective-permute-start(f32[1,8,4096]{2,1,0:T(8,128)S(1)} %shard_map.135), channel_id=1, source_target_pairs={{0,128},{8,136},{16,144},{24,152},{32,160},{40,168},{48,176},{56,1... | collective-permute-start | bytes 393224 | tf_op jit(solution)/shard_map/ppermute | solution.py:439
  60.7 59.4 %collective-permute-start.2 = (f32[10,8,3072]{2,1,0:T(8,128)}, f32[10,8,3072]{2,1,0:T(8,128)}, u32[]{:S(2)}, u32[]{:S(2)}) collective-permute-start(f32[10,8,3072]{2,1,0:T(8,128)} %get-tuple-element.27), channel_id=1, source_target_pairs={{0,1},{1,2},{2,3},{3,4},{4,5},{5,6},{6,7},{7,0},{8,9},{9,10},{10,1... | collective-permute-start | bytes 2949128 | tf_op jit(solution)/shard_map/ppermute | solution.py:405
  63.1 94.5 %collective-permute-start.3 = (f32[10,8,3072]{2,1,0:T(8,128)}, f32[10,8,3072]{2,1,0:T(8,128)}, u32[]{:S(2)}, u32[]{:S(2)}) collective-permute-start(f32[10,8,3072]{2,1,0:T(8,128)} %get-tuple-element.28), channel_id=1, source_target_pairs={{1,0},{2,1},{3,2},{4,3},{5,4},{6,5},{7,6},{0,7},{9,8},{10,9},{11,1... | collective-permute-start | bytes 2949128 | tf_op jit(solution)/shard_map/ppermute | solution.py:406
  67.3 50.8 %collective-permute-start = (f32[6,8,3072]{2,1,0:T(8,128)}, f32[6,8,3072]{2,1,0:T(8,128)}, u32[]{:S(2)}, u32[]{:S(2)}) collective-permute-start(f32[6,8,3072]{2,1,0:T(8,128)} %get-tuple-element.25), channel_id=1, source_target_pairs={{0,1},{1,2},{2,3},{3,4},{4,5},{5,6},{6,7},{7,0},{8,9},{9,10},{10,1... | collective-permute-start | bytes 1769480 | tf_op jit(solution)/shard_map/ppermute | solution.py:405
  67.9 50.0 %collective-permute-start.22 = (f32[1,8,4096]{2,1,0:T(8,128)S(1)}, f32[1,8,4096]{2,1,0:T(8,128)S(1)}, u32[]{:S(2)}, u32[]{:S(2)}) collective-permute-start(f32[1,8,4096]{2,1,0:T(8,128)S(1)} %shard_map.134), channel_id=1, source_target_pairs={{0,128},{8,136},{16,144},{24,152},{32,160},{40,168},{48,176},{56,1... | collective-permute-start | bytes 393224 | tf_op jit(solution)/shard_map/ppermute | solution.py:439
  68.1 52.8 %collective-permute-start.27 = (f32[1,8,4096]{2,1,0:T(8,128)S(1)}, f32[1,8,4096]{2,1,0:T(8,128)S(1)}, u32[]{:S(2)}, u32[]{:S(2)}) collective-permute-start(f32[1,8,4096]{2,1,0:T(8,128)S(1)} %broadcast_select_fusion.refs_1_.rest_1_), channel_id=1, source_target_pairs={{0,112},{8,120},{16,0},{24,8},{32,16},{40,24},{48,32},{56,40},{64,... | collective-permute-start | bytes 393224 | tf_op jit(solution)/shard_map/ppermute | solution.py:448
  127.6 13.7 %collective-permute-start.35 = (f32[1,8,4096]{2,1,0:T(8,128)S(1)}, f32[1,8,4096]{2,1,0:T(8,128)S(1)}, u32[]{:S(2)}, u32[]{:S(2)}) collective-permute-start(f32[1,8,4096]{2,1,0:T(8,128)S(1)} %collective-permute-done.31.refs_3_.rest_9_), channel_id=1, source_target_pairs={{0,112},{8,120},{16,0},{24,8},{32,16},{40,24},{48,32},{56,40},{64,... | collective-permute-start | bytes 393224 | tf_op jit(solution)/shard_map/ppermute | solution.py:448
  128.5 15.8 %collective-permute-start.32 = (f32[1,8,4096]{2,1,0:T(8,128)S(1)}, f32[1,8,4096]{2,1,0:T(8,128)S(1)}, u32[]{:S(2)}, u32[]{:S(2)}) collective-permute-start(f32[1,8,4096]{2,1,0:T(8,128)S(1)} %collective-permute-done.28.refs_0_.rest_6_), channel_id=1, source_target_pairs={{0,16},{8,24},{16,32},{24,40},{32,48},{40,56},{48,64},{56,72},{64,... | collective-permute-start | bytes 393224 | tf_op jit(solution)/shard_map/ppermute | solution.py:448
  130.8 14.0 %collective-permute-start.34 = (f32[1,8,4096]{2,1,0:T(8,128)S(1)}, f32[1,8,4096]{2,1,0:T(8,128)S(1)}, u32[]{:S(2)}, u32[]{:S(2)}) collective-permute-start(f32[1,8,4096]{2,1,0:T(8,128)S(1)} %collective-permute-done.30.refs_2_.rest_8_), channel_id=1, source_target_pairs={{0,16},{8,24},{16,32},{24,40},{32,48},{40,56},{48,64},{56,72},{64,... | collective-permute-start | bytes 393224 | tf_op jit(solution)/shard_map/ppermute | solution.py:448
  131.8 38.0 %collective-permute-start.38 = (f32[6,8,4096]{2,1,0:T(8,128)}, f32[6,8,4096]{2,1,0:T(8,128)S(1)}, u32[]{:S(2)}, u32[]{:S(2)}) collective-permute-start(f32[6,8,4096]{2,1,0:T(8,128)} %shard_map.136), channel_id=1, source_target_pairs={{0,8},{8,0},{16,24},{24,16},{32,40},{40,32},{48,56},{56,48},{64,72... | collective-permute-start | bytes 2359304 | tf_op jit(solution)/shard_map/ppermute | solution.py:456
  144.3 8.5 %collective-permute-start.37 = (f32[1,8,4096]{2,1,0:T(8,128)S(1)}, f32[1,8,4096]{2,1,0:T(8,128)S(1)}, u32[]{:S(2)}, u32[]{:S(2)}) collective-permute-start(f32[1,8,4096]{2,1,0:T(8,128)S(1)} %collective-permute-done.35.refs_3_.rest_13_), channel_id=1, source_target_pairs={{0,112},{8,120},{16,0},{24,8},{32,16},{40,24},{48,32},{56,40},{64,... | collective-permute-start | bytes 393224 | tf_op jit(solution)/shard_map/ppermute | solution.py:448
  144.8 11.4 %collective-permute-start.36 = (f32[1,8,4096]{2,1,0:T(8,128)S(1)}, f32[1,8,4096]{2,1,0:T(8,128)S(1)}, u32[]{:S(2)}, u32[]{:S(2)}) collective-permute-start(f32[1,8,4096]{2,1,0:T(8,128)S(1)} %collective-permute-done.32.refs_0_.rest_10_), channel_id=1, source_target_pairs={{0,16},{8,24},{16,32},{24,40},{32,48},{40,56},{48,64},{56,72},{64,... | collective-permute-start | bytes 393224 | tf_op jit(solution)/shard_map/ppermute | solution.py:448
  146.5 19.1 %collective-permute-start.1 = (f32[6,8,3072]{2,1,0:T(8,128)}, f32[6,8,3072]{2,1,0:T(8,128)}, u32[]{:S(2)}, u32[]{:S(2)}) collective-permute-start(f32[6,8,3072]{2,1,0:T(8,128)} %get-tuple-element.26), channel_id=1, source_target_pairs={{1,0},{2,1},{3,2},{4,3},{5,4},{6,5},{7,6},{0,7},{9,8},{10,9},{11,1... | collective-permute-start | bytes 1769480 | tf_op jit(solution)/shard_map/ppermute | solution.py:406
  152.7 17.1 %collective-permute-start.39 = (f32[4,8,4096]{2,1,0:T(8,128)}, f32[4,8,4096]{2,1,0:T(8,128)}, u32[]{:S(2)}, u32[]{:S(2)}) collective-permute-start(f32[4,8,4096]{2,1,0:T(8,128)} %shard_map.137), channel_id=1, source_target_pairs={{0,8},{8,0},{16,24},{24,16},{32,40},{40,32},{48,56},{56,48},{64,72... | collective-permute-start | bytes 1572872 | tf_op jit(solution)/shard_map/ppermute | solution.py:456
  156.2 13.6 %collective-permute-start.40 = (f32[4,8,4096]{2,1,0:T(8,128)}, f32[4,8,4096]{2,1,0:T(8,128)}, u32[]{:S(2)}, u32[]{:S(2)}) collective-permute-start(f32[4,8,4096]{2,1,0:T(8,128)} %shard_map.138), channel_id=1, source_target_pairs={{0,8},{8,0},{16,24},{24,16},{32,40},{40,32},{48,56},{56,48},{64,72... | collective-permute-start | bytes 1572872 | tf_op jit(solution)/shard_map/ppermute | solution.py:456
  157.7 12.1 %collective-permute-start.41 = (f32[2,8,4096]{2,1,0:T(8,128)}, f32[2,8,4096]{2,1,0:T(8,128)}, u32[]{:S(2)}, u32[]{:S(2)}) collective-permute-start(f32[2,8,4096]{2,1,0:T(8,128)} %shard_map.139), channel_id=1, source_target_pairs={{0,8},{8,0},{16,24},{24,16},{32,40},{40,32},{48,56},{56,48},{64,72... | collective-permute-start | bytes 786440 | tf_op jit(solution)/shard_map/ppermute | solution.py:456
  (45 other events, 404.6 us)
